TPU v7x, 32 devices: a whole 2x2x4 slice. The times are simulated.
32 devices in a mesh: lat: 4 (over y, core), lon: 8 (over z, x).
Axes of the slice: x: 2, y: 2, z: 4, core: 2. Of those that a mesh axis runs over, the one named last changes fastest.
Arguments:
- field_in: bfloat16 [512, 64, 300], P('lat', 'lon'), may hold values from -6 to 6
- sea_mask: int32 [512, 64], P('lat', 'lon'), may hold values 0 or 1
- mirror: int32 [64], replicated, may hold values from 0 to 63, as said below
- kernel: float32 [49, 300], replicated, may hold values from -0.875 to 0.875
- norm_gain: float32 [300], replicated, may hold values from 0.1 to 1.9
- proj_in: bfloat16 [300, 1200], replicated, may hold values from -0.375 to 0.375
- proj_out: bfloat16 [1200, 300], replicated, may hold values from -0.1875 to 0.1875
- cotangent: bfloat16 [512, 64, 300], P('lat', 'lon'), may hold values from -6 to 6
Outputs:
- block_out: bfloat16 [512, 64, 300], P('lat', 'lon')
- grad_field: bfloat16 [512, 64, 300], P('lat', 'lon')
- grad_in: float32 [300, 1200], replicated
- grad_out: float32 [1200, 300], replicated
- grad_kernel: float32 [49, 300], replicated
- grad_gain: float32 [300], replicated
Inputs may be any that keep to these rules, and one draw needn't show every extreme that they name: mirror[i] = (s - 1 - i) mod 64 for one s, so mirror[mirror[i]] = i.
All inputs are finite; a program needn't handle non-finite values. No bound on the sum of `sea_mask` on one device may be relied on, other than what follows from the above.
Results may differ from a plain program's by a relative error of at most 0.0057.
Values may be sent and summed in bfloat16 or wider, within the bound.
No kernel may reach another device: no remote copies, remote signals or barrier semaphores. Data moves between devices by JAX's collectives and lax.ppermute only.
A program may use at most 128 MiB of HBM per device.

v0:
```python
import jax
import jax.numpy as jnp
from jax import lax
from jax.sharding import PartitionSpec as P


def extended(block, sides, width):
    for axis, dim in sides:
        count = lax.axis_size(axis)
        forward = [(i, i + 1) for i in range(count - 1)]
        forward.append((count - 1, 0))
        backward = [(target, source) for source, target in forward]
        low = lax.ppermute(
            lax.slice_in_dim(block, block.shape[dim] - width, None, axis=dim), axis, forward
        )
        high = lax.ppermute(lax.slice_in_dim(block, 0, width, axis=dim), axis, backward)
        block = jnp.concatenate([low, block, high], axis=dim)
    return block


def gelu_pair(value):
    coeff = 0.7978845608028654
    inner = coeff * (value + 0.044715 * value * value * value)
    tanh_val = jnp.tanh(inner)
    result = 0.5 * value * (1.0 + tanh_val)
    slope = 0.5 * (1.0 + tanh_val) + 0.5 * value * (1.0 - tanh_val * tanh_val) * coeff * (
        1.0 + 0.134145 * value * value
    )
    return (result, slope)


def depthwise(ext, kernel, nrows, ncols):
    total = jnp.zeros((nrows, ncols, kernel.shape[1]), jnp.float32)
    for tap_a in range(7):
        for tap_b in range(7):
            total = total + kernel[7 * tap_a + tap_b] * ext[
                tap_a : tap_a + nrows, tap_b : tap_b + ncols
            ].astype(jnp.float32)
    return total


def transposed(padded, kernel, nrows, ncols):
    total = jnp.zeros((nrows, ncols, kernel.shape[1]), jnp.float32)
    for tap_a in range(7):
        for tap_b in range(7):
            window = padded[6 - tap_a : 6 - tap_a + nrows, 6 - tap_b : 6 - tap_b + ncols].astype(
                jnp.float32
            )
            total = total + kernel[7 * tap_a + tap_b] * window
    return total


def local_block(conv_flat, field_flat, mask_col, cot_flat, norm_gain, proj_in, proj_out):
    mean = jnp.mean(conv_flat, axis=-1, keepdims=True)
    centered = conv_flat - mean
    var = jnp.mean(centered * centered, axis=-1, keepdims=True)
    rstd = lax.rsqrt(var + 1e-06)
    nhat = centered * rstd
    normed = (nhat * norm_gain).astype(jnp.bfloat16)
    pre = jnp.dot(normed, proj_in, preferred_element_type=jnp.float32)
    act, slope = gelu_pair(pre)
    act = act.astype(jnp.bfloat16)
    mixed = jnp.dot(act, proj_out, preferred_element_type=jnp.float32)
    result = (mask_col * (field_flat + mixed)).astype(jnp.bfloat16)
    back = cot_flat * mask_col
    dw_out = lax.dot_general(
        act, back, (((0,), (0,)), ((), ())), preferred_element_type=jnp.float32
    )
    grad_hidden = lax.dot_general(
        back, proj_out, (((1,), (1,)), ((), ())), preferred_element_type=jnp.float32
    )
    grad_pre = (grad_hidden * slope).astype(jnp.bfloat16)
    dw_in = lax.dot_general(
        normed, grad_pre, (((0,), (0,)), ((), ())), preferred_element_type=jnp.float32
    )
    grad_norm = lax.dot_general(
        grad_pre, proj_in, (((1,), (1,)), ((), ())), preferred_element_type=jnp.float32
    )
    dgain = jnp.sum(grad_norm * nhat, axis=0)
    scaled = grad_norm * norm_gain
    gconv = rstd * (
        scaled
        - jnp.mean(scaled, axis=-1, keepdims=True)
        - nhat * jnp.mean(scaled * nhat, axis=-1, keepdims=True)
    )
    return (result, gconv.astype(jnp.bfloat16), dw_in, dw_out, dgain)


def body(field_in, sea_mask, mirror, kernel, norm_gain, proj_in, proj_out, cotangent):
    nrows, ncols, width = field_in.shape
    n_lon = lax.axis_size("lon")
    n_lat = lax.axis_size("lat")
    total_cols = ncols * n_lon
    band = lax.axis_index("lat")
    is_top = band == n_lat - 1
    is_bottom = band == 0
    start = lax.axis_index("lon") * ncols
    maskf = sea_mask.astype(jnp.bfloat16)[:, :, None]
    masked = field_in * maskf
    ext = extended(masked, (("lat", 0), ("lon", 1)), 3)
    top_rows = lax.all_gather(masked[nrows - 3 :], "lon", axis=1, tiled=True)
    ext_cols = (start - 3 + jnp.arange(ncols + 6, dtype=jnp.int32)) % total_cols
    north = jnp.take(top_rows[::-1], jnp.take(mirror, ext_cols), axis=1)
    lower = jnp.where(is_bottom, jnp.zeros_like(ext[:3]), ext[:3])
    upper = jnp.where(is_top, north, ext[nrows + 3 :])
    ext = jnp.concatenate([lower, ext[3 : nrows + 3], upper], axis=0)
    conv = depthwise(ext, kernel, nrows, ncols)
    cells = nrows * ncols
    mask_col = maskf.reshape(cells, 1)
    block_out, gconv, dw_in, dw_out, dgain = local_block(
        conv.reshape(cells, width),
        field_in.reshape(cells, width),
        mask_col,
        cotangent.reshape(cells, width),
        norm_gain,
        proj_in,
        proj_out,
    )
    gconv = gconv.reshape(nrows, ncols, width)
    gconv_f = gconv.astype(jnp.float32)
    taps = []
    for tap_a in range(7):
        for tap_b in range(7):
            taps.append(
                jnp.sum(
                    gconv_f * ext[tap_a : tap_a + nrows, tap_b : tap_b + ncols].astype(jnp.float32),
                    axis=(0, 1),
                )
            )
    dkernel = jnp.stack(taps, axis=0)
    gext = extended(gconv, (("lat", 0), ("lon", 1)), 3)
    glower = jnp.where(is_bottom, jnp.zeros_like(gext[:3]), gext[:3])
    gupper = jnp.where(is_top, jnp.zeros_like(gext[:3]), gext[nrows + 3 :])
    spare = jnp.zeros((3, ncols + 6, width), jnp.bfloat16)
    gpad = jnp.concatenate([glower, gext[3 : nrows + 3], gupper, spare], axis=0)
    dfull = transposed(gpad, kernel, nrows + 3, ncols)
    own_mirror = jnp.take(mirror, start + jnp.arange(ncols, dtype=jnp.int32))
    fold_all = lax.all_gather(dfull[nrows:], "lon", axis=1, tiled=True)
    fold = jnp.take(fold_all[::-1], own_mirror, axis=1)
    fold = jnp.where(is_top, fold, jnp.zeros_like(fold))
    dmasked = dfull[:nrows] + jnp.concatenate(
        [jnp.zeros((nrows - 3, ncols, width), jnp.float32), fold], axis=0
    )
    back = (cotangent * maskf).astype(jnp.float32)
    grad_field = (back + maskf * dmasked).astype(jnp.bfloat16)
    sum_in, sum_out, sum_kernel, sum_gain = lax.psum(
        (dw_in, dw_out, dkernel, dgain), ("lat", "lon")
    )
    factor = 1.0 / jnp.sqrt(jnp.float32(nrows * n_lat * total_cols))
    return (
        block_out.reshape(nrows, ncols, width),
        grad_field,
        sum_in * factor,
        sum_out * factor,
        sum_kernel * factor,
        sum_gain * factor,
    )


def solution(mesh):
    in_specs = (
        P("lat", "lon", None),
        P("lat", "lon"),
        P(),
        P(),
        P(),
        P(),
        P(),
        P("lat", "lon", None),
    )
    out_specs = (P("lat", "lon", None), P("lat", "lon", None), P(), P(), P(), P())
    return jax.shard_map(body, mesh=mesh, in_specs=in_specs, out_specs=out_specs, check_vma=False)
```

profile of v0, /device:TPU:0, one launch (start us, length us, event | category | flops | bytes accessed | tf_op | source)
XLA Modules:
  0.0 347.2 jit_solution(4353511875321528051)
XLA Ops:
  10.9 2.0 collective-permute-start.1
  18.2 2.2 collective-permute-start.2
  20.4 3.1 collective-permute-start.3
  23.5 36.8 %all_gather.6 = bf16[3,64,300]{2,1,0:T(8,128)(2,1)S(1)} all-gather(bf16[3,8,300]{2,1,0:T(8,128)(2,1)S(1)} %copy.43), channel_id=1, replica_groups=mesh['lat'=4,'lon'=8] {'lon'}, dimensions={1}, use_global_device_ids=true | all-gather | bytes 129600 | tf_op jit(solution)/shard_map/all_gather | solution.py:101
  60.4 2.5 copy.52
  62.9 2.3 copy.51
  68.5 2.9 copy.49
  77.1 18.2 %fusion.173 = (f32[128,8]{0,1:T(8,128)S(1)}, f32[128,8,300]{2,0,1:T(8,128)S(1)}) fusion(bf16[3,14,300]{2,0,1:T(4,128)(2,1)S(1)} %get-tuple-element.142, bf16[128,14,300]{2,0,1:T(8,128)(2,1)S(1)} %slice.871, f32[300]{0:T(512)S(1)} %copy-done.109, f32[300]{0:T(512)S(1)} %copy-done.110, f32[300]{0:T(512)S(1)} %get-tuple-element.83, ...), kind=kLoop, calls=%fused_computation.453 | loop fusion | flops 84786176 | bytes 6720144 | tf_op jit(solution)/shard_map/reduce_sum | solution.py:54
  95.3 2.1 copy.114
  101.4 2.4 fusion.171
  103.8 4.8 %fusion.6 = bf16[1024,1200]{0,1:T(8,128)(2,1)S(1)} fusion(f32[1024,1200]{0,1:T(8,128)S(1)} %fusion.171, bf16[1200,300]{0,1:T(8,128)(2,1)S(1)} %copy-done.118, bf16[128,8,300]{2,1,0:T(8,128)(2,1)S(1)} %copy-done.15, bf16[1024]{0:T(1024)(128)(2,1)S(1)} %copy-done.114), kind=kOutput, calls=%fused_computation.101 | convolution fusion | flops 760934400 | bytes 8709248 | tf_op jit(solution)/shard_map/dot_general | solution.py:69
  112.8 4.7 %fusion.82 = (f32[300]{0:T(512)S(1)}, f32[300]{0:T(512)S(1)}, f32[300]{0:T(512)S(1)}, f32[300]{0:T(512)S(1)}, f32[300]{0:T(512)S(1)}, /*index=5*/f32[300]{0:T(512)S(1)}) fusion(bf16[134,11,300]{2,0,1:T(8,128)(2,1)} %copy-done.3, bf16[128,8,300]{2,1,0:T(8,128)(2,1)S(1)} %bitcast.38, bf16[134,11,300]{2,0,1:T(8,128)(2,1)} %copy-done.2), kind=kLoop, calls=%fused_computation.240 | loop fusion | flops 5835000 | bytes 4308000 | tf_op jit(solution)/shard_map/reduce_sum | solution.py:125
  117.5 2.6 fusion.100
  120.1 2.9 fusion.103
  125.1 2.3 fusion.74
  127.4 2.3 fusion.73
  129.6 2.6 fusion.102
  132.2 2.8 fusion.101
  135.1 2.2 fusion.170
  137.3 3.2 fusion.161
  144.3 5.7 %fusion.108 = bf16[1024,300]{0,1:T(8,128)(2,1)} fusion(f32[1024,300]{0,1:T(8,128)} %copy.49, bf16[1200,300]{0,1:T(8,128)(2,1)} %param.14, f32[1024]{0:T(1024)S(1)} %copy-done.115, f32[1024,1200]{0,1:T(8,128)} %copy-done.9), kind=kOutput, calls=%fused_computation.274 | convolution fusion | flops 749260800 | bytes 7482496 | tf_op jit(solution)/shard_map/dot_general | solution.py:63
  150.2 38.7 %all-reduce.1 = (f32[49,300]{1,0:T(8,128)S(1)}, f32[300]{0:T(512)S(1)}) all-reduce(f32[49,300]{1,0:T(8,128)S(1)} %stack.199, f32[300]{0:T(512)S(1)} %get-tuple-element.24), channel_id=1, replica_groups=mesh['lat'=4,'lon'=8] {'lat','lon'}, use_global_device_ids=true, to_apply=%region_55.56 | all-reduce | flops 15000 | bytes 120000 | tf_op jit(solution)/shard_map/psum | solution.py:146
  189.9 2.2 collective-permute-start.6
  192.1 2.5 collective-permute-start.7
  198.8 8.6 %collective-permute-done.6 = bf16[134,3,300]{2,0,1:T(8,128)(2,1)S(1)} collective-permute-done((bf16[134,3,300]{2,0,1:T(8,128)(2,1)}, bf16[134,3,300]{2,0,1:T(8,128)(2,1)S(1)}, u32[]{:S(2)}, u32[]{:S(2)}) %collective-permute-start.6) | collective-permute-done | bytes 241232 | tf_op jit(solution)/shard_map/ppermute | solution.py:13
  207.4 2.8 collective-permute-done.7
  212.7 18.6 %multiply_add_fusion.1 = f32[131,8,300]{2,0,1:T(8,128)S(1)} fusion(bf16[3,14,300]{2,0,1:T(4,128)(2,1)S(1)} %get-tuple-element.140, bf16[3,14,300]{2,0,1:T(4,128)(2,1)S(1)} %get-tuple-element.139, bf16[128,14,300]{2,0,1:T(8,128)(2,1)S(1)} %slice.960, bf16[134,14,300]{2,0,1:T(8,128)(2,1)S(1)} %get-tuple-element.144, ...), kind=kLoop, calls=%fused_computation.164 | loop fusion | flops 59107200 | bytes 24450000 | tf_op jit(solution)/shard_map/add | solution.py:49
  231.4 31.3 %all_gather.7 = f32[3,64,300]{2,1,0:T(8,128)S(1)} all-gather(f32[3,8,300]{2,1,0:T(8,128)S(1)} %copy.59), channel_id=1, replica_groups=mesh['lat'=4,'lon'=8] {'lon'}, dimensions={1}, use_global_device_ids=true | all-gather | bytes 259200 | tf_op jit(solution)/shard_map/all_gather | solution.py:138
  263.7 2.8 rev.7
  269.6 2.3 copy.63
  271.9 63.9 %all-reduce.5.cloned.1.call-done = (f32[300,1200]{1,0:T(8,128)}, f32[1200,300]{0,1:T(8,128)}) async-done(((f32[300,1200]{1,0:T(8,128)}, f32[1200,300]{0,1:T(8,128)}), (f32[300,1200]{1,0:T(8,128)}, f32[1200,300]{0,1:T(8,128)})) %all-reduce.5.cloned.1.call-update) | async-done | bytes 2880016 | tf_op jit(solution)/shard_map/psum | solution.py:146
  335.8 2.8 broadcast_multiply_fusion
  (376 shorter events, 43.0 us)
Async XLA Ops:
  7.2 94.2 %copy-start = (bf16[300,1200]{1,0:T(8,128)(2,1)S(1)}, bf16[300,1200]{1,0:T(8,128)(2,1)}, u32[]{:S(2)}) copy-start(bf16[300,1200]{1,0:T(8,128)(2,1)} %param.13) | copy-start | bytes 2160004
  7.2 328.6 %all-reduce.5.cloned.1.call-start = ((), (), s32[]{:S(2)}) async-start(), calls=%async_computation | async-start | bytes 6225920 | tf_op jit(solution)/shard_map/psum | solution.py:146
  8.6 67.0 %copy-start.19 = (bf16[128,8]{0,1:T(8,128)(2,1)}, bf16[128,8]{0,1:T(8,128)(2,1)S(1)}, u32[]{:S(2)}) copy-start(bf16[128,8]{0,1:T(8,128)(2,1)S(1)} %get-tuple-element.136) | copy-start | bytes 6148
  10.4 6.8 %collective-permute-start = (bf16[3,8,300]{2,0,1:T(4,128)(2,1)S(1)}, bf16[3,8,300]{2,0,1:T(4,128)(2,1)S(1)}, u32[]{:S(2)}, u32[]{:S(2)}) collective-permute-start(bf16[3,8,300]{2,0,1:T(4,128)(2,1)S(1)} %get-tuple-element.151), channel_id=1, source_target_pairs={{0,8},{8,16},{16,24},{24,0},{1,9},{9,17},{17,25},{25,1},{2,10},{10... | collective-permute-start | bytes 43208 | tf_op jit(solution)/shard_map/ppermute | solution.py:13
  10.9 6.3 %collective-permute-start.1 = (bf16[3,8,300]{2,0,1:T(4,128)(2,1)S(1)}, bf16[3,8,300]{2,0,1:T(4,128)(2,1)S(1)}, u32[]{:S(2)}, u32[]{:S(2)}) collective-permute-start(bf16[3,8,300]{2,0,1:T(4,128)(2,1)S(1)} %get-tuple-element.152), channel_id=1, source_target_pairs={{8,0},{16,8},{24,16},{0,24},{9,1},{17,9},{25,17},{1,25},{10,2},{18... | collective-permute-start | bytes 43208 | tf_op jit(solution)/shard_map/ppermute | solution.py:16
  14.3 61.3 %copy-start.22 = (f32[300]{0:T(512)}, f32[300]{0:T(512)S(1)}, u32[]{:S(2)}) copy-start(f32[300]{0:T(512)S(1)} %get-tuple-element.82) | copy-start | bytes 3604
  14.3 61.3 %copy-start.24 = (f32[300]{0:T(512)}, f32[300]{0:T(512)S(1)}, u32[]{:S(2)}) copy-start(f32[300]{0:T(512)S(1)} %get-tuple-element.83) | copy-start | bytes 3604
  14.3 61.3 %copy-start.26 = (f32[300]{0:T(512)}, f32[300]{0:T(512)S(1)}, u32[]{:S(2)}) copy-start(f32[300]{0:T(512)S(1)} %get-tuple-element.84) | copy-start | bytes 3604
  14.3 61.3 %copy-start.28 = (f32[300]{0:T(512)}, f32[300]{0:T(512)S(1)}, u32[]{:S(2)}) copy-start(f32[300]{0:T(512)S(1)} %get-tuple-element.85) | copy-start | bytes 3604
  14.3 61.3 %copy-start.30 = (f32[300]{0:T(512)}, f32[300]{0:T(512)S(1)}, u32[]{:S(2)}) copy-start(f32[300]{0:T(512)S(1)} %get-tuple-element.86) | copy-start | bytes 3604
  14.3 61.3 %copy-start.32 = (f32[300]{0:T(512)}, f32[300]{0:T(512)S(1)}, u32[]{:S(2)}) copy-start(f32[300]{0:T(512)S(1)} %get-tuple-element.87) | copy-start | bytes 3604
  14.3 61.3 %copy-start.34 = (f32[300]{0:T(512)}, f32[300]{0:T(512)S(1)}, u32[]{:S(2)}) copy-start(f32[300]{0:T(512)S(1)} %get-tuple-element.88) | copy-start | bytes 3604
  14.3 61.3 %copy-start.36 = (f32[300]{0:T(512)}, f32[300]{0:T(512)S(1)}, u32[]{:S(2)}) copy-start(f32[300]{0:T(512)S(1)} %get-tuple-element.89) | copy-start | bytes 3604
  14.3 61.3 %copy-start.38 = (f32[300]{0:T(512)}, f32[300]{0:T(512)S(1)}, u32[]{:S(2)}) copy-start(f32[300]{0:T(512)S(1)} %get-tuple-element.90) | copy-start | bytes 3604
  14.3 61.3 %copy-start.40 = (f32[300]{0:T(512)}, f32[300]{0:T(512)S(1)}, u32[]{:S(2)}) copy-start(f32[300]{0:T(512)S(1)} %get-tuple-element.91) | copy-start | bytes 3604
  14.3 61.3 %copy-start.42 = (f32[300]{0:T(512)}, f32[300]{0:T(512)S(1)}, u32[]{:S(2)}) copy-start(f32[300]{0:T(512)S(1)} %get-tuple-element.92) | copy-start | bytes 3604
  14.4 61.3 %copy-start.44 = (f32[300]{0:T(512)}, f32[300]{0:T(512)S(1)}, u32[]{:S(2)}) copy-start(f32[300]{0:T(512)S(1)} %get-tuple-element.93) | copy-start | bytes 3604
  14.4 61.3 %copy-start.46 = (f32[300]{0:T(512)}, f32[300]{0:T(512)S(1)}, u32[]{:S(2)}) copy-start(f32[300]{0:T(512)S(1)} %get-tuple-element.94) | copy-start | bytes 3604
  14.4 61.3 %copy-start.48 = (f32[300]{0:T(512)}, f32[300]{0:T(512)S(1)}, u32[]{:S(2)}) copy-start(f32[300]{0:T(512)S(1)} %get-tuple-element.95) | copy-start | bytes 3604
  14.4 61.3 %copy-start.50 = (f32[300]{0:T(512)}, f32[300]{0:T(512)S(1)}, u32[]{:S(2)}) copy-start(f32[300]{0:T(512)S(1)} %get-tuple-element.96) | copy-start | bytes 3604
  14.4 61.3 %copy-start.52 = (f32[300]{0:T(512)}, f32[300]{0:T(512)S(1)}, u32[]{:S(2)}) copy-start(f32[300]{0:T(512)S(1)} %get-tuple-element.97) | copy-start | bytes 3604
  14.4 61.3 %copy-start.54 = (f32[300]{0:T(512)}, f32[300]{0:T(512)S(1)}, u32[]{:S(2)}) copy-start(f32[300]{0:T(512)S(1)} %get-tuple-element.98) | copy-start | bytes 3604
  14.4 61.3 %copy-start.56 = (f32[300]{0:T(512)}, f32[300]{0:T(512)S(1)}, u32[]{:S(2)}) copy-start(f32[300]{0:T(512)S(1)} %get-tuple-element.99) | copy-start | bytes 3604
  14.4 61.3 %copy-start.58 = (f32[300]{0:T(512)}, f32[300]{0:T(512)S(1)}, u32[]{:S(2)}) copy-start(f32[300]{0:T(512)S(1)} %get-tuple-element.100) | copy-start | bytes 3604
  15.2 60.6 %copy-start.70 = (f32[300]{0:T(512)}, f32[300]{0:T(512)S(1)}, u32[]{:S(2)}) copy-start(f32[300]{0:T(512)S(1)} %get-tuple-element.106) | copy-start | bytes 3604
  15.2 60.6 %copy-start.72 = (f32[300]{0:T(512)}, f32[300]{0:T(512)S(1)}, u32[]{:S(2)}) copy-start(f32[300]{0:T(512)S(1)} %get-tuple-element.107) | copy-start | bytes 3604
  18.2 54.4 %collective-permute-start.2 = (bf16[134,3,300]{2,0,1:T(8,128)(2,1)}, bf16[134,3,300]{2,0,1:T(8,128)(2,1)S(1)}, u32[]{:S(2)}, u32[]{:S(2)}) collective-permute-start(bf16[134,3,300]{2,0,1:T(8,128)(2,1)} %get-tuple-element.149), channel_id=1, source_target_pairs={{0,1},{1,2},{2,3},{3,4},{4,5},{5,6},{6,7},{7,0},{8,9},{9,10},{10,1... | collective-permute-start | bytes 723608 | tf_op jit(solution)/shard_map/ppermute | solution.py:13
  20.4 52.2 %collective-permute-start.3 = (bf16[134,3,300]{2,0,1:T(8,128)(2,1)}, bf16[134,3,300]{2,0,1:T(8,128)(2,1)S(1)}, u32[]{:S(2)}, u32[]{:S(2)}) collective-permute-start(bf16[134,3,300]{2,0,1:T(8,128)(2,1)} %get-tuple-element.150), channel_id=1, source_target_pairs={{1,0},{2,1},{3,2},{4,3},{5,4},{6,5},{7,6},{0,7},{9,8},{10,9},{11,1... | collective-permute-start | bytes 723608 | tf_op jit(solution)/shard_map/ppermute | solution.py:16
  142.3 46.6 %collective-permute-start.4 = (bf16[3,8,300]{2,0,1:T(4,128)(2,1)S(1)}, bf16[3,8,300]{2,0,1:T(4,128)(2,1)S(1)}, u32[]{:S(2)}, u32[]{:S(2)}) collective-permute-start(bf16[3,8,300]{2,0,1:T(4,128)(2,1)S(1)} %copy.54), channel_id=1, source_target_pairs={{0,8},{8,16},{16,24},{24,0},{1,9},{9,17},{17,25},{25,1},{2,10},{10... | collective-permute-start | bytes 43208 | tf_op jit(solution)/shard_map/ppermute | solution.py:13
  142.5 46.5 %collective-permute-start.5 = (bf16[3,8,300]{2,0,1:T(4,128)(2,1)S(1)}, bf16[3,8,300]{2,0,1:T(4,128)(2,1)S(1)}, u32[]{:S(2)}, u32[]{:S(2)}) collective-permute-start(bf16[3,8,300]{2,0,1:T(4,128)(2,1)S(1)} %copy.57), channel_id=1, source_target_pairs={{8,0},{16,8},{24,16},{0,24},{9,1},{17,9},{25,17},{1,25},{10,2},{18... | collective-permute-start | bytes 43208 | tf_op jit(solution)/shard_map/ppermute | solution.py:16
  189.9 17.5 %collective-permute-start.6 = (bf16[134,3,300]{2,0,1:T(8,128)(2,1)}, bf16[134,3,300]{2,0,1:T(8,128)(2,1)S(1)}, u32[]{:S(2)}, u32[]{:S(2)}) collective-permute-start(bf16[134,3,300]{2,0,1:T(8,128)(2,1)} %get-tuple-element.145), channel_id=1, source_target_pairs={{0,1},{1,2},{2,3},{3,4},{4,5},{5,6},{6,7},{7,0},{8,9},{9,10},{10,1... | collective-permute-start | bytes 723608 | tf_op jit(solution)/shard_map/ppermute | solution.py:13
  192.1 18.1 %collective-permute-start.7 = (bf16[134,3,300]{2,0,1:T(8,128)(2,1)S(1)}, bf16[134,3,300]{2,0,1:T(8,128)(2,1)S(1)}, u32[]{:S(2)}, u32[]{:S(2)}) collective-permute-start(bf16[134,3,300]{2,0,1:T(8,128)(2,1)S(1)} %get-tuple-element.146), channel_id=1, source_target_pairs={{1,0},{2,1},{3,2},{4,3},{5,4},{6,5},{7,6},{0,7},{9,8},{10,9},{11,1... | collective-permute-start | bytes 723608 | tf_op jit(solution)/shard_map/ppermute | solution.py:16
  (100 other events, 738.9 us)
Sparse Core Ops, SparseCore 0:
  198.2 137.5 all-reduce.4
where the time goes:
time: 351 us; the launch traced here: 347 us
  blocking collectives  107 us (30%)
  waiting for transfers between devices  75.4 us (21%)
  other arithmetic  74.9 us (21%)
  local copies, waits for them, and re-layouts  39.1 us (11%)
  matrix products  19.6 us (6%)
  between operations  16.9 us (5%)
  starting transfers between devices  14.4 us (4%)
    psum x1, waiting for transfers between devices, body(): lax.psum((dw_in, dw_out, dkernel, dgain), ('lat', 'lon'))  63.9 us
    psum x1, blocking collectives, body(): lax.psum((dw_in, dw_out, dkernel, dgain), ('lat', 'lon'))  38.7 us
    all_gather x1, blocking collectives, body(): top_rows = lax.all_gather(masked[nrows - 3:], 'lon', axis=1, tiled=True)  36.8 us
    all_gather x1, blocking collectives, body(): fold_all = lax.all_gather(dfull[nrows:], 'lon', axis=1, tiled=True)  31.3 us
    reduce_sum x8, other arithmetic, body(): jnp.sum(gconv_f * ext[tap_a:tap_a + nrows, tap_b:tap_b + ncols].astype(jn...  22.2 us
    add x1, other arithmetic, transposed(): total = total + kernel[7 * tap_a + tap_b] * window  18.6 us
    reduce_sum x1, other arithmetic, local_block(): mean = jnp.mean(conv_flat, axis=-1, keepdims=True)  18.2 us
    unnamed x251, local copies, waits for them, and re-layouts  13.5 us
  transfers between devices with their start and end apart: 9, of which 3 were waited for; matrix products, arithmetic and copies ran while one was open for 16% of the time, Pallas kernels for 0%

commit v1 on v0

v1 whole, which is shorter than its diff:
```python
import jax
import jax.numpy as jnp
import numpy as np
from jax import lax
from jax.experimental import pallas as pl
from jax.experimental.pallas import tpu as pltpu
from jax.sharding import PartitionSpec as P

F32 = jnp.float32
BF16 = jnp.bfloat16
AXES = ("lat", "lon")
SUB = 8
COLS = 8
QC = COLS + 6
LT = 3
CP = LT * 128
HB = 256
VM = pl.BlockSpec(memory_space=pltpu.VMEM)
SM = pl.BlockSpec(memory_space=pltpu.SMEM)
LIMIT = 60 * 1024 * 1024

EVEN_LON, EVEN_LAT, IS_TOP, LON, START, ME = range(6)


def params():
    return pltpu.CompilerParams(vmem_limit_bytes=LIMIT)


def lanes(l, width):
    return min(128, width - 128 * l)


def tap_rows(k_ref, ks, width):
    ks[...] = jnp.zeros_like(ks)
    for l in range(LT):
        w = lanes(l, width)
        ks[l, : k_ref.shape[0], :w] = k_ref[:, 128 * l : 128 * l + w]


def prepare_kernel(sc, mask_ref, f_ref, c_ref, mf_ref, bk_ref, mk_ref, p1_ref, p2_ref, pad, rows, ct):
    nrows, _, width = f_ref.shape
    tt = nrows // SUB
    m_t = mask_ref[...].astype(F32).T
    for src, dst in ((f_ref, mf_ref), (c_ref, ct)):
        pad[:, :, 256:] = jnp.zeros((nrows, COLS, 128), BF16)
        pad[:, :, :width] = src[...]
        for j in range(nrows):
            s, t = j // tt, j % tt
            m = jnp.broadcast_to(m_t[:, j : j + 1], (COLS, 128))
            at = pl.ds(t * 64 + s, COLS, stride=SUB)
            if src is f_ref:
                mk_ref[at, :] = m
            for l in range(LT):
                v = pad[j, :, 128 * l : 128 * (l + 1)].astype(F32) * m
                dst[l, at, :] = v
                if src is f_ref and (j < 3 or j >= nrows - 3):
                    rows[(0 if j < 3 else 3) + (j if j < 3 else j - nrows + 3), :, 128 * l : 128 * (l + 1)] = v
    for l in range(LT):
        bk_ref[:, 128 * l : 128 * (l + 1)] = ct[l].astype(BF16)
    even = sc[EVEN_LAT]
    p1_ref[...] = rows[pl.ds(3 * even, 3)].astype(BF16)
    p2_ref[...] = rows[pl.ds(3 - 3 * even, 3)].astype(BF16)


def strips_kernel(sc, x_ref, p1_ref, p2_ref, q1_ref, q2_ref, lu):
    n = x_ref.shape[1]
    tt = n // 64
    even_lat, even_lon = sc[EVEN_LAT], sc[EVEN_LON]
    lower = jnp.where(even_lat == 1, p2_ref[...].astype(F32), p1_ref[...].astype(F32))
    upper = jnp.where(even_lat == 1, p1_ref[...].astype(F32), p2_ref[...].astype(F32))
    for l in range(LT):
        for r in range(3):
            lu[l, 8 * r : 8 * r + 8, :] = lower[r, :, 128 * l : 128 * (l + 1)]
            lu[l, 24 + 8 * r : 32 + 8 * r, :] = upper[r, :, 128 * l : 128 * (l + 1)]
        lu[l, 48:, :] = jnp.zeros((16, 128), F32)
    for q_ref, first in ((q1_ref, 5 * even_lon), (q2_ref, 5 - 5 * even_lon)):
        for l in range(LT):
            for c in range(3):
                for t in range(0, tt, 2):
                    a = x_ref[l, pl.ds(pl.multiple_of(t * 64 + (first + c) * 8, 8), 8), :]
                    b = x_ref[l, pl.ds(pl.multiple_of(t * 64 + 64 + (first + c) * 8, 8), 8), :]
                    q_ref[l, (c * tt + t) * 8 : (c * tt + t) * 8 + 16, :] = jnp.concatenate([a, b], 0).astype(BF16)
            k = [lu[l, pl.ds(first + c, 8, stride=8), :] for c in range(3)]
            k.append(jnp.zeros((8, 128), F32))
            q_ref[l, 3 * tt * 8 : 3 * tt * 8 + 32, :] = jnp.concatenate(k, 0).astype(BF16)


def extend(sc, ext, x_ref, q1_ref, q2_ref, p1_ref, p2_ref):
    tt = x_ref.shape[1] // 64
    even_lat, even_lon, top = sc[EVEN_LAT], sc[EVEN_LON], sc[IS_TOP]
    for l in range(LT):
        for t in range(tt):
            ext[l, ((t + 3) * QC + 3) * 8 : ((t + 3) * QC + 3) * 8 + 64, :] = x_ref[l, t * 64 : t * 64 + 64, :]
    sides = ((q1_ref, 11 * even_lon), (q2_ref, 11 - 11 * even_lon))
    for q_ref, first in sides:
        for l in range(LT):
            for c in range(3):
                for t in range(0, tt, 2):
                    v = q_ref[l, (c * tt + t) * 8 : (c * tt + t) * 8 + 16, :].astype(F32)
                    for u in range(2):
                        ext[l, pl.ds(pl.multiple_of(((t + u + 3) * QC + first + c) * 8, 8), 8), :] = v[8 * u : 8 * u + 8]
    for l in range(LT):
        for r in range(3):
            for q in range(QC):
                lo = ext[l, ((tt + r) * QC + q) * 8 : ((tt + r) * QC + q) * 8 + 8, :]
                ext[l, (r * QC + q) * 8 : (r * QC + q) * 8 + 8, :] = pltpu.roll(lo, 1, 0)
                hi = ext[l, ((3 + r) * QC + q) * 8 : ((3 + r) * QC + q) * 8 + 8, :]
                at = ((tt + 3 + r) * QC + q) * 8
                ext[l, at : at + 8, :] = pltpu.roll(hi, 7, 0)
    keep = (1 - top).astype(F32)
    p1, p2 = p1_ref[...].astype(F32), p2_ref[...].astype(F32)
    lower = jnp.where(even_lat == 1, p2, p1)
    upper = jnp.where(even_lat == 1, p1, p2) * keep
    for l in range(LT):
        for r in range(3):
            ext[l, pl.ds((r * QC + 3) * 8, 8, stride=8), :] = lower[r, :, 128 * l : 128 * (l + 1)]
            ext[l, pl.ds(((tt + 3 + r) * QC + 3) * 8 + 7, 8, stride=8), :] = upper[r, :, 128 * l : 128 * (l + 1)]
    for q_ref, first in sides:
        for l in range(LT):
            corner = q_ref[l, 3 * tt * 8 : 3 * tt * 8 + 32, :].astype(F32)
            for c in range(3):
                for r in range(3):
                    ext[l, pl.ds((r * QC + first + c) * 8, 1), :] = corner[8 * c + r : 8 * c + r + 1]
                    ext[l, pl.ds(((tt + 3 + r) * QC + first + c) * 8 + 7, 1), :] = corner[8 * c + 3 + r : 8 * c + 4 + r] * keep


def fold_rows(sc, mir, fold_ref, buf, dst, base):
    units = fold_ref.shape[0]
    for l in range(LT):
        for u in range(units):
            for r in range(3):
                at = (u * 3 + r) * 8
                buf[l, at : at + 8, :] = fold_ref[u, r, :, 128 * l : 128 * (l + 1)].astype(F32)
    total = mir.shape[0]
    for q in range(QC):
        col = sc[START] - 3 + q
        col = jnp.where(col < 0, col + total, col)
        col = jnp.where(col >= total, col - total, col)
        m = mir[col]
        unit = lax.bitwise_xor(lax.shift_right_logical(m, 3), sc[LON])
        at = unit * 24 + lax.bitwise_and(m, 7)
        for k in range(3):
            for l in range(LT):
                dst[l, pl.ds(base + (k * QC + q) * 8 + 7, 1), :] = buf[l, pl.ds(at + (2 - k) * 8, 1), :]


def correlate(ext, ks, tt, flip, store):
    for l in range(LT):

        def column(i, carry, l=l):
            acc = [None] * tt
            for b in range(7):
                k = []
                for a in range(7):
                    tap = 7 * a + b
                    tap = 48 - tap if flip else tap
                    k.append(jnp.broadcast_to(ks[l, tap : tap + 1, :], (8, 128)))
                for u in range(tt + 6):
                    e = ext[l, pl.ds(pl.multiple_of((u * QC + i + b) * 8, 8), 8), :]
                    for a in range(7):
                        t = u - a
                        if 0 <= t < tt:
                            v = k[a] * e
                            acc[t] = v if acc[t] is None else acc[t] + v
            for t in range(tt):
                store(l, t, i, acc[t])
            return carry

        lax.fori_loop(0, COLS, column, 0)


def block_kernel(
    width, sc, mir, k_ref, gain_ref, win_ref, wout_ref, mf_ref, bk_ref, mk_ref, q1_ref, q2_ref, p1_ref, p2_ref, fold_ref,
    out_ref, ext, gc_ref, g1_ref, g2_ref, dw_ref, dgain_ref,
    ks, buf, conv, normed, act, gp, res, rows,
):
    cells = mf_ref.shape[1]
    tt = cells // 64
    hidden = win_ref.shape[1]
    extend(sc, ext, mf_ref, q1_ref, q2_ref, p1_ref, p2_ref)

    @pl.when(sc[IS_TOP] == 1)
    def _():
        fold_rows(sc, mir, fold_ref, buf, ext, (tt + 3) * QC * 8)

    tap_rows(k_ref, ks, width)

    def put(l, t, i, v):
        conv[pl.ds(pl.multiple_of(t * 64 + i * 8, 8), 8), 128 * l : 128 * (l + 1)] = v

    correlate(ext, ks, tt, False, put)
    size = 256
    gain = gain_ref[...]
    valid = (lax.broadcasted_iota(jnp.int32, (1, CP), 1) < width).astype(F32)
    dgain_ref[...] = jnp.zeros_like(dgain_ref)
    inv = 1.0 / width
    coeff = 0.7978845608028654

    def chunk(n, carry):
        at = pl.ds(pl.multiple_of(n * size, size), size)
        x = conv[at, :]
        mean = jnp.sum(x, axis=-1, keepdims=True) * inv
        cen = (x - mean) * valid
        var = jnp.sum(cen * cen, axis=-1, keepdims=True) * inv
        rstd = lax.rsqrt(var + 1e-06)
        nhat = cen * rstd
        nb = (nhat * gain).astype(BF16)
        normed[at, :] = nb
        back = bk_ref[at, :]
        for h in range(0, hidden, HB):
            v = jnp.dot(nb, win_ref[:, h : h + HB], preferred_element_type=F32)
            g = lax.dot_general(back, wout_ref[h : h + HB, :], (((1,), (1,)), ((), ())), preferred_element_type=F32)
            v2 = v * v
            half = 0.5 + 0.5 * jnp.tanh(v * (coeff + (coeff * 0.044715) * v2))
            a = v * half
            slope = half + a * (1.0 - half) * (2.0 * coeff + (2.0 * coeff * 0.134145) * v2)
            act[at, h : h + HB] = a.astype(BF16)
            gp[at, h : h + HB] = (g * slope).astype(BF16)
        mixed = jnp.dot(act[at, :], wout_ref[...], preferred_element_type=F32)
        gn = lax.dot_general(gp[at, :], win_ref[...], (((1,), (1,)), ((), ())), preferred_element_type=F32)
        m = mk_ref[at, :]
        for l in range(LT):
            res[l, at, :] = mf_ref[l, at, :] + m * mixed[:, 128 * l : 128 * (l + 1)]
        dgain_ref[...] += jnp.broadcast_to(jnp.sum(gn * nhat, axis=0, keepdims=True), dgain_ref.shape)
        s = gn * gain
        m1 = jnp.sum(s, axis=-1, keepdims=True) * inv
        m2 = jnp.sum(s * nhat, axis=-1, keepdims=True) * inv
        gc = (rstd * (s - m1 - nhat * m2) * valid).astype(BF16).astype(F32)
        for l in range(LT):
            gc_ref[l, at, :] = gc[:, 128 * l : 128 * (l + 1)]
        return carry

    lax.fori_loop(0, cells // size, chunk, 0)
    for l in range(LT):
        for r in range(3):
            rows[r, :, 128 * l : 128 * (l + 1)] = gc_ref[l, pl.ds(r * 64, 8, stride=8), :]
            rows[3 + r, :, 128 * l : 128 * (l + 1)] = gc_ref[l, pl.ds((tt - 3 + r) * 64 + 7, 8, stride=8), :]
    even = sc[EVEN_LAT]
    g1_ref[...] = rows[pl.ds(3 * even, 3)].astype(BF16)
    g2_ref[...] = rows[pl.ds(3 - 3 * even, 3)].astype(BF16)
    for m, (left, right) in enumerate(((normed, gp), (bk_ref, act))):
        tiles = (hidden // 128) * (DWR // 16)
        for h in range(0, hidden, HB):
            d = lax.dot_general(
                left[...], right[:, h : h + HB], (((0,), (0,)), ((), ())), preferred_element_type=F32
            ).astype(BF16)
            for u in range(HB // 128):
                first = m * tiles + (h // 128 + u) * (DWR // 16)
                for r in range(DWR // 16):
                    dw_ref[first + r] = d[16 * r : 16 * r + 16, 128 * u : 128 * u + 128]
    for j in range(tt * SUB):
        s, t = j // tt, j % tt
        for l in range(LT):
            w = lanes(l, width)
            out_ref[j, :, 128 * l : 128 * l + w] = res[l, pl.ds(t * 64 + s, 8, stride=8), :][:, :w].astype(BF16)


DWR = 304
DKR = 64


def taps_kernel(ext, gc_ref, dgain_ref, dk_ref, part, rows):
    tt = gc_ref.shape[1] // 64
    for l in range(LT):

        def tap_column(b, carry, l=l):
            acc = [jnp.zeros((8, 128), F32)] * 7
            for i in range(COLS):
                g = [gc_ref[l, t * 64 + i * 8 : t * 64 + i * 8 + 8, :] for t in range(tt)]
                for u in range(tt + 6):
                    e = ext[l, pl.ds(pl.multiple_of((u * QC + i + b) * 8, 8), 8), :]
                    for a in range(7):
                        t = u - a
                        if 0 <= t < tt:
                            acc[a] = acc[a] + g[t] * e
            for a in range(7):
                part[l, pl.ds(pl.multiple_of((7 * a + b) * 8, 8), 8), :] = acc[a]
            return carry

        lax.fori_loop(0, 7, tap_column, 0)
    rows[...] = jnp.zeros_like(rows)
    for l in range(LT):
        for k in range(49):
            rows[l, k : k + 1, :] = jnp.sum(part[l, 8 * k : 8 * k + 8, :], axis=0, keepdims=True)
        rows[l, 49:50, :] = dgain_ref[0:1, 128 * l : 128 * (l + 1)]
        for r in range(DKR // 16):
            dk_ref[l * (DKR // 16) + r] = rows[l, 16 * r : 16 * r + 16, :].astype(BF16)


def field_kernel(
    width, sc, mir, k_ref, gc_ref, bk_ref, mk_ref, q1_ref, q2_ref, p1_ref, p2_ref, fold_ref, out_ref, ks, buf, ext, ghost, dm
):
    cells = gc_ref.shape[1]
    tt = cells // 64
    extend(sc, ext, gc_ref, q1_ref, q2_ref, p1_ref, p2_ref)
    tap_rows(k_ref, ks, width)

    def put(l, t, i, v):
        dm[l, pl.ds(pl.multiple_of(t * 64 + i * 8, 8), 8), :] = v

    correlate(ext, ks, tt, True, put)

    @pl.when(sc[IS_TOP] == 1)
    def _():
        ghost[...] = jnp.zeros_like(ghost)
        fold_rows(sc, mir, fold_ref, buf, ghost, 0)
        for l in range(LT):

            def column(i, carry, l=l):
                for k in range(3):
                    at = pl.ds(pl.multiple_of((tt - 1 - k) * 64 + i * 8, 8), 8)
                    acc = dm[l, at, :]
                    for r in range(3 - k):
                        for b in range(7):
                            tap = 7 * (4 + k + r) + b
                            e = ghost[l, pl.ds(pl.multiple_of((r * QC + i + b) * 8, 8), 8), :]
                            acc = acc + jnp.broadcast_to(ks[l, tap : tap + 1, :], (8, 128)) * e
                    dm[l, at, :] = acc
                return carry

            lax.fori_loop(0, COLS, column, 0)

    for l in range(LT):
        for n in range(0, cells, 64):
            dm[l, n : n + 64, :] = dm[l, n : n + 64, :] * mk_ref[n : n + 64, :] + bk_ref[
                n : n + 64, 128 * l : 128 * (l + 1)
            ].astype(F32)
    for j in range(tt * SUB):
        s, t = j // tt, j % tt
        for l in range(LT):
            w = lanes(l, width)
            out_ref[j, :, 128 * l : 128 * l + w] = dm[l, pl.ds(t * 64 + s, 8, stride=8), :][:, :w].astype(BF16)


def unpack_kernel(width, hidden, factor, per, sc, x_ref, gin_ref, gout_ref, gk_ref, gg_ref):
    blocks = (hidden + 127) // 128
    blocks += blocks % 2
    tr = DWR // 16

    def tile(n):
        chunk = lax.bitwise_xor(jnp.int32(n // per), sc[ME])
        return x_ref[chunk * per + n % per].astype(F32) * factor

    for cb in range(blocks):
        w = min(128, hidden - 128 * cb)
        if w <= 0:
            continue
        for r in range(tr):
            rows = min(16, width - 16 * r)
            gin_ref[16 * r : 16 * r + rows, 128 * cb : 128 * cb + w] = tile(cb * tr + r)[:rows, :w]
        parts = [tile((blocks + cb) * tr + r) for r in range(tr)] + [jnp.zeros((CP - DWR, 128), F32)]
        full = jnp.concatenate(parts, axis=0).T
        gout_ref[128 * cb : 128 * cb + w, :] = full[:w, :width]
    for l in range(LT):
        w = lanes(l, width)
        base = 2 * blocks * tr + l * (DKR // 16)
        taps = jnp.concatenate([tile(base + r) for r in range(DKR // 16)], axis=0)
        gk_ref[:, 128 * l : 128 * l + w] = taps[:49, :w]
        gg_ref[:, 128 * l : 128 * l + w] = taps[49:50, :w]


def swaps(n_lat, n_lon, bits):
    ml, mo = bits
    return [(l * n_lon + o, (l ^ ml) * n_lon + (o ^ mo)) for l in range(n_lat) for o in range(n_lon)]


def lat_swaps(n_lat, n_lon):
    first = [(l * n_lon + o, (l ^ 1) * n_lon + o) for l in range(n_lat) for o in range(n_lon)]
    second = []
    for l in range(n_lat):
        for o in range(n_lon):
            if l == n_lat - 1:
                second.append((l * n_lon + o, l * n_lon + (o ^ 1)))
            elif l > 0:
                other = l + 1 if l % 2 else l - 1
                second.append((l * n_lon + o, other * n_lon + o))
    return first, second


def lon_swaps(n_lat, n_lon):
    first = [(l * n_lon + o, l * n_lon + (o ^ 1)) for l in range(n_lat) for o in range(n_lon)]
    second = []
    for l in range(n_lat):
        for o in range(n_lon):
            other = (o + 1) % n_lon if o % 2 else (o - 1) % n_lon
            second.append((l * n_lon + o, l * n_lon + other))
    return first, second


def fold_gather(mine, other, n_lat, n_lon):
    buf = jnp.stack([mine, other])
    bit = 2
    top = n_lat - 1
    while bit < n_lon:
        pairs = [(top * n_lon + o, top * n_lon + (o ^ bit)) for o in range(n_lon)]
        buf = jnp.concatenate([buf, lax.ppermute(buf, AXES, pairs)])
        bit *= 2
    return buf


def stages(n_lat, n_lon):
    out = [[(1, 0)]]
    rest = [(1 << b, 0) for b in range(1, n_lat.bit_length() - 1)] + [(0, 1 << b) for b in range(n_lon.bit_length() - 1)]
    while rest:
        out.append(rest[:2])
        rest = rest[2:]
    return out


def group_index(group, lat, lon):
    value = jnp.int32(0)
    for ml, mo in group:
        bit = (lat & ml) != 0 if ml else (lon & mo) != 0
        value = 2 * value + bit.astype(jnp.int32)
    return value


def group_masks(group):
    masks = []
    for d in range(1 << len(group)):
        ml = mo = 0
        for k, (gl, go) in enumerate(group):
            if d >> (len(group) - 1 - k) & 1:
                ml, mo = ml | gl, mo | go
        masks.append((ml, mo))
    return masks


def all_sum(x, lat, lon, n_lat, n_lon):
    groups = stages(n_lat, n_lon)
    for group in groups:
        n = 1 << len(group)
        x = x.reshape((n, x.shape[0] // n) + x.shape[1:])
        idx = group_index(group, lat, lon)
        masks = group_masks(group)
        got = []
        for d in range(1, n):
            piece = lax.dynamic_index_in_dim(x, idx ^ d, 0, False)
            got.append(lax.ppermute(piece, AXES, swaps(n_lat, n_lon, masks[d])))
        total = lax.dynamic_index_in_dim(x, idx, 0, False).astype(F32)
        for g in got:
            total = total + g.astype(F32)
        x = total.astype(BF16)
    for group in reversed(groups):
        masks = group_masks(group)
        x = jnp.concatenate(
            [x] + [lax.ppermute(x, AXES, swaps(n_lat, n_lon, masks[d])) for d in range(1, len(masks))], axis=0
        )
    return x


def body(field_in, sea_mask, mirror, kernel, norm_gain, proj_in, proj_out, cotangent):
    nrows, ncols, width = field_in.shape
    hidden = proj_in.shape[1]
    n_lat, n_lon = lax.axis_size("lat"), lax.axis_size("lon")
    assert ncols == COLS and nrows % 16 == 0 and n_lat % 2 == 0 and n_lon % 2 == 0
    lat, lon = lax.axis_index("lat"), lax.axis_index("lon")
    cells = nrows * ncols
    tt = nrows // SUB
    groups = stages(n_lat, n_lon)
    me = jnp.int32(0)
    for group in groups:
        me = (me << len(group)) + group_index(group, lat, lon)
    sc = jnp.stack(
        [1 - lon % 2, 1 - lat % 2, (lat == n_lat - 1).astype(jnp.int32), lon, lon * ncols, me, jnp.int32(0), jnp.int32(0)]
    ).astype(jnp.int32)
    hp = -(-hidden // HB) * HB
    win = jnp.pad(proj_in, ((0, CP - width), (0, hp - hidden)))
    wout = jnp.pad(proj_out, ((0, hp - hidden), (0, CP - width)))
    gain = jnp.pad(norm_gain, (0, CP - width)).reshape(1, CP)

    s = jax.ShapeDtypeStruct
    row_msg = s((3, COLS, CP), BF16)
    strip_msg = s((LT, 3 * tt * 8 + 32, 128), BF16)
    mf, bk, mk, p1, p2 = pl.pallas_call(
        prepare_kernel,
        out_shape=(s((LT, cells, 128), F32), s((cells, CP), BF16), s((cells, 128), F32), row_msg, row_msg),
        in_specs=[SM, VM, VM, VM],
        out_specs=(VM,) * 5,
        scratch_shapes=[
            pltpu.VMEM((nrows, COLS, CP), BF16),
            pltpu.VMEM((6, COLS, CP), F32),
            pltpu.VMEM((LT, cells, 128), F32),
        ],
        compiler_params=params(),
        name="prepare",
    )(sc, sea_mask, field_in, cotangent)

    lat1, lat2 = lat_swaps(n_lat, n_lon)
    lon1, lon2 = lon_swaps(n_lat, n_lon)

    def halo(x, own1, own2):
        r1 = lax.ppermute(own1, AXES, lat1)
        r2 = lax.ppermute(own2, AXES, lat2)
        q1, q2 = pl.pallas_call(
            strips_kernel,
            out_shape=(strip_msg, strip_msg),
            in_specs=[SM, VM, VM, VM],
            out_specs=(VM, VM),
            scratch_shapes=[pltpu.VMEM((LT, 64, 128), F32)],
            compiler_params=params(),
            name="strips",
        )(sc, x, r1, r2)
        c1 = lax.ppermute(q1, AXES, lon1)
        c2 = lax.ppermute(q2, AXES, lon2)
        return c1, c2, r1, r2, fold_gather(own2, r2, n_lat, n_lon)

    halos = halo(mf, p1, p2)
    blocks = hp // 128
    count = 2 * blocks * (DWR // 16)
    out, ext, gc, g1, g2, dw, dgain = pl.pallas_call(
        lambda *refs: block_kernel(width, *refs),
        out_shape=(
            s((nrows, COLS, width), BF16),
            s((LT, (tt + 6) * QC * 8, 128), F32),
            s((LT, cells, 128), F32),
            row_msg,
            row_msg,
            s((count, 16, 128), BF16),
            s((8, CP), F32),
        ),
        in_specs=[SM, SM] + [VM] * 12,
        out_specs=(VM,) * 7,
        scratch_shapes=[
            pltpu.VMEM((LT, 56, 128), F32),
            pltpu.VMEM((LT, n_lon * 24, 128), F32),
            pltpu.VMEM((cells, CP), F32),
            pltpu.VMEM((cells, CP), BF16),
            pltpu.VMEM((cells, hp), BF16),
            pltpu.VMEM((cells, hp), BF16),
            pltpu.VMEM((LT, cells, 128), F32),
            pltpu.VMEM((6, COLS, CP), F32),
        ],
        compiler_params=params(),
        name="block",
    )(sc, mirror, kernel, gain, win, wout, mf, bk, mk, *halos)

    ghalos = halo(gc, g1, g2)
    dk = pl.pallas_call(
        taps_kernel,
        out_shape=s((LT * DKR // 16, 16, 128), BF16),
        in_specs=[VM] * 3,
        out_specs=VM,
        scratch_shapes=[pltpu.VMEM((LT, 49 * 8, 128), F32), pltpu.VMEM((LT, DKR, 128), F32)],
        compiler_params=params(),
        name="taps",
    )(ext, gc, dgain)
    grad_field = pl.pallas_call(
        lambda *refs: field_kernel(width, *refs),
        out_shape=s((nrows, COLS, width), BF16),
        in_specs=[SM, SM] + [VM] * 9,
        out_specs=VM,
        scratch_shapes=[
            pltpu.VMEM((LT, 56, 128), F32),
            pltpu.VMEM((LT, n_lon * 24, 128), F32),
            pltpu.VMEM((LT, (tt + 6) * QC * 8, 128), F32),
            pltpu.VMEM((LT, 3 * QC * 8, 128), F32),
            pltpu.VMEM((LT, cells, 128), F32),
        ],
        compiler_params=params(),
        name="field",
    )(sc, mirror, kernel, gc, bk, mk, *ghalos)

    devices = n_lat * n_lon
    used = count + LT * DKR // 16
    per = -(-used // devices)
    packed = jnp.concatenate([dw, dk, jnp.zeros((per * devices - used, 16, 128), BF16)], axis=0)
    summed = all_sum(packed, lat, lon, n_lat, n_lon)
    factor = float(1.0 / np.sqrt(np.float32(nrows * n_lat * ncols * n_lon)))
    gin, gout, gk, gg = pl.pallas_call(
        lambda *refs: unpack_kernel(width, hidden, factor, per, *refs),
        out_shape=(s((width, hidden), F32), s((hidden, width), F32), s((49, width), F32), s((1, width), F32)),
        in_specs=[SM, VM],
        out_specs=(VM,) * 4,
        compiler_params=params(),
        name="unpack",
    )(sc, summed)
    return out, grad_field, gin, gout, gk, gg.reshape(width)


def solution(mesh):
    in_specs = (
        P("lat", "lon", None),
        P("lat", "lon"),
        P(),
        P(),
        P(),
        P(),
        P(),
        P("lat", "lon", None),
    )
    out_specs = (P("lat", "lon", None), P("lat", "lon", None), P(), P(), P(), P())
    return jax.shard_map(body, mesh=mesh, in_specs=in_specs, out_specs=out_specs, check_vma=False)
```

time: 351 us -> 172 us (0.49)
  blocking collectives: 107 us -> 0 us
  other arithmetic: 74.9 us -> 9.21 us
  Pallas kernels: 0 us -> 56 us
  waiting for transfers between devices: 75.4 us -> 39.7 us
  starting transfers between devices: 14.4 us -> 42 us
  matrix products: 19.6 us -> 0 us
  between operations: 16.9 us -> 0.98 us
  local copies, waits for them, and re-layouts: 39.1 us -> 23.8 us
    all_gather x2 -> x0, blocking collectives: 68.2 us -> none  [the longest x1 36.8 us: body(): top_rows = lax.all_gather(masked[nrows - 3:], 'lon', axis=1, tiled=True)]
    psum x1 -> x0, waiting for transfers between devices: 63.9 us -> none  [body(): lax.psum((dw_in, dw_out, dkernel, dgain), ('lat', 'lon'))]
    pallas_call x0 -> x7, Pallas kernels: none -> 56 us  [the longest x1 20.2 us: body(): pl.pallas_call(lambda *refs: block_kernel(width, *refs), out_shape=(s((nr...]
    reduce_sum x10 -> x0, other arithmetic: 40.7 us -> none  [the longest x8 22.2 us: body(): jnp.sum(gconv_f * ext[tap_a:tap_a + nrows, tap_b:tap_b + ncols].astype(jn...]
    psum x1 -> x0, blocking collectives: 38.7 us -> none  [body(): lax.psum((dw_in, dw_out, dkernel, dgain), ('lat', 'lon'))]
    ppermute x8 -> x26, waiting for transfers between devices: 11.5 us -> 39.7 us  [the longest x7 16.8 us: all_sum(): got.append(lax.ppermute(piece, AXES, swaps(n_lat, n_lon, masks[d])))]
    ppermute x8 -> x26, starting transfers between devices: 14.4 us -> 42 us  [the longest x2 11 us: halo(): r1 = lax.ppermute(own1, AXES, lat1)]
    dot_general x6 -> x0, matrix products: 19.6 us -> none  [the longest x1 5.75 us: local_block(): mixed = jnp.dot(act, proj_out, preferred_element_type=jnp.float32)]
  transfers between devices with their start and end apart: 9 -> 26, of which waited for: 3 -> 15; matrix products, arithmetic and copies ran while one was open for 16% -> 9% of each run, Pallas kernels for 0% -> 9%
where the time goes in v1:
time: 172 us
  Pallas kernels  56 us (33%)
  starting transfers between devices  42 us (24%)
  waiting for transfers between devices  39.7 us (23%)
  local copies, waits for them, and re-layouts  23.8 us (14%)
  other arithmetic  9.21 us (5%)
    pallas_call x1, Pallas kernels, body(): pl.pallas_call(lambda *refs: block_kernel(width, *refs), out_shape=(s((nr...  20.2 us
    unnamed x49, local copies, waits for them, and re-layouts  19.1 us
    ppermute x7, waiting for transfers between devices, all_sum(): got.append(lax.ppermute(piece, AXES, swaps(n_lat, n_lon, masks[d])))  16.8 us
    ppermute x2, waiting for transfers between devices, halo(): c1 = lax.ppermute(q1, AXES, lon1)  14 us
    pallas_call x1, Pallas kernels, body(): pl.pallas_call(taps_kernel, out_shape=s((LT * DKR // 16, 16, 128), BF16),...  12.3 us
    ppermute x2, starting transfers between devices, halo(): r1 = lax.ppermute(own1, AXES, lat1)  11 us
    pallas_call x1, Pallas kernels, body(): pl.pallas_call(lambda *refs: field_kernel(width, *refs), out_shape=s((nro...  10.7 us
    ppermute x7, starting transfers between devices, all_sum(): got.append(lax.ppermute(piece, AXES, swaps(n_lat, n_lon, masks[d])))  9.51 us
  transfers between devices with their start and end apart: 26, of which 15 were waited for; matrix products, arithmetic and copies ran while one was open for 9% of the time, Pallas kernels for 9%

profile of v1, /device:TPU:0, one launch (start us, length us, event | category | flops | bytes accessed | tf_op | source)
XLA Modules:
  0.0 171.7 jit_solution(4238517217632969296)
XLA Ops:
  0.7 2.6 %copy.16.f_ref = bf16[128,8,300]{2,1,0:T(8,128)(2,1)} copy(bf16[128,8,300]{0,1,2:T(8,128)(2,1)} %param.8) | data formatting | bytes 1228800 | tf_op args[0]
  3.3 1.5 copy.17.c_ref
  6.1 4.3 %prepare.1 = (f32[3,1024,128]{2,1,0:T(8,128)}, bf16[1024,384]{1,0:T(8,128)(2,1)}, f32[1024,128]{1,0:T(8,128)}, bf16[3,8,384]{2,1,0:T(8,128)(2,1)}, bf16[3,8,384]{2,1,0:T(8,128)(2,1)}) custom-call(s32[8]{0:T(128)} %stack.49.sc.refs_0_, s32[128,8]{1,0:T(8,128)} %copy.15.mask_ref, bf16[128,8,300]{2,1,0:T(8,128)(2,1)} %copy.16.f_ref, ...), custom_call_target="tpu_custom_call" | custom-call | tf_op jit(solution)/shard_map/prepare/pallas_call | solution.py:475
  12.6 6.0 %collective-permute-start = (bf16[3,8,384]{2,1,0:T(8,128)(2,1)}, bf16[3,8,384]{2,1,0:T(8,128)(2,1)S(1)}, u32[]{:S(2)}, u32[]{:S(2)}) collective-permute-start(bf16[3,8,384]{2,1,0:T(8,128)(2,1)} %get-tuple-element.29), channel_id=1, source_target_pairs={{0,8},{1,9},{2,10},{3,11},{4,12},{5,13},{6,14},{7,15},{8,0},{9,1},... | collective-permute-start | bytes 55304 | tf_op jit(solution)/shard_map/ppermute | solution.py:493
  20.3 2.4 %strips.2 = (bf16[3,416,128]{2,1,0:T(8,128)(2,1)}, bf16[3,416,128]{2,1,0:T(8,128)(2,1)}) custom-call(s32[8]{0:T(128)} %stack.49.sc.refs_0_, f32[3,1024,128]{2,1,0:T(8,128)} %get-tuple-element.26.x_ref.refs_6_, bf16[3,8,384]{2,1,0:T(8,128)(2,1)} %copy-done.13, bf16[3,8,384]{2,1,0:T(8,128)(2,1)} %copy-done.6), custom_call_target="tpu_custom_call" | custom-call | tf_op jit(solution)/shard_map/strips/pallas_call | solution.py:495
  24.2 3.6 %collective-permute-start.3 = (bf16[3,416,128]{2,1,0:T(8,128)(2,1)}, bf16[3,416,128]{2,1,0:T(8,128)(2,1)S(1)}, u32[]{:S(2)}, u32[]{:S(2)}) collective-permute-start(bf16[3,416,128]{2,1,0:T(8,128)(2,1)} %get-tuple-element.32), channel_id=1, source_target_pairs={{0,7},{1,2},{2,1},{3,4},{4,3},{5,6},{6,5},{7,0},{8,15},{9,10},{10,... | collective-permute-start | bytes 958472 | tf_op jit(solution)/shard_map/ppermute | solution.py:505
  33.7 5.9 %collective-permute-done.2.refs_9_ = bf16[3,416,128]{2,1,0:T(8,128)(2,1)S(1)} collective-permute-done((bf16[3,416,128]{2,1,0:T(8,128)(2,1)}, bf16[3,416,128]{2,1,0:T(8,128)(2,1)S(1)}, u32[]{:S(2)}, u32[]{:S(2)}) %collective-permute-start.2) | collective-permute-done | bytes 319520 | tf_op jit(solution)/shard_map/ppermute | solution.py:504
  40.4 20.2 %block.1 = (bf16[128,8,300]{2,1,0:T(8,128)(2,1)}, f32[3,2464,128]{2,1,0:T(8,128)}, f32[3,1024,128]{2,1,0:T(8,128)}, bf16[3,8,384]{2,1,0:T(8,128)(2,1)}, bf16[3,8...) custom-call(s32[8]{0:T(128)} %stack.49.sc.refs_0_, s32[64]{0:T(128)} %refs_1_.3, ...), custom_call_target="tpu_custom_call" | custom-call | tf_op jit(solution)/shard_map/block/pallas_call | solution.py:511
  60.6 12.3 %taps.1 = bf16[12,16,128]{2,1,0:T(8,128)(2,1)} custom-call(f32[3,2464,128]{2,1,0:T(8,128)} %get-tuple-element.40.ext, f32[3,1024,128]{2,1,0:T(8,128)} %get-tuple-element.34.x_ref.refs_3_.gc_ref, f32[8,384]{1,0:T(8,128)} %get-tuple-element.41.dgain_ref), custom_call_target="tpu_custom_call" | custom-call | tf_op jit(solution)/shard_map/taps/pallas_call | solution.py:539
  72.8 3.1 %maximum_maximum_fusion = bf16[416,16,128]{2,1,0:T(8,128)(2,1)S(1)} fusion(bf16[12,16,128]{2,1,0:T(8,128)(2,1)} %taps.1, bf16[380,16,128]{2,1,0:T(8,128)(2,1)} %get-tuple-element.39, bf16[416]{0:T(512)(128)(2,1)S(1)} %pad.21.clone), kind=kLoop, calls=%fused_computation | loop fusion | flops 1703936 | bytes 3310400 | tf_op jit(solution)/shard_map/concatenate | solution.py:567
  76.2 2.3 %collective-permute-done.12 = bf16[208,16,128]{2,1,0:T(8,128)(2,1)S(1)} collective-permute-done((bf16[208,16,128]{2,1,0:T(8,128)(2,1)S(1)}, bf16[208,16,128]{2,1,0:T(8,128)(2,1)S(1)}, u32[]{:S(2)}, u32[]{:S(2)}) %collective-permute-start.12) | collective-permute-done | bytes 852000 | tf_op jit(solution)/shard_map/ppermute | solution.py:439
  78.9 1.6 collective-permute-start.13
  80.5 3.4 %collective-permute-start.14 = (bf16[52,16,128]{2,1,0:T(8,128)(2,1)S(1)}, bf16[52,16,128]{2,1,0:T(8,128)(2,1)S(1)}, u32[]{:S(2)}, u32[]{:S(2)}) collective-permute-start(bf16[52,16,128]{2,1,0:T(8,128)(2,1)S(1)} %get-tuple-element.56), channel_id=1, source_target_pairs={{0,16},{1,17},{2,18},{3,19},{4,20},{5,21},{6,22},{7,23},{8,24},{9,... | collective-permute-start | bytes 638984 | tf_op jit(solution)/shard_map/ppermute | solution.py:439
  83.9 2.8 %collective-permute-done.13 = bf16[52,16,128]{2,1,0:T(8,128)(2,1)S(1)} collective-permute-done((bf16[52,16,128]{2,1,0:T(8,128)(2,1)S(1)}, bf16[52,16,128]{2,1,0:T(8,128)(2,1)S(1)}, u32[]{:S(2)}, u32[]{:S(2)}) %collective-permute-start.13) | collective-permute-done | bytes 213024 | tf_op jit(solution)/shard_map/ppermute | solution.py:439
  86.7 6.3 %collective-permute-done.14 = bf16[52,16,128]{2,1,0:T(8,128)(2,1)S(1)} collective-permute-done((bf16[52,16,128]{2,1,0:T(8,128)(2,1)S(1)}, bf16[52,16,128]{2,1,0:T(8,128)(2,1)S(1)}, u32[]{:S(2)}, u32[]{:S(2)}) %collective-permute-start.14) | collective-permute-done | bytes 213024 | tf_op jit(solution)/shard_map/ppermute | solution.py:439
  93.9 2.7 %collective-permute-start.16 = (bf16[13,16,128]{2,1,0:T(8,128)(2,1)S(1)}, bf16[13,16,128]{2,1,0:T(8,128)(2,1)S(1)}, u32[]{:S(2)}, u32[]{:S(2)}) collective-permute-start(bf16[13,16,128]{2,1,0:T(8,128)(2,1)S(1)} %get-tuple-element.63), channel_id=1, source_target_pairs={{0,4},{1,5},{2,6},{3,7},{4,0},{5,1},{6,2},{7,3},{8,12},{9,13},{10,... | collective-permute-start | bytes 159752 | tf_op jit(solution)/shard_map/ppermute | solution.py:439
  99.6 1.6 collective-permute-done.17
  101.3 1.7 collective-permute-done.18
  103.6 1.9 %collective-permute-start.20 = (bf16[13,16,128]{2,1,0:T(8,128)(2,1)S(1)}, bf16[13,16,128]{2,1,0:T(8,128)(2,1)S(1)}, u32[]{:S(2)}, u32[]{:S(2)}) collective-permute-start(bf16[13,16,128]{2,1,0:T(8,128)(2,1)S(1)} %get-tuple-element.53), channel_id=1, source_target_pairs={{0,2},{1,3},{2,0},{3,1},{4,6},{5,7},{6,4},{7,5},{8,10},{9,11},{10,... | collective-permute-start | bytes 159752 | tf_op jit(solution)/shard_map/ppermute | solution.py:447
  105.5 2.5 %collective-permute-start.21 = (bf16[13,16,128]{2,1,0:T(8,128)(2,1)S(1)}, bf16[13,16,128]{2,1,0:T(8,128)(2,1)S(1)}, u32[]{:S(2)}, u32[]{:S(2)}) collective-permute-start(bf16[13,16,128]{2,1,0:T(8,128)(2,1)S(1)} %get-tuple-element.53), channel_id=1, source_target_pairs={{0,6},{1,7},{2,4},{3,5},{4,2},{5,3},{6,0},{7,1},{8,14},{9,15},{10,... | collective-permute-start | bytes 159752 | tf_op jit(solution)/shard_map/ppermute | solution.py:447
  109.0 2.5 %collective-permute-done.21 = bf16[13,16,128]{2,1,0:T(8,128)(2,1)S(1)} collective-permute-done((bf16[13,16,128]{2,1,0:T(8,128)(2,1)S(1)}, bf16[13,16,128]{2,1,0:T(8,128)(2,1)S(1)}, u32[]{:S(2)}, u32[]{:S(2)}) %collective-permute-start.21) | collective-permute-done | bytes 53280 | tf_op jit(solution)/shard_map/ppermute | solution.py:447
  111.5 1.5 collective-permute-start.22
  118.7 2.6 %collective-permute-done.23 = bf16[52,16,128]{2,1,0:T(8,128)(2,1)S(1)} collective-permute-done((bf16[52,16,128]{2,1,0:T(8,128)(2,1)S(1)}, bf16[52,16,128]{2,1,0:T(8,128)(2,1)S(1)}, u32[]{:S(2)}, u32[]{:S(2)}) %collective-permute-start.23) | collective-permute-done | bytes 213024 | tf_op jit(solution)/shard_map/ppermute | solution.py:447
  124.2 5.0 %collective-permute-start.6 = (bf16[3,8,384]{2,1,0:T(8,128)(2,1)S(1)}, bf16[3,8,384]{2,1,0:T(8,128)(2,1)S(1)}, u32[]{:S(2)}, u32[]{:S(2)}) collective-permute-start(bf16[3,8,384]{2,1,0:T(8,128)(2,1)S(1)} %copy-done.17), channel_id=1, source_target_pairs={{0,8},{1,9},{2,10},{3,11},{4,12},{5,13},{6,14},{7,15},{8,0},{9,1},... | collective-permute-start | bytes 55304 | tf_op jit(solution)/shard_map/ppermute | solution.py:493
  130.6 2.4 %strips.3 = (bf16[3,416,128]{2,1,0:T(8,128)(2,1)}, bf16[3,416,128]{2,1,0:T(8,128)(2,1)}) custom-call(s32[8]{0:T(128)} %stack.49.sc.refs_0_, f32[3,1024,128]{2,1,0:T(8,128)} %get-tuple-element.34.x_ref.refs_3_.gc_ref, bf16[3,8,384]{2,1,0:T(8,128)(2,1)} %copy-done.12, bf16[3,8,384]{2,1,0:T(8,128)(2,1)} %copy-done.5), custom_call_target="tpu_custom_call" | custom-call | tf_op jit(solution)/shard_map/strips/pallas_call | solution.py:495
  133.0 3.7 %collective-permute-start.9 = (bf16[3,416,128]{2,1,0:T(8,128)(2,1)}, bf16[3,416,128]{2,1,0:T(8,128)(2,1)}, u32[]{:S(2)}, u32[]{:S(2)}) collective-permute-start(bf16[3,416,128]{2,1,0:T(8,128)(2,1)} %get-tuple-element.38), channel_id=1, source_target_pairs={{0,7},{1,2},{2,1},{3,4},{4,3},{5,6},{6,5},{7,0},{8,15},{9,10},{10,... | collective-permute-start | bytes 958472 | tf_op jit(solution)/shard_map/ppermute | solution.py:505
  140.2 1.6 pad_maximum_fusion.2.refs_10_
  141.8 8.1 %collective-permute-done.8.refs_6_ = bf16[3,416,128]{2,1,0:T(8,128)(2,1)} collective-permute-done((bf16[3,416,128]{2,1,0:T(8,128)(2,1)}, bf16[3,416,128]{2,1,0:T(8,128)(2,1)}, u32[]{:S(2)}, u32[]{:S(2)}) %collective-permute-start.8) | collective-permute-done | bytes 319520 | tf_op jit(solution)/shard_map/ppermute | solution.py:504
  149.9 10.7 %field.1 = bf16[128,8,300]{2,1,0:T(8,128)(2,1)} custom-call(s32[8]{0:T(128)} %stack.49.sc.refs_0_, s32[64]{0:T(128)} %refs_1_.3, f32[49,300]{1,0:T(8,128)} %refs_2_.3, f32[3,1024,128]{2,1,0:T(8,128)} %get-tuple-element.34.x_ref.refs_3_.gc_ref, bf16[1024,384]{1,0:T(8,128)(2,1)} %get-tuple-element.27.refs_7_.refs_4_, ...), custom_call_target="tpu_custom_call" | custom-call | tf_op jit(solution)/shard_map/field/pallas_call | solution.py:548
  160.6 2.6 %copy.19 = bf16[128,8,300]{0,1,2:T(8,128)(2,1)} copy(bf16[128,8,300]{2,1,0:T(8,128)(2,1)} %field.1) | data formatting | bytes 1228800
  164.6 3.8 %unpack.1 = (f32[300,1200]{1,0:T(8,128)}, f32[1200,300]{1,0:T(8,128)}, f32[49,300]{1,0:T(8,128)}, f32[1,300]{1,0:T(1,128)}) custom-call(s32[8]{0:T(128)} %stack.49.sc.refs_0_, bf16[416,16,128]{2,1,0:T(8,128)(2,1)} %copy-done), custom_call_target="tpu_custom_call" | custom-call | tf_op jit(solution)/shard_map/unpack/pallas_call | solution.py:570
  168.4 2.7 %copy.20 = f32[1200,300]{0,1:T(8,128)} copy(f32[1200,300]{1,0:T(8,128)} %get-tuple-element.49) | data formatting | bytes 2880000
  (101 shorter events, 35.0 us)
Async XLA Ops:
  6.1 23.1 %copy-start.2 = (bf16[1200,300]{0,1:T(8,128)(2,1)S(1)}, bf16[1200,300]{0,1:T(8,128)(2,1)}, u32[]{:S(2)}) copy-start(bf16[1200,300]{0,1:T(8,128)(2,1)} %param.14) | copy-start | bytes 2160004
  10.4 17.3 %copy-start.11 = (bf16[3,8,384]{2,1,0:T(8,128)(2,1)S(1)}, bf16[3,8,384]{2,1,0:T(8,128)(2,1)}, u32[]{:S(2)}) copy-start(bf16[3,8,384]{2,1,0:T(8,128)(2,1)} %get-tuple-element.30) | copy-start | bytes 55300
  10.4 0.8 collective-permute-start.1
  11.2 8.5 %copy-start.6 = (bf16[3,8,384]{2,1,0:T(8,128)(2,1)}, bf16[3,8,384]{2,1,0:T(8,128)(2,1)S(1)}, u32[]{:S(2)}) copy-start(bf16[3,8,384]{2,1,0:T(8,128)(2,1)S(1)} %collective-permute-done.1.p2_ref.refs_12_) | copy-start | bytes 55300
  12.0 15.8 %collective-permute-start.4 = (bf16[2,3,8,384]{3,2,1,0:T(8,128)(2,1)S(1)}, bf16[2,3,8,384]{3,2,1,0:T(8,128)(2,1)S(1)}, u32[]{:S(2)}, u32[]{:S(2)}) collective-permute-start(bf16[2,3,8,384]{3,2,1,0:T(8,128)(2,1)S(1)} %pad_maximum_fusion.5), channel_id=1, source_target_pairs={{24,26},{25,27},{26,24},{27,25},{28,30},{29,31},{30,28},{31,29}} | collective-permute-start | bytes 110600 | tf_op jit(solution)/shard_map/ppermute | solution.py:396
  12.6 7.1 %collective-permute-start = (bf16[3,8,384]{2,1,0:T(8,128)(2,1)}, bf16[3,8,384]{2,1,0:T(8,128)(2,1)S(1)}, u32[]{:S(2)}, u32[]{:S(2)}) collective-permute-start(bf16[3,8,384]{2,1,0:T(8,128)(2,1)} %get-tuple-element.29), channel_id=1, source_target_pairs={{0,8},{1,9},{2,10},{3,11},{4,12},{5,13},{6,14},{7,15},{8,0},{9,1},... | collective-permute-start | bytes 55304 | tf_op jit(solution)/shard_map/ppermute | solution.py:493
  22.7 16.8 %collective-permute-start.2 = (bf16[3,416,128]{2,1,0:T(8,128)(2,1)}, bf16[3,416,128]{2,1,0:T(8,128)(2,1)S(1)}, u32[]{:S(2)}, u32[]{:S(2)}) collective-permute-start(bf16[3,416,128]{2,1,0:T(8,128)(2,1)} %get-tuple-element.31), channel_id=1, source_target_pairs={{0,1},{1,0},{2,3},{3,2},{4,5},{5,4},{6,7},{7,6},{8,9},{9,8},{10,11... | collective-permute-start | bytes 958472 | tf_op jit(solution)/shard_map/ppermute | solution.py:504
  24.2 15.4 %collective-permute-start.3 = (bf16[3,416,128]{2,1,0:T(8,128)(2,1)}, bf16[3,416,128]{2,1,0:T(8,128)(2,1)S(1)}, u32[]{:S(2)}, u32[]{:S(2)}) collective-permute-start(bf16[3,416,128]{2,1,0:T(8,128)(2,1)} %get-tuple-element.32), channel_id=1, source_target_pairs={{0,7},{1,2},{2,1},{3,4},{4,3},{5,6},{6,5},{7,0},{8,15},{9,10},{10,... | collective-permute-start | bytes 958472 | tf_op jit(solution)/shard_map/ppermute | solution.py:505
  28.5 4.4 %collective-permute-start.5 = (bf16[4,3,8,384]{3,2,1,0:T(8,128)(2,1)S(1)}, bf16[4,3,8,384]{3,2,1,0:T(8,128)(2,1)S(1)}, u32[]{:S(2)}, u32[]{:S(2)}) collective-permute-start(bf16[4,3,8,384]{3,2,1,0:T(8,128)(2,1)S(1)} %pad_maximum_fusion.3), channel_id=1, source_target_pairs={{24,28},{25,29},{26,30},{27,31},{28,24},{29,25},{30,26},{31,27}} | collective-permute-start | bytes 221192 | tf_op jit(solution)/shard_map/ppermute | solution.py:396
  76.1 2.4 %collective-permute-start.12 = (bf16[208,16,128]{2,1,0:T(8,128)(2,1)S(1)}, bf16[208,16,128]{2,1,0:T(8,128)(2,1)S(1)}, u32[]{:S(2)}, u32[]{:S(2)}) collective-permute-start(bf16[208,16,128]{2,1,0:T(8,128)(2,1)S(1)} %dynamic-slice_bitcast_fusion), channel_id=1, source_target_pairs={{0,8},{1,9},{2,10},{3,11},{4,12},{5,13},{6,14},{7,15},{8,0},{9,1},... | collective-permute-start | bytes 2555912 | tf_op jit(solution)/shard_map/ppermute | solution.py:439
  78.9 7.8 %collective-permute-start.13 = (bf16[52,16,128]{2,1,0:T(8,128)(2,1)S(1)}, bf16[52,16,128]{2,1,0:T(8,128)(2,1)S(1)}, u32[]{:S(2)}, u32[]{:S(2)}) collective-permute-start(bf16[52,16,128]{2,1,0:T(8,128)(2,1)S(1)} %get-tuple-element.54), channel_id=1, source_target_pairs={{0,1},{1,0},{2,3},{3,2},{4,5},{5,4},{6,7},{7,6},{8,9},{9,8},{10,11... | collective-permute-start | bytes 638984 | tf_op jit(solution)/shard_map/ppermute | solution.py:439
  80.5 12.5 %collective-permute-start.14 = (bf16[52,16,128]{2,1,0:T(8,128)(2,1)S(1)}, bf16[52,16,128]{2,1,0:T(8,128)(2,1)S(1)}, u32[]{:S(2)}, u32[]{:S(2)}) collective-permute-start(bf16[52,16,128]{2,1,0:T(8,128)(2,1)S(1)} %get-tuple-element.56), channel_id=1, source_target_pairs={{0,16},{1,17},{2,18},{3,19},{4,20},{5,21},{6,22},{7,23},{8,24},{9,... | collective-permute-start | bytes 638984 | tf_op jit(solution)/shard_map/ppermute | solution.py:439
  83.9 9.8 %collective-permute-start.15 = (bf16[52,16,128]{2,1,0:T(8,128)(2,1)S(1)}, bf16[52,16,128]{2,1,0:T(8,128)(2,1)S(1)}, u32[]{:S(2)}, u32[]{:S(2)}) collective-permute-start(bf16[52,16,128]{2,1,0:T(8,128)(2,1)S(1)} %get-tuple-element.55), channel_id=1, source_target_pairs={{0,17},{1,16},{2,19},{3,18},{4,21},{5,20},{6,23},{7,22},{8,25},{9,... | collective-permute-start | bytes 638984 | tf_op jit(solution)/shard_map/ppermute | solution.py:439
  93.9 28.9 %copy-start.10 = (bf16[3,8,384]{2,1,0:T(8,128)(2,1)S(1)}, bf16[3,8,384]{2,1,0:T(8,128)(2,1)}, u32[]{:S(2)}) copy-start(bf16[3,8,384]{2,1,0:T(8,128)(2,1)} %get-tuple-element.36) | copy-start | bytes 55300
  93.9 30.2 %copy-start.17 = (bf16[3,8,384]{2,1,0:T(8,128)(2,1)S(1)}, bf16[3,8,384]{2,1,0:T(8,128)(2,1)}, u32[]{:S(2)}) copy-start(bf16[3,8,384]{2,1,0:T(8,128)(2,1)} %get-tuple-element.35) | copy-start | bytes 55300
  93.9 5.7 %collective-permute-start.16 = (bf16[13,16,128]{2,1,0:T(8,128)(2,1)S(1)}, bf16[13,16,128]{2,1,0:T(8,128)(2,1)S(1)}, u32[]{:S(2)}, u32[]{:S(2)}) collective-permute-start(bf16[13,16,128]{2,1,0:T(8,128)(2,1)S(1)} %get-tuple-element.63), channel_id=1, source_target_pairs={{0,4},{1,5},{2,6},{3,7},{4,0},{5,1},{6,2},{7,3},{8,12},{9,13},{10,... | collective-permute-start | bytes 159752 | tf_op jit(solution)/shard_map/ppermute | solution.py:439
  96.6 4.7 %collective-permute-start.17 = (bf16[13,16,128]{2,1,0:T(8,128)(2,1)S(1)}, bf16[13,16,128]{2,1,0:T(8,128)(2,1)S(1)}, u32[]{:S(2)}, u32[]{:S(2)}) collective-permute-start(bf16[13,16,128]{2,1,0:T(8,128)(2,1)S(1)} %get-tuple-element.65), channel_id=1, source_target_pairs={{0,2},{1,3},{2,0},{3,1},{4,6},{5,7},{6,4},{7,5},{8,10},{9,11},{10,... | collective-permute-start | bytes 159752 | tf_op jit(solution)/shard_map/ppermute | solution.py:439
  97.0 5.9 %collective-permute-start.18 = (bf16[13,16,128]{2,1,0:T(8,128)(2,1)S(1)}, bf16[13,16,128]{2,1,0:T(8,128)(2,1)S(1)}, u32[]{:S(2)}, u32[]{:S(2)}) collective-permute-start(bf16[13,16,128]{2,1,0:T(8,128)(2,1)S(1)} %get-tuple-element.64), channel_id=1, source_target_pairs={{0,6},{1,7},{2,4},{3,5},{4,2},{5,3},{6,0},{7,1},{8,14},{9,15},{10,... | collective-permute-start | bytes 159752 | tf_op jit(solution)/shard_map/ppermute | solution.py:439
  103.6 5.4 %collective-permute-start.19 = (bf16[13,16,128]{2,1,0:T(8,128)(2,1)S(1)}, bf16[13,16,128]{2,1,0:T(8,128)(2,1)S(1)}, u32[]{:S(2)}, u32[]{:S(2)}) collective-permute-start(bf16[13,16,128]{2,1,0:T(8,128)(2,1)S(1)} %get-tuple-element.53), channel_id=1, source_target_pairs={{0,4},{1,5},{2,6},{3,7},{4,0},{5,1},{6,2},{7,3},{8,12},{9,13},{10,... | collective-permute-start | bytes 159752 | tf_op jit(solution)/shard_map/ppermute | solution.py:447
  103.6 5.4 %collective-permute-start.20 = (bf16[13,16,128]{2,1,0:T(8,128)(2,1)S(1)}, bf16[13,16,128]{2,1,0:T(8,128)(2,1)S(1)}, u32[]{:S(2)}, u32[]{:S(2)}) collective-permute-start(bf16[13,16,128]{2,1,0:T(8,128)(2,1)S(1)} %get-tuple-element.53), channel_id=1, source_target_pairs={{0,2},{1,3},{2,0},{3,1},{4,6},{5,7},{6,4},{7,5},{8,10},{9,11},{10,... | collective-permute-start | bytes 159752 | tf_op jit(solution)/shard_map/ppermute | solution.py:447
  105.5 5.9 %collective-permute-start.21 = (bf16[13,16,128]{2,1,0:T(8,128)(2,1)S(1)}, bf16[13,16,128]{2,1,0:T(8,128)(2,1)S(1)}, u32[]{:S(2)}, u32[]{:S(2)}) collective-permute-start(bf16[13,16,128]{2,1,0:T(8,128)(2,1)S(1)} %get-tuple-element.53), channel_id=1, source_target_pairs={{0,6},{1,7},{2,4},{3,5},{4,2},{5,3},{6,0},{7,1},{8,14},{9,15},{10,... | collective-permute-start | bytes 159752 | tf_op jit(solution)/shard_map/ppermute | solution.py:447
  111.5 6.4 %collective-permute-start.22 = (bf16[52,16,128]{2,1,0:T(8,128)(2,1)S(1)}, bf16[52,16,128]{2,1,0:T(8,128)(2,1)S(1)}, u32[]{:S(2)}, u32[]{:S(2)}) collective-permute-start(bf16[52,16,128]{2,1,0:T(8,128)(2,1)S(1)} %pad_maximum_fusion), channel_id=1, source_target_pairs={{0,1},{1,0},{2,3},{3,2},{4,5},{5,4},{6,7},{7,6},{8,9},{9,8},{10,11... | collective-permute-start | bytes 638984 | tf_op jit(solution)/shard_map/ppermute | solution.py:447
  113.0 8.3 %collective-permute-start.23 = (bf16[52,16,128]{2,1,0:T(8,128)(2,1)S(1)}, bf16[52,16,128]{2,1,0:T(8,128)(2,1)S(1)}, u32[]{:S(2)}, u32[]{:S(2)}) collective-permute-start(bf16[52,16,128]{2,1,0:T(8,128)(2,1)S(1)} %pad_maximum_fusion), channel_id=1, source_target_pairs={{0,16},{1,17},{2,18},{3,19},{4,20},{5,21},{6,22},{7,23},{8,24},{9,... | collective-permute-start | bytes 638984 | tf_op jit(solution)/shard_map/ppermute | solution.py:447
  113.8 8.2 %collective-permute-start.24 = (bf16[52,16,128]{2,1,0:T(8,128)(2,1)S(1)}, bf16[52,16,128]{2,1,0:T(8,128)(2,1)S(1)}, u32[]{:S(2)}, u32[]{:S(2)}) collective-permute-start(bf16[52,16,128]{2,1,0:T(8,128)(2,1)S(1)} %pad_maximum_fusion), channel_id=1, source_target_pairs={{0,17},{1,16},{2,19},{3,18},{4,21},{5,20},{6,23},{7,22},{8,25},{9,... | collective-permute-start | bytes 638984 | tf_op jit(solution)/shard_map/ppermute | solution.py:447
  118.7 20.1 %copy-start.1 = (bf16[128,8,300]{2,1,0:T(8,128)(2,1)S(1)}, bf16[128,8,300]{2,1,0:T(8,128)(2,1)}, u32[]{:S(2)}) copy-start(bf16[128,8,300]{2,1,0:T(8,128)(2,1)} %get-tuple-element.46) | copy-start | bytes 1843204
  122.8 40.4 %collective-permute-start.25 = (bf16[208,16,128]{2,1,0:T(8,128)(2,1)}, bf16[208,16,128]{2,1,0:T(8,128)(2,1)S(1)}, u32[]{:S(2)}, u32[]{:S(2)}) collective-permute-start(bf16[208,16,128]{2,1,0:T(8,128)(2,1)} %get-tuple-element.57), channel_id=1, source_target_pairs={{0,8},{1,9},{2,10},{3,11},{4,12},{5,13},{6,14},{7,15},{8,0},{9,1},... | collective-permute-start | bytes 2555912 | tf_op jit(solution)/shard_map/ppermute | solution.py:447
  122.8 0.7 collective-permute-start.7
  123.5 13.3 %collective-permute-start.10 = (bf16[2,3,8,384]{3,2,1,0:T(8,128)(2,1)S(1)}, bf16[2,3,8,384]{3,2,1,0:T(8,128)(2,1)S(1)}, u32[]{:S(2)}, u32[]{:S(2)}) collective-permute-start(bf16[2,3,8,384]{3,2,1,0:T(8,128)(2,1)S(1)} %pad_maximum_fusion.6), channel_id=1, source_target_pairs={{24,26},{25,27},{26,24},{27,25},{28,30},{29,31},{30,28},{31,29}} | collective-permute-start | bytes 110600 | tf_op jit(solution)/shard_map/ppermute | solution.py:396
  124.2 5.8 %collective-permute-start.6 = (bf16[3,8,384]{2,1,0:T(8,128)(2,1)S(1)}, bf16[3,8,384]{2,1,0:T(8,128)(2,1)S(1)}, u32[]{:S(2)}, u32[]{:S(2)}) collective-permute-start(bf16[3,8,384]{2,1,0:T(8,128)(2,1)S(1)} %copy-done.17), channel_id=1, source_target_pairs={{0,8},{1,9},{2,10},{3,11},{4,12},{5,13},{6,14},{7,15},{8,0},{9,1},... | collective-permute-start | bytes 55304 | tf_op jit(solution)/shard_map/ppermute | solution.py:493
  133.0 16.9 %collective-permute-start.8 = (bf16[3,416,128]{2,1,0:T(8,128)(2,1)}, bf16[3,416,128]{2,1,0:T(8,128)(2,1)}, u32[]{:S(2)}, u32[]{:S(2)}) collective-permute-start(bf16[3,416,128]{2,1,0:T(8,128)(2,1)} %get-tuple-element.37), channel_id=1, source_target_pairs={{0,1},{1,0},{2,3},{3,2},{4,5},{5,4},{6,7},{7,6},{8,9},{9,8},{10,11... | collective-permute-start | bytes 958472 | tf_op jit(solution)/shard_map/ppermute | solution.py:504
  133.0 16.9 %collective-permute-start.9 = (bf16[3,416,128]{2,1,0:T(8,128)(2,1)}, bf16[3,416,128]{2,1,0:T(8,128)(2,1)}, u32[]{:S(2)}, u32[]{:S(2)}) collective-permute-start(bf16[3,416,128]{2,1,0:T(8,128)(2,1)} %get-tuple-element.38), channel_id=1, source_target_pairs={{0,7},{1,2},{2,1},{3,4},{4,3},{5,6},{6,5},{7,0},{8,15},{9,10},{10,... | collective-permute-start | bytes 958472 | tf_op jit(solution)/shard_map/ppermute | solution.py:505
  137.5 2.8 %collective-permute-start.11 = (bf16[4,3,8,384]{3,2,1,0:T(8,128)(2,1)S(1)}, bf16[4,3,8,384]{3,2,1,0:T(8,128)(2,1)}, u32[]{:S(2)}, u32[]{:S(2)}) collective-permute-start(bf16[4,3,8,384]{3,2,1,0:T(8,128)(2,1)S(1)} %pad_maximum_fusion.4), channel_id=1, source_target_pairs={{24,28},{25,29},{26,30},{27,31},{28,24},{29,25},{30,26},{31,27}} | collective-permute-start | bytes 221192 | tf_op jit(solution)/shard_map/ppermute | solution.py:396
  (12 other events, 27.1 us)

commit v2 on v1

v2 whole, which is shorter than its diff:
```python
import jax
import jax.numpy as jnp
import numpy as np
from jax import lax
from jax.experimental import pallas as pl
from jax.experimental.pallas import tpu as pltpu
from jax.sharding import PartitionSpec as P

F32 = jnp.float32
BF16 = jnp.bfloat16
AXES = ("lat", "lon")
SUB = 8
COLS = 8
QC = COLS + 6
LT = 3
CP = LT * 128
HB = 256
VM = pl.BlockSpec(memory_space=pltpu.VMEM)
SM = pl.BlockSpec(memory_space=pltpu.SMEM)

EVEN_LON, EVEN_LAT, IS_TOP, LON, START, ME = range(6)


def cost(us):
    return pl.CostEstimate(flops=int(us * 1e6), bytes_accessed=int(us * 2e6), transcendentals=0)


def params(mib=60):
    return pltpu.CompilerParams(vmem_limit_bytes=mib * 1024 * 1024)


def lanes(l, width):
    return min(128, width - 128 * l)


def tap_rows(k_ref, ks, width):
    ks[...] = jnp.zeros_like(ks)
    for l in range(LT):
        w = lanes(l, width)
        ks[l, : k_ref.shape[0], :w] = k_ref[:, 128 * l : 128 * l + w]


def to_cells(src, l, i, put):
    x = src[pl.ds(l * 1024 + i, 128, stride=8), :].T
    for s in range(SUB):
        for t in (0, 8):
            put(pl.ds(t * 64 + i * 8 + s, 8, stride=64), x[16 * s + t : 16 * s + t + 8])


def to_channels(src, dst):
    for l in range(LT):
        for i in range(COLS):
            parts = [src[l, pl.ds(t * 64 + i * 8 + s, 8, stride=64), :] for s in range(SUB) for t in (0, 8)]
            dst[pl.ds(l * 1024 + i, 128, stride=8), :] = jnp.concatenate(parts, axis=0).T


def row_messages(sc, x_ref, rows, p1_ref, p2_ref):
    tt = x_ref.shape[1] // 64
    for l in range(LT):
        for r in range(3):
            rows[r, :, 128 * l : 128 * (l + 1)] = x_ref[l, pl.ds(r * 64, 8, stride=8), :]
            rows[3 + r, :, 128 * l : 128 * (l + 1)] = x_ref[l, pl.ds((tt - 3 + r) * 64 + 7, 8, stride=8), :]
    even = sc[EVEN_LAT]
    p1_ref[...] = rows[pl.ds(3 * even, 3)].astype(BF16)
    p2_ref[...] = rows[pl.ds(3 - 3 * even, 3)].astype(BF16)


def strip_messages(sc, x_ref, q1_ref, q2_ref):
    tt = x_ref.shape[1] // 64
    even = sc[EVEN_LON]
    for q_ref, first in ((q1_ref, 5 * even), (q2_ref, 5 - 5 * even)):
        for l in range(LT):
            for c in range(3):
                for t in range(0, tt, 2):
                    a = x_ref[l, pl.ds(pl.multiple_of(t * 64 + (first + c) * 8, 8), 8), :]
                    b = x_ref[l, pl.ds(pl.multiple_of(t * 64 + 64 + (first + c) * 8, 8), 8), :]
                    q_ref[l, (c * tt + t) * 8 : (c * tt + t) * 8 + 16, :] = jnp.concatenate([a, b], 0).astype(BF16)


def prepare_kernel(sc, mask_ref, f_ref, c_ref, mf_ref, bk_ref, q1_ref, q2_ref, p1_ref, p2_ref, cm, rows, ct):
    width = f_ref.shape[0]
    m = mask_ref[...].astype(F32)[None]
    cm[width * 8 :, :] = jnp.zeros((cm.shape[0] - width * 8, 128), F32)
    for src, dst in ((f_ref, mf_ref), (c_ref, ct)):
        cm[: width * 8, :] = (src[...].astype(F32) * m).reshape(width * 8, 128)
        for l in range(LT):
            for i in range(COLS):

                def put(at, v, l=l, dst=dst):
                    dst[l, at, :] = v

                to_cells(cm, l, i, put)
    strip_messages(sc, mf_ref, q1_ref, q2_ref)
    row_messages(sc, mf_ref, rows, p1_ref, p2_ref)
    for l in range(LT):
        bk_ref[:, 128 * l : 128 * (l + 1)] = ct[l].astype(BF16)


def extend(sc, ext, x_ref, q1_ref, q2_ref, p1_ref, p2_ref, c1_ref, c2_ref):
    tt = x_ref.shape[1] // 64
    even_lat, even_lon, top = sc[EVEN_LAT], sc[EVEN_LON], sc[IS_TOP]
    for l in range(LT):
        for t in range(tt):
            ext[l, ((t + 3) * QC + 3) * 8 : ((t + 3) * QC + 3) * 8 + 64, :] = x_ref[l, t * 64 : t * 64 + 64, :]
    sides = ((q1_ref, c1_ref, even_lon), (q2_ref, c2_ref, 1 - even_lon))
    for q_ref, _, right in sides:
        for l in range(LT):
            for c in range(3):
                for t in range(0, tt, 2):
                    v = q_ref[l, (c * tt + t) * 8 : (c * tt + t) * 8 + 16, :].astype(F32)
                    for u in range(2):
                        at = ((t + u + 3) * QC + 11 * right + c) * 8
                        ext[l, pl.ds(pl.multiple_of(at, 8), 8), :] = v[8 * u : 8 * u + 8]
    for l in range(LT):
        for r in range(3):
            for q in range(QC):
                lo = ext[l, ((tt + r) * QC + q) * 8 : ((tt + r) * QC + q) * 8 + 8, :]
                ext[l, (r * QC + q) * 8 : (r * QC + q) * 8 + 8, :] = pltpu.roll(lo, 1, 0)
                hi = ext[l, ((3 + r) * QC + q) * 8 : ((3 + r) * QC + q) * 8 + 8, :]
                at = ((tt + 3 + r) * QC + q) * 8
                ext[l, at : at + 8, :] = pltpu.roll(hi, 7, 0)
    keep = (1 - top).astype(F32)
    p1, p2 = p1_ref[...].astype(F32), p2_ref[...].astype(F32)
    lower = jnp.where(even_lat == 1, p2, p1)
    upper = jnp.where(even_lat == 1, p1, p2) * keep
    for l in range(LT):
        for r in range(3):
            ext[l, pl.ds((r * QC + 3) * 8, 8, stride=8), :] = lower[r, :, 128 * l : 128 * (l + 1)]
            ext[l, pl.ds(((tt + 3 + r) * QC + 3) * 8 + 7, 8, stride=8), :] = upper[r, :, 128 * l : 128 * (l + 1)]
    for _, c_ref, right in sides:
        first = 11 * right
        for r in range(3):
            lo = c_ref[even_lat, r].astype(F32)
            up = c_ref[1 - even_lat, r].astype(F32) * keep
            for c in range(3):
                lo_row = jnp.where(right == 1, lo[c : c + 1], lo[5 + c : 6 + c])
                up_row = jnp.where(right == 1, up[c : c + 1], up[5 + c : 6 + c])
                for l in range(LT):
                    ext[l, pl.ds((r * QC + first + c) * 8, 1), :] = lo_row[:, 128 * l : 128 * (l + 1)]
                    at = ((tt + 3 + r) * QC + first + c) * 8 + 7
                    ext[l, pl.ds(at, 1), :] = up_row[:, 128 * l : 128 * (l + 1)]


def fold_rows(sc, mir, fold_refs, buf, dst, base):
    first = 0
    for ref in fold_refs:
        for u in range(ref.shape[0]):
            for r in range(3):
                at = ((first + u) * 3 + r) * 8
                v = ref[u, r].astype(F32)
                for l in range(LT):
                    buf[l, at : at + 8, :] = v[:, 128 * l : 128 * (l + 1)]
        first += ref.shape[0]
    total = mir.shape[0]
    for q in range(QC):
        col = sc[START] - 3 + q
        col = jnp.where(col < 0, col + total, col)
        col = jnp.where(col >= total, col - total, col)
        m = mir[col]
        unit = lax.shift_right_logical(m, 3) - sc[LON] + 1 + sc[EVEN_LON]
        unit = jnp.where(unit < 0, unit + first, unit)
        unit = jnp.where(unit >= first, unit - first, unit)
        at = unit * 24 + lax.bitwise_and(m, 7)
        for k in range(3):
            for l in range(LT):
                dst[l, pl.ds(base + (k * QC + q) * 8 + 7, 1), :] = buf[l, pl.ds(at + (2 - k) * 8, 1), :]


def correlate(ext, ks, tt, flip, store):
    for l in range(LT):

        def column(i, carry, l=l):
            acc = [None] * tt
            for b in range(7):
                k = []
                for a in range(7):
                    tap = 7 * a + b
                    tap = 48 - tap if flip else tap
                    k.append(jnp.broadcast_to(ks[l, tap : tap + 1, :], (8, 128)))
                for u in range(tt + 6):
                    e = ext[l, pl.ds(pl.multiple_of((u * QC + i + b) * 8, 8), 8), :]
                    for a in range(7):
                        t = u - a
                        if 0 <= t < tt:
                            v = k[a] * e
                            acc[t] = v if acc[t] is None else acc[t] + v
            for t in range(tt):
                store(l, t, i, acc[t])
            return carry

        lax.fori_loop(0, COLS, column, 0)


DWR = 304
DKR = 64


def block_kernel(width, nf, sc, mir, k_ref, gain_ref, win_ref, wout_ref, mask_ref, f_ref, mf_ref, bk_ref, *refs):
    halos, folds = refs[:6], refs[6 : 6 + nf]
    out_ref, ext, gc_ref, q1_ref, q2_ref, g1_ref, g2_ref, dw_ref, dgain_ref = refs[6 + nf : 15 + nf]
    ks, buf, conv, normed, act, gp, res, rows, cm = refs[15 + nf :]
    cells = mf_ref.shape[1]
    tt = cells // 64
    hidden = win_ref.shape[1]
    extend(sc, ext, mf_ref, *halos)

    @pl.when(sc[IS_TOP] == 1)
    def _():
        fold_rows(sc, mir, folds, buf, ext, (tt + 3) * QC * 8)

    tap_rows(k_ref, ks, width)

    def put(l, t, i, v):
        conv[pl.ds(pl.multiple_of(t * 64 + i * 8, 8), 8), 128 * l : 128 * (l + 1)] = v

    correlate(ext, ks, tt, False, put)
    size = 256
    gain = gain_ref[...]
    valid = (lax.broadcasted_iota(jnp.int32, (1, CP), 1) < width).astype(F32)
    dgain_ref[...] = jnp.zeros_like(dgain_ref)
    inv = 1.0 / width
    coeff = 0.7978845608028654
    nt = (((1,), (1,)), ((), ()))

    def chunk(n, carry):
        at = pl.ds(pl.multiple_of(n * size, size), size)
        x = conv[at, :]
        mean = jnp.sum(x, axis=-1, keepdims=True) * inv
        cen = (x - mean) * valid
        var = jnp.sum(cen * cen, axis=-1, keepdims=True) * inv
        rstd = lax.rsqrt(var + 1e-06)
        nhat = cen * rstd
        nb = (nhat * gain).astype(BF16)
        normed[at, :] = nb
        back = bk_ref[at, :]
        for h in range(0, hidden, HB):
            v = jnp.dot(nb, win_ref[:, h : h + HB], preferred_element_type=F32)
            g = jnp.dot(back, wout_ref[:, h : h + HB], preferred_element_type=F32)
            v2 = v * v
            half = 0.5 + 0.5 * jnp.tanh(v * (coeff + (coeff * 0.044715) * v2))
            a = v * half
            slope = half + a * (1.0 - half) * (2.0 * coeff + (2.0 * coeff * 0.134145) * v2)
            act[at, h : h + HB] = a.astype(BF16)
            gp[at, h : h + HB] = (g * slope).astype(BF16)
        mixed = lax.dot_general(act[at, :], wout_ref[...], nt, preferred_element_type=F32)
        gn = lax.dot_general(gp[at, :], win_ref[...], nt, preferred_element_type=F32)
        for l in range(LT):
            res[l, at, :] = mixed[:, 128 * l : 128 * (l + 1)]
        dgain_ref[...] += jnp.broadcast_to(jnp.sum(gn * nhat, axis=0, keepdims=True), dgain_ref.shape)
        s = gn * gain
        m1 = jnp.sum(s, axis=-1, keepdims=True) * inv
        m2 = jnp.sum(s * nhat, axis=-1, keepdims=True) * inv
        gc = (rstd * (s - m1 - nhat * m2) * valid).astype(BF16).astype(F32)
        for l in range(LT):
            gc_ref[l, at, :] = gc[:, 128 * l : 128 * (l + 1)]
        return carry

    lax.fori_loop(0, cells // size, chunk, 0)
    strip_messages(sc, gc_ref, q1_ref, q2_ref)
    row_messages(sc, gc_ref, rows, g1_ref, g2_ref)
    tiles = (hidden // 128) * (DWR // 16)
    for m, (left, right) in enumerate(((normed, gp), (bk_ref, act))):
        for h in range(0, hidden, HB):
            d = lax.dot_general(
                left[...], right[:, h : h + HB], (((0,), (0,)), ((), ())), preferred_element_type=F32
            ).astype(BF16)
            for u in range(HB // 128):
                first = m * tiles + (h // 128 + u) * (DWR // 16)
                for r in range(DWR // 16):
                    dw_ref[first + r] = d[16 * r : 16 * r + 16, 128 * u : 128 * u + 128]
    dw_ref[2 * tiles :] = jnp.zeros((dw_ref.shape[0] - 2 * tiles, 16, 128), BF16)
    to_channels(res, cm)
    mixed = cm[: width * 8, :].reshape(width, 8, 128)
    out_ref[...] = (mask_ref[...].astype(F32)[None] * (f_ref[...].astype(F32) + mixed)).astype(BF16)


def taps_kernel(count, ext, gc_ref, dgain_ref, dw_ref, dk_ref, part, rows, tiles, sem):
    tt = gc_ref.shape[1] // 64
    for l in range(LT):

        def tap_column(b, carry, l=l):
            acc = [[None, None] for _ in range(7)]
            for i in range(COLS):
                g = [gc_ref[l, t * 64 + i * 8 : t * 64 + i * 8 + 8, :] for t in range(tt)]
                for u in range(tt + 6):
                    e = ext[l, pl.ds(pl.multiple_of((u * QC + i + b) * 8, 8), 8), :]
                    for a in range(7):
                        t = u - a
                        if 0 <= t < tt:
                            v = g[t] * e
                            acc[a][u % 2] = v if acc[a][u % 2] is None else acc[a][u % 2] + v
            for a in range(7):
                part[l, pl.ds(pl.multiple_of((7 * a + b) * 8, 8), 8), :] = acc[a][0] + acc[a][1]
            return carry

        lax.fori_loop(0, 7, tap_column, 0)
    rows[...] = jnp.zeros_like(rows)
    for l in range(LT):
        for k in range(49):
            rows[l, k : k + 1, :] = jnp.sum(part[l, 8 * k : 8 * k + 8, :], axis=0, keepdims=True)
        rows[l, 49:50, :] = dgain_ref[0:1, 128 * l : 128 * (l + 1)]
        for r in range(DKR // 16):
            tiles[l * (DKR // 16) + r] = rows[l, 16 * r : 16 * r + 16, :].astype(BF16)
    copy = pltpu.make_async_copy(tiles, dk_ref.at[pl.ds(count, LT * (DKR // 16))], sem)
    copy.start()
    copy.wait()


def field_kernel(width, nf, sc, mir, k_ref, mask_ref, c_ref, gc_ref, *refs):
    halos, folds = refs[:6], refs[6 : 6 + nf]
    out_ref, ks, buf, ext, ghost, dm, cm = refs[6 + nf :]
    cells = gc_ref.shape[1]
    tt = cells // 64
    extend(sc, ext, gc_ref, *halos)
    tap_rows(k_ref, ks, width)

    def put(l, t, i, v):
        dm[l, pl.ds(pl.multiple_of(t * 64 + i * 8, 8), 8), :] = v

    correlate(ext, ks, tt, True, put)

    @pl.when(sc[IS_TOP] == 1)
    def _():
        ghost[...] = jnp.zeros_like(ghost)
        fold_rows(sc, mir, folds, buf, ghost, 0)
        for l in range(LT):

            def column(i, carry, l=l):
                for k in range(3):
                    at = pl.ds(pl.multiple_of((tt - 1 - k) * 64 + i * 8, 8), 8)
                    acc = dm[l, at, :]
                    for r in range(3 - k):
                        for b in range(7):
                            tap = 7 * (4 + k + r) + b
                            e = ghost[l, pl.ds(pl.multiple_of((r * QC + i + b) * 8, 8), 8), :]
                            acc = acc + jnp.broadcast_to(ks[l, tap : tap + 1, :], (8, 128)) * e
                    dm[l, at, :] = acc
                return carry

            lax.fori_loop(0, COLS, column, 0)

    to_channels(dm, cm)
    total = cm[: width * 8, :].reshape(width, 8, 128)
    out_ref[...] = (mask_ref[...].astype(F32)[None] * (c_ref[...].astype(F32) + total)).astype(BF16)


def unpack_kernel(width, hidden, factor, per, sc, x_ref, gin_ref, gout_ref, gk_ref, gg_ref):
    blocks = (hidden + 127) // 128
    blocks += blocks % 2
    tr = DWR // 16

    def tile(n):
        chunk = lax.bitwise_xor(jnp.int32(n // per), sc[ME])
        return x_ref[chunk * per + n % per].astype(F32) * factor

    for cb in range(blocks):
        w = min(128, hidden - 128 * cb)
        if w <= 0:
            continue
        for r in range(tr):
            rows = min(16, width - 16 * r)
            gin_ref[16 * r : 16 * r + rows, 128 * cb : 128 * cb + w] = tile(cb * tr + r)[:rows, :w]
            gout_ref[16 * r : 16 * r + rows, 128 * cb : 128 * cb + w] = tile((blocks + cb) * tr + r)[:rows, :w]
    for l in range(LT):
        w = lanes(l, width)
        base = 2 * blocks * tr + l * (DKR // 16)
        taps = jnp.concatenate([tile(base + r) for r in range(DKR // 16)], axis=0)
        gk_ref[:, 128 * l : 128 * l + w] = taps[:49, :w]
        gg_ref[:, 128 * l : 128 * l + w] = taps[49:50, :w]


def swaps(n_lat, n_lon, bits):
    ml, mo = bits
    return [(l * n_lon + o, (l ^ ml) * n_lon + (o ^ mo)) for l in range(n_lat) for o in range(n_lon)]


def lat_swaps(n_lat, n_lon):
    first = [(l * n_lon + o, (l ^ 1) * n_lon + o) for l in range(n_lat) for o in range(n_lon)]
    second = []
    for l in range(n_lat):
        for o in range(n_lon):
            if l == n_lat - 1:
                second.append((l * n_lon + o, l * n_lon + (o ^ 1)))
            elif l > 0:
                other = l + 1 if l % 2 else l - 1
                second.append((l * n_lon + o, other * n_lon + o))
    return first, second


def lon_swaps(n_lat, n_lon):
    first = [(l * n_lon + o, l * n_lon + (o ^ 1)) for l in range(n_lat) for o in range(n_lon)]
    second = []
    for l in range(n_lat):
        for o in range(n_lon):
            other = (o + 1) % n_lon if o % 2 else (o - 1) % n_lon
            second.append((l * n_lon + o, l * n_lon + other))
    return first, second


def fold_gather(own, pair, c2, even_lon, n_lat, n_lon):
    up = jnp.stack([c2[1], c2[2], own, pair])
    down = jnp.stack([pair, own, c2[2], c2[1]])
    units = [jnp.where(even_lon, up, down)]
    top = n_lat - 1
    step = 4
    while step < n_lon:
        have = jnp.concatenate(units) if len(units) > 1 else units[0]
        pairs = [(top * n_lon + (o + step) % n_lon, top * n_lon + o) for o in range(n_lon)]
        units.append(lax.ppermute(have, AXES, pairs))
        step *= 2
    return units


def stages(n_lat, n_lon):
    out = [[(1, 0)]]
    rest = [(1 << b, 0) for b in range(1, n_lat.bit_length() - 1)] + [(0, 1 << b) for b in range(n_lon.bit_length() - 1)]
    while rest:
        out.append(rest[:2])
        rest = rest[2:]
    return out


def group_index(group, lat, lon):
    value = jnp.int32(0)
    for ml, mo in group:
        bit = (lat & ml) != 0 if ml else (lon & mo) != 0
        value = 2 * value + bit.astype(jnp.int32)
    return value


def group_masks(group):
    masks = []
    for d in range(1 << len(group)):
        ml = mo = 0
        for k, (gl, go) in enumerate(group):
            if d >> (len(group) - 1 - k) & 1:
                ml, mo = ml | gl, mo | go
        masks.append((ml, mo))
    return masks


def all_sum(x, beside, lat, lon, n_lat, n_lon):
    groups = stages(n_lat, n_lon)
    for k, group in enumerate(groups):
        n = 1 << len(group)
        x = x.reshape((n, x.shape[0] // n) + x.shape[1:])
        idx = group_index(group, lat, lon)
        masks = group_masks(group)
        got = []
        for d in range(1, n):
            piece = lax.dynamic_index_in_dim(x, idx ^ d, 0, False)
            got.append(lax.ppermute(piece, AXES, swaps(n_lat, n_lon, masks[d])))
        if k == 1:
            got, beside = lax.optimization_barrier((got, beside))
        total = lax.dynamic_index_in_dim(x, idx, 0, False).astype(F32)
        for g in got:
            total = total + g.astype(F32)
        x = total.astype(BF16)
    for group in reversed(groups):
        masks = group_masks(group)
        x = jnp.concatenate(
            [x] + [lax.ppermute(x, AXES, swaps(n_lat, n_lon, masks[d])) for d in range(1, len(masks))], axis=0
        )
    return x, beside


def body(field_in, sea_mask, mirror, kernel, norm_gain, proj_in, proj_out, cotangent):
    nrows, ncols, width = field_in.shape
    hidden = proj_in.shape[1]
    n_lat, n_lon = lax.axis_size("lat"), lax.axis_size("lon")
    assert ncols == COLS and nrows % 16 == 0 and n_lat % 2 == 0 and n_lon % 2 == 0
    lat, lon = lax.axis_index("lat"), lax.axis_index("lon")
    cells = nrows * ncols
    tt = nrows // SUB
    groups = stages(n_lat, n_lon)
    me = jnp.int32(0)
    for group in groups:
        me = (me << len(group)) + group_index(group, lat, lon)
    sc = jnp.stack(
        [1 - lon % 2, 1 - lat % 2, (lat == n_lat - 1).astype(jnp.int32), lon, lon * ncols, me, jnp.int32(0), jnp.int32(0)]
    ).astype(jnp.int32)
    assert nrows == 128 and n_lon % 4 == 0
    hp = -(-hidden // HB) * HB
    win = jnp.pad(proj_in, ((0, CP - width), (0, hp - hidden)))
    wout = jnp.pad(proj_out.T, ((0, CP - width), (0, hp - hidden)))
    gain = jnp.pad(norm_gain, (0, CP - width)).reshape(1, CP)
    field_c = field_in.transpose(2, 1, 0)
    cot_c = cotangent.transpose(2, 1, 0)
    mask_c = sea_mask.T

    s = jax.ShapeDtypeStruct
    row_msg = s((3, COLS, CP), BF16)
    strip_msg = s((LT, 3 * tt * 8, 128), BF16)
    channels = pltpu.VMEM((CP * 8, 128), F32)
    mf, bk, q1, q2, p1, p2 = pl.pallas_call(
        prepare_kernel,
        out_shape=(s((LT, cells, 128), F32), s((cells, CP), BF16), strip_msg, strip_msg, row_msg, row_msg),
        in_specs=[SM, VM, VM, VM],
        out_specs=(VM,) * 6,
        scratch_shapes=[channels, pltpu.VMEM((6, COLS, CP), F32), pltpu.VMEM((LT, cells, 128), F32)],
        compiler_params=params(9),
        name="prepare",
        cost_estimate=cost(5),
    )(sc, mask_c, field_c, cot_c)

    lat1, lat2 = lat_swaps(n_lat, n_lon)
    lon1, lon2 = lon_swaps(n_lat, n_lon)

    def halo(q1, q2, p1, p2):
        s1 = lax.ppermute(q1, AXES, lon1)
        s2 = lax.ppermute(q2, AXES, lon2)
        r1 = lax.ppermute(p1, AXES, lat1)
        r2 = lax.ppermute(p2, AXES, lat2)
        rows = jnp.stack([r1, r2, p2])
        c1 = lax.ppermute(rows, AXES, lon1)
        c2 = lax.ppermute(rows, AXES, lon2)
        folds = fold_gather(p2, r2, c2, lon % 2 == 0, n_lat, n_lon)
        return [s1, s2, r1, r2, c1, c2] + folds, rows

    halos, _ = halo(q1, q2, p1, p2)
    nf = len(halos) - 6
    count = 2 * (hp // 128) * (DWR // 16)
    devices = n_lat * n_lon
    per = -(-(count + LT * DKR // 16) // devices)
    out, ext, gc, q1, q2, g1, g2, dw, dgain = pl.pallas_call(
        lambda *refs: block_kernel(width, nf, *refs),
        out_shape=(
            s((width, COLS, nrows), BF16),
            s((LT, (tt + 6) * QC * 8, 128), F32),
            s((LT, cells, 128), F32),
            strip_msg,
            strip_msg,
            row_msg,
            row_msg,
            s((per * devices, 16, 128), BF16),
            s((8, CP), F32),
        ),
        in_specs=[SM, SM] + [VM] * (len(halos) + 8),
        out_specs=(VM,) * 9,
        scratch_shapes=[
            pltpu.VMEM((LT, 56, 128), F32),
            pltpu.VMEM((LT, n_lon * 24, 128), F32),
            pltpu.VMEM((cells, CP), F32),
            pltpu.VMEM((cells, CP), BF16),
            pltpu.VMEM((cells, hp), BF16),
            pltpu.VMEM((cells, hp), BF16),
            pltpu.VMEM((LT, cells, 128), F32),
            pltpu.VMEM((6, COLS, CP), F32),
            channels,
        ],
        compiler_params=params(20),
        name="block",
        cost_estimate=cost(20),
    )(sc, mirror, kernel, gain, win, wout, mask_c, field_c, mf, bk, *halos)

    ghalos, rows = halo(q1, q2, g1, g2)
    gc_late, _ = lax.optimization_barrier((gc, rows))
    packed = pl.pallas_call(
        lambda *refs: taps_kernel(count, *refs),
        out_shape=s((per * devices, 16, 128), BF16),
        in_specs=[VM] * 3 + [pl.BlockSpec(memory_space=pl.ANY)],
        out_specs=pl.BlockSpec(memory_space=pl.ANY),
        scratch_shapes=[
            pltpu.VMEM((LT, 49 * 8, 128), F32),
            pltpu.VMEM((LT, DKR, 128), F32),
            pltpu.VMEM((LT * DKR // 16, 16, 128), BF16),
            pltpu.SemaphoreType.DMA,
        ],
        input_output_aliases={3: 0},
        compiler_params=params(6),
        name="taps",
        cost_estimate=cost(9),
    )(ext, gc_late, dgain, dw)
    grad_field = pl.pallas_call(
        lambda *refs: field_kernel(width, nf, *refs),
        out_shape=s((width, COLS, nrows), BF16),
        in_specs=[SM, SM] + [VM] * (len(ghalos) + 4),
        out_specs=VM,
        scratch_shapes=[
            pltpu.VMEM((LT, 56, 128), F32),
            pltpu.VMEM((LT, n_lon * 24, 128), F32),
            pltpu.VMEM((LT, (tt + 6) * QC * 8, 128), F32),
            pltpu.VMEM((LT, 3 * QC * 8, 128), F32),
            pltpu.VMEM((LT, cells, 128), F32),
            channels,
        ],
        compiler_params=params(12),
        name="field",
        cost_estimate=cost(11),
    )(sc, mirror, kernel, mask_c, cot_c, gc, *ghalos)

    packed, _ = lax.optimization_barrier((packed, ghalos))
    summed, grad_field = all_sum(packed, grad_field, lat, lon, n_lat, n_lon)
    factor = float(1.0 / np.sqrt(np.float32(nrows * n_lat * ncols * n_lon)))
    gin, gout, gk, gg = pl.pallas_call(
        lambda *refs: unpack_kernel(width, hidden, factor, per, *refs),
        out_shape=(s((width, hidden), F32), s((width, hidden), F32), s((49, width), F32), s((1, width), F32)),
        in_specs=[SM, VM],
        out_specs=(VM,) * 4,
        compiler_params=params(8),
        name="unpack",
        cost_estimate=cost(4),
    )(sc, summed)
    return out.transpose(2, 1, 0), grad_field.transpose(2, 1, 0), gin, gout.T, gk, gg.reshape(width)


def solution(mesh):
    in_specs = (
        P("lat", "lon", None),
        P("lat", "lon"),
        P(),
        P(),
        P(),
        P(),
        P(),
        P("lat", "lon", None),
    )
    out_specs = (P("lat", "lon", None), P("lat", "lon", None), P(), P(), P(), P())
    return jax.shard_map(body, mesh=mesh, in_specs=in_specs, out_specs=out_specs, check_vma=False)
```

time: 172 us -> 141 us (0.82)
  Pallas kernels: 56 us -> 43.5 us
  local copies, waits for them, and re-layouts: 23.8 us -> 15.1 us
  other arithmetic: 9.21 us -> 3.91 us
  waiting for transfers between devices: 39.7 us -> 34.8 us
    ppermute x7, waiting for transfers between devices: 16.8 us -> 5.8 us  [all_sum(): got.append(lax.ppermute(piece, AXES, swaps(n_lat, n_lon, masks[d])))]
    pallas_call x5 -> x3, Pallas kernels: 47.9 us -> 37.7 us  [the longest x1 18.2 us: body(): pl.pallas_call(lambda *refs: block_kernel(width, nf, *refs), out_shape=(s...]
    concatenate x5 -> x0, other arithmetic: 6.84 us -> none  [the longest x4 3.73 us: fold_gather(): buf = jnp.concatenate([buf, lax.ppermute(buf, AXES, pairs)])]
    ppermute x7, waiting for transfers between devices: 7.05 us -> 13.7 us  [all_sum(): lax.ppermute(x, AXES, swaps(n_lat, n_lon, masks[d]))]
    ppermute x12 -> x14, starting transfers between devices: 24.5 us -> 18.5 us  [the longest x2 6.61 us: halo(): c2 = lax.ppermute(rows, AXES, lon2)]
    ppermute x7, starting transfers between devices: 9.51 us -> 15.3 us  [all_sum(): got.append(lax.ppermute(piece, AXES, swaps(n_lat, n_lon, masks[d])))]
    unnamed x49 -> x52, local copies, waits for them, and re-layouts: 19.1 us -> 13.3 us
    convert_element_type x2, other arithmetic: 0.34 us -> 2.55 us  [all_sum(): x = total.astype(BF16)]
  transfers between devices with their start and end apart: 26 -> 28, of which waited for: 15 -> 15; matrix products, arithmetic and copies ran while one was open for 9% -> 0% of each run, Pallas kernels for 9% -> 14%
where the time goes in v2:
time: 141 us; the launch traced here: 140 us
  Pallas kernels  43.5 us (31%)
  starting transfers between devices  41.9 us (30%)
  waiting for transfers between devices  34.8 us (25%)
  local copies, waits for them, and re-layouts  15.1 us (11%)
  other arithmetic  3.91 us (3%)
    pallas_call x1, Pallas kernels, body(): pl.pallas_call(lambda *refs: block_kernel(width, nf, *refs), out_shape=(s...  18.2 us
    ppermute x7, starting transfers between devices, all_sum(): got.append(lax.ppermute(piece, AXES, swaps(n_lat, n_lon, masks[d])))  15.3 us
    ppermute x7, waiting for transfers between devices, all_sum(): lax.ppermute(x, AXES, swaps(n_lat, n_lon, masks[d]))  13.7 us
    unnamed x52, local copies, waits for them, and re-layouts  13.3 us
    ppermute x2, waiting for transfers between devices, halo(): c1 = lax.ppermute(rows, AXES, lon1)  12.4 us
    pallas_call x1, Pallas kernels, body(): pl.pallas_call(lambda *refs: field_kernel(width, nf, *refs), out_shape=s(...  9.92 us
    pallas_call x1, Pallas kernels, body(): pl.pallas_call(lambda *refs: taps_kernel(count, *refs), out_shape=s((per...  9.6 us
    ppermute x7, starting transfers between devices, all_sum(): lax.ppermute(x, AXES, swaps(n_lat, n_lon, masks[d]))  8.08 us
  transfers between devices with their start and end apart: 28, of which 15 were waited for; matrix products, arithmetic and copies ran while one was open for 0% of the time, Pallas kernels for 14%

profile of v2, /device:TPU:0, one launch (start us, length us, event | category | flops | bytes accessed | tf_op | source)
XLA Modules:
  0.0 140.2 jit_solution(1157605897778602757)
XLA Ops:
  3.6 3.3 %prepare.1 = (f32[3,1024,128]{2,1,0:T(8,128)S(1)}, bf16[1024,384]{1,0:T(8,128)(2,1)S(1)}, bf16[3,384,128]{2,1,0:T(8,128)(2,1)S(1)}, bf16[3,384,128]{2,1,0:T(8,12...) custom-call(s32[8]{0:T(128)S(1)} %stack.77.sc.refs_0_, s32[8,128]{1,0:T(8,128)S(1)} %bitcast.62, ...), custom_call_target="tpu_custom_call" | custom-call | flops 5000000 | bytes 10000000 | tf_op jit(solution)/shard_map/prepare/pallas_call | solution.py:495
  10.3 5.9 %collective-permute-start.5 = (bf16[3,3,8,384]{3,2,1,0:T(8,128)(2,1)S(1)}, bf16[3,3,8,384]{3,2,1,0:T(8,128)(2,1)S(1)}, u32[]{:S(2)}, u32[]{:S(2)}) collective-permute-start(bf16[3,3,8,384]{3,2,1,0:T(8,128)(2,1)S(1)} %pad_maximum_fusion.1), channel_id=1, source_target_pairs={{0,7},{1,2},{2,1},{3,4},{4,3},{5,6},{6,5},{7,0},{8,15},{9,10},{10,... | collective-permute-start | bytes 165896 | tf_op jit(solution)/shard_map/ppermute | solution.py:516
  16.3 1.9 %collective-permute-start.1 = (bf16[3,384,128]{2,1,0:T(8,128)(2,1)S(1)}, bf16[3,384,128]{2,1,0:T(8,128)(2,1)S(1)}, u32[]{:S(2)}, u32[]{:S(2)}) collective-permute-start(bf16[3,384,128]{2,1,0:T(8,128)(2,1)S(1)} %get-tuple-element.34), channel_id=1, source_target_pairs={{0,7},{1,2},{2,1},{3,4},{4,3},{5,6},{6,5},{7,0},{8,15},{9,10},{10,... | collective-permute-start | bytes 884744 | tf_op jit(solution)/shard_map/ppermute | solution.py:511
  19.7 12.4 %collective-permute-done.4.refs_14_ = bf16[3,3,8,384]{3,2,1,0:T(8,128)(2,1)S(1)} collective-permute-done((bf16[3,3,8,384]{3,2,1,0:T(8,128)(2,1)S(1)}, bf16[3,3,8,384]{3,2,1,0:T(8,128)(2,1)S(1)}, u32[]{:S(2)}, u32[]{:S(2)}) %collective-permute-start.4) | collective-permute-done | bytes 55328 | tf_op jit(solution)/shard_map/ppermute | solution.py:515
  35.4 18.2 %block.1 = (bf16[300,8,128]{2,1,0:T(8,128)(2,1)}, f32[3,2464,128]{2,1,0:T(8,128)S(1)}, f32[3,1024,128]{2,1,0:T(8,128)S(1)}, bf16[3,384,128]{2,1,0:T(8,128)(2,1)}...) custom-call(s32[8]{0:T(128)S(1)} %stack.77.sc.refs_0_, ...), custom_call_target="tpu_custom_call" | custom-call | flops 20000000 | bytes 40000000 | tf_op jit(solution)/shard_map/block/pallas_call | solution.py:525
  53.7 1.8 %copy-done = f32[3,2464,128]{2,1,0:T(8,128)} copy-done((f32[3,2464,128]{2,1,0:T(8,128)}, f32[3,2464,128]{2,1,0:T(8,128)S(1)}, u32[]{:S(2)}) %copy-start) | copy-done | bytes 3784728
  55.5 2.0 %collective-permute-start.7 = (bf16[3,8,384]{2,1,0:T(8,128)(2,1)S(1)}, bf16[3,8,384]{2,1,0:T(8,128)(2,1)S(1)}, u32[]{:S(2)}, u32[]{:S(2)}) collective-permute-start(bf16[3,8,384]{2,1,0:T(8,128)(2,1)S(1)} %get-tuple-element.40), channel_id=1, source_target_pairs={{0,8},{1,9},{2,10},{3,11},{4,12},{5,13},{6,14},{7,15},{8,0},{9,1},... | collective-permute-start | bytes 55304 | tf_op jit(solution)/shard_map/ppermute | solution.py:512
  59.7 4.0 %collective-permute-start.10 = (bf16[3,384,128]{2,1,0:T(8,128)(2,1)}, bf16[3,384,128]{2,1,0:T(8,128)(2,1)}, u32[]{:S(2)}, u32[]{:S(2)}) collective-permute-start(bf16[3,384,128]{2,1,0:T(8,128)(2,1)} %get-tuple-element.46), channel_id=1, source_target_pairs={{0,7},{1,2},{2,1},{3,4},{4,3},{5,6},{6,5},{7,0},{8,15},{9,10},{10,... | collective-permute-start | bytes 884744 | tf_op jit(solution)/shard_map/ppermute | solution.py:511
  63.7 2.3 %collective-permute-done.12.refs_11_ = bf16[3,3,8,384]{3,2,1,0:T(8,128)(2,1)S(1)} collective-permute-done((bf16[3,3,8,384]{3,2,1,0:T(8,128)(2,1)}, bf16[3,3,8,384]{3,2,1,0:T(8,128)(2,1)S(1)}, u32[]{:S(2)}, u32[]{:S(2)}) %collective-permute-start.12) | collective-permute-done | bytes 55328 | tf_op jit(solution)/shard_map/ppermute | solution.py:516
  66.1 1.3 collective-permute-start.13
  67.4 2.1 %copy-done.1 = f32[3,2464,128]{2,1,0:T(8,128)S(1)} copy-done((f32[3,2464,128]{2,1,0:T(8,128)S(1)}, f32[3,2464,128]{2,1,0:T(8,128)}, u32[]{:S(2)}) %copy-start.1) | copy-done | bytes 3784728
  69.5 9.6 %taps.1 = bf16[416,16,128]{2,1,0:T(8,128)(2,1)S(1)} custom-call(f32[3,2464,128]{2,1,0:T(8,128)S(1)} %copy-done.1, f32[3,1024,128]{2,1,0:T(8,128)S(1)} %get-tuple-element.42.refs_1_.refs_5_, f32[8,384]{1,0:T(8,128)S(1)} %get-tuple-element.43.refs_2_, bf16[416,16,128]{2,1,0:T(8,128)(2,1)S(1)} %get-tuple-element.44.refs_3_), custom_call_target="tpu_custom_call", output_to_operand_aliasing={{}: (3, {})} | custom-call | flops 9000000 | bytes 18000000 | tf_op jit(solution)/shard_map/taps/pallas_call | solution.py:558
  80.2 5.7 %collective-permute-start.14 = (bf16[208,16,128]{2,1,0:T(8,128)(2,1)}, bf16[208,16,128]{2,1,0:T(8,128)(2,1)}, u32[]{:S(2)}, u32[]{:S(2)}) collective-permute-start(bf16[208,16,128]{2,1,0:T(8,128)(2,1)} %dynamic-slice_bitcast_fusion), channel_id=1, source_target_pairs={{0,8},{1,9},{2,10},{3,11},{4,12},{5,13},{6,14},{7,15},{8,0},{9,1},... | collective-permute-start | bytes 2555912 | tf_op jit(solution)/shard_map/ppermute | solution.py:452
  85.9 2.3 %collective-permute-done.14 = bf16[208,16,128]{2,1,0:T(8,128)(2,1)} collective-permute-done((bf16[208,16,128]{2,1,0:T(8,128)(2,1)}, bf16[208,16,128]{2,1,0:T(8,128)(2,1)}, u32[]{:S(2)}, u32[]{:S(2)}) %collective-permute-start.14) | collective-permute-done | bytes 852000 | tf_op jit(solution)/shard_map/ppermute | solution.py:452
  88.3 1.4 fusion
  90.7 1.8 %collective-permute-start.15 = (bf16[52,16,128]{2,1,0:T(8,128)(2,1)S(1)}, bf16[52,16,128]{2,1,0:T(8,128)(2,1)S(1)}, u32[]{:S(2)}, u32[]{:S(2)}) collective-permute-start(bf16[52,16,128]{2,1,0:T(8,128)(2,1)S(1)} %get-tuple-element.60), channel_id=1, source_target_pairs={{0,1},{1,0},{2,3},{3,2},{4,5},{5,4},{6,7},{7,6},{8,9},{9,8},{10,11... | collective-permute-start | bytes 638984 | tf_op jit(solution)/shard_map/ppermute | solution.py:452
  92.5 3.3 %collective-permute-start.16 = (bf16[52,16,128]{2,1,0:T(8,128)(2,1)S(1)}, bf16[52,16,128]{2,1,0:T(8,128)(2,1)S(1)}, u32[]{:S(2)}, u32[]{:S(2)}) collective-permute-start(bf16[52,16,128]{2,1,0:T(8,128)(2,1)S(1)} %get-tuple-element.59), channel_id=1, source_target_pairs={{0,16},{1,17},{2,18},{3,19},{4,20},{5,21},{6,22},{7,23},{8,24},{9,... | collective-permute-start | bytes 638984 | tf_op jit(solution)/shard_map/ppermute | solution.py:452
  95.8 9.9 %field.1 = bf16[300,8,128]{2,1,0:T(8,128)(2,1)} custom-call(s32[8]{0:T(128)S(1)} %stack.77.sc.refs_0_, s32[64]{0:T(128)S(1)} %copy-done.18, f32[49,300]{1,0:T(8,128)S(1)} %copy-done.10, s32[8,128]{1,0:T(8,128)S(1)} %bitcast.64, bf16[300,8,128]{2,1,0:T(8,128)(2,1)S(1)} %bitcast.49, f32[3,1024,128]{2,1,0:T(8,128)S(1)} %get-tuple-element.42.refs_1_.refs_5_, ...), custom_call_target="tpu_custom_call" | custom-call | flops 11000000 | bytes 22000000 | tf_op jit(solution)/shard_map/field/pallas_call | solution.py:574
  107.0 1.7 %collective-permute-start.18 = (bf16[13,16,128]{2,1,0:T(8,128)(2,1)S(1)}, bf16[13,16,128]{2,1,0:T(8,128)(2,1)S(1)}, u32[]{:S(2)}, u32[]{:S(2)}) collective-permute-start(bf16[13,16,128]{2,1,0:T(8,128)(2,1)S(1)} %get-tuple-element.67), channel_id=1, source_target_pairs={{0,4},{1,5},{2,6},{3,7},{4,0},{5,1},{6,2},{7,3},{8,12},{9,13},{10,... | collective-permute-start | bytes 159752 | tf_op jit(solution)/shard_map/ppermute | solution.py:452
  108.8 2.6 %collective-permute-start.20 = (bf16[13,16,128]{2,1,0:T(8,128)(2,1)S(1)}, bf16[13,16,128]{2,1,0:T(8,128)(2,1)S(1)}, u32[]{:S(2)}, u32[]{:S(2)}) collective-permute-start(bf16[13,16,128]{2,1,0:T(8,128)(2,1)S(1)} %get-tuple-element.68), channel_id=1, source_target_pairs={{0,6},{1,7},{2,4},{3,5},{4,2},{5,3},{6,0},{7,1},{8,14},{9,15},{10,... | collective-permute-start | bytes 159752 | tf_op jit(solution)/shard_map/ppermute | solution.py:452
  111.4 2.1 %collective-permute-done.18 = bf16[13,16,128]{2,1,0:T(8,128)(2,1)S(1)} collective-permute-done((bf16[13,16,128]{2,1,0:T(8,128)(2,1)S(1)}, bf16[13,16,128]{2,1,0:T(8,128)(2,1)S(1)}, u32[]{:S(2)}, u32[]{:S(2)}) %collective-permute-start.18) | collective-permute-done | bytes 53280 | tf_op jit(solution)/shard_map/ppermute | solution.py:452
  113.6 1.3 collective-permute-done.20
  115.4 2.6 %collective-permute-start.22 = (bf16[13,16,128]{2,1,0:T(8,128)(2,1)S(1)}, bf16[13,16,128]{2,1,0:T(8,128)(2,1)S(1)}, u32[]{:S(2)}, u32[]{:S(2)}) collective-permute-start(bf16[13,16,128]{2,1,0:T(8,128)(2,1)S(1)} %get-tuple-element.57), channel_id=1, source_target_pairs={{0,2},{1,3},{2,0},{3,1},{4,6},{5,7},{6,4},{7,5},{8,10},{9,11},{10,... | collective-permute-start | bytes 159752 | tf_op jit(solution)/shard_map/ppermute | solution.py:462
  118.0 1.3 collective-permute-start.23
  119.4 1.8 %collective-permute-done.21 = bf16[13,16,128]{2,1,0:T(8,128)(2,1)S(1)} collective-permute-done((bf16[13,16,128]{2,1,0:T(8,128)(2,1)S(1)}, bf16[13,16,128]{2,1,0:T(8,128)(2,1)S(1)}, u32[]{:S(2)}, u32[]{:S(2)}) %collective-permute-start.21) | collective-permute-done | bytes 53280 | tf_op jit(solution)/shard_map/ppermute | solution.py:462
  121.2 2.8 %collective-permute-done.23 = bf16[13,16,128]{2,1,0:T(8,128)(2,1)S(1)} collective-permute-done((bf16[13,16,128]{2,1,0:T(8,128)(2,1)S(1)}, bf16[13,16,128]{2,1,0:T(8,128)(2,1)S(1)}, u32[]{:S(2)}, u32[]{:S(2)}) %collective-permute-start.23) | collective-permute-done | bytes 53280 | tf_op jit(solution)/shard_map/ppermute | solution.py:462
  124.0 1.5 %collective-permute-start.24 = (bf16[52,16,128]{2,1,0:T(8,128)(2,1)S(1)}, bf16[52,16,128]{2,1,0:T(8,128)(2,1)S(1)}, u32[]{:S(2)}, u32[]{:S(2)}) collective-permute-start(bf16[52,16,128]{2,1,0:T(8,128)(2,1)S(1)} %pad_maximum_fusion), channel_id=1, source_target_pairs={{0,1},{1,0},{2,3},{3,2},{4,5},{5,4},{6,7},{7,6},{8,9},{9,8},{10,11... | collective-permute-start | bytes 638984 | tf_op jit(solution)/shard_map/ppermute | solution.py:462
  125.5 2.0 %collective-permute-start.25 = (bf16[52,16,128]{2,1,0:T(8,128)(2,1)S(1)}, bf16[52,16,128]{2,1,0:T(8,128)(2,1)S(1)}, u32[]{:S(2)}, u32[]{:S(2)}) collective-permute-start(bf16[52,16,128]{2,1,0:T(8,128)(2,1)S(1)} %pad_maximum_fusion), channel_id=1, source_target_pairs={{0,16},{1,17},{2,18},{3,19},{4,20},{5,21},{6,22},{7,23},{8,24},{9,... | collective-permute-start | bytes 638984 | tf_op jit(solution)/shard_map/ppermute | solution.py:462
  127.6 3.5 %collective-permute-done.24 = bf16[52,16,128]{2,1,0:T(8,128)(2,1)S(1)} collective-permute-done((bf16[52,16,128]{2,1,0:T(8,128)(2,1)S(1)}, bf16[52,16,128]{2,1,0:T(8,128)(2,1)S(1)}, u32[]{:S(2)}, u32[]{:S(2)}) %collective-permute-start.24) | collective-permute-done | bytes 213024 | tf_op jit(solution)/shard_map/ppermute | solution.py:462
  131.2 2.5 %collective-permute-done.25 = bf16[52,16,128]{2,1,0:T(8,128)(2,1)S(1)} collective-permute-done((bf16[52,16,128]{2,1,0:T(8,128)(2,1)S(1)}, bf16[52,16,128]{2,1,0:T(8,128)(2,1)S(1)}, u32[]{:S(2)}, u32[]{:S(2)}) %collective-permute-start.25) | collective-permute-done | bytes 213024 | tf_op jit(solution)/shard_map/ppermute | solution.py:462
  134.7 2.4 %collective-permute-done.27 = bf16[208,16,128]{2,1,0:T(8,128)(2,1)S(1)} collective-permute-done((bf16[208,16,128]{2,1,0:T(8,128)(2,1)S(1)}, bf16[208,16,128]{2,1,0:T(8,128)(2,1)S(1)}, u32[]{:S(2)}, u32[]{:S(2)}) %collective-permute-start.27) | collective-permute-done | bytes 852000 | tf_op jit(solution)/shard_map/ppermute | solution.py:462
  137.2 2.4 %unpack.1 = (f32[300,1200]{1,0:T(8,128)}, f32[300,1200]{1,0:T(8,128)}, f32[49,300]{1,0:T(8,128)}, f32[1,300]{1,0:T(1,128)S(1)}) custom-call(s32[8]{0:T(128)S(1)} %stack.77.sc.refs_0_, bf16[416,16,128]{2,1,0:T(8,128)(2,1)S(1)} %constant_dynamic-update-slice_fusion.7.refs_1_), custom_call_target="tpu_custom_call" | custom-call | flops 4000000 | bytes 8000000 | tf_op jit(solution)/shard_map/unpack/pallas_call | solution.py:595
  (105 shorter events, 19.2 us)
Async XLA Ops:
  3.6 15.8 %copy-start.20 = (bf16[300,1200]{1,0:T(8,128)(2,1)S(1)}, bf16[300,1200]{1,0:T(8,128)(2,1)}, u32[]{:S(2)}) copy-start(bf16[300,1200]{1,0:T(8,128)(2,1)} %param.13) | copy-start | bytes 2160004
  3.6 15.9 %copy-start.21 = (bf16[1200,300]{0,1:T(8,128)(2,1)S(1)}, bf16[1200,300]{0,1:T(8,128)(2,1)}, u32[]{:S(2)}) copy-start(bf16[1200,300]{0,1:T(8,128)(2,1)} %param.14) | copy-start | bytes 2160004
  9.0 1.3 collective-permute-start.2
  9.5 0.8 collective-permute-start.3
  10.3 8.1 %collective-permute-start.5 = (bf16[3,3,8,384]{3,2,1,0:T(8,128)(2,1)S(1)}, bf16[3,3,8,384]{3,2,1,0:T(8,128)(2,1)S(1)}, u32[]{:S(2)}, u32[]{:S(2)}) collective-permute-start(bf16[3,3,8,384]{3,2,1,0:T(8,128)(2,1)S(1)} %pad_maximum_fusion.1), channel_id=1, source_target_pairs={{0,7},{1,2},{2,1},{3,4},{4,3},{5,6},{6,5},{7,0},{8,15},{9,10},{10,... | collective-permute-start | bytes 165896 | tf_op jit(solution)/shard_map/ppermute | solution.py:516
  16.3 15.8 %collective-permute-start = (bf16[3,384,128]{2,1,0:T(8,128)(2,1)S(1)}, bf16[3,384,128]{2,1,0:T(8,128)(2,1)S(1)}, u32[]{:S(2)}, u32[]{:S(2)}) collective-permute-start(bf16[3,384,128]{2,1,0:T(8,128)(2,1)S(1)} %get-tuple-element.33), channel_id=1, source_target_pairs={{0,1},{1,0},{2,3},{3,2},{4,5},{5,4},{6,7},{7,6},{8,9},{9,8},{10,11... | collective-permute-start | bytes 884744 | tf_op jit(solution)/shard_map/ppermute | solution.py:510
  16.3 16.5 %collective-permute-start.1 = (bf16[3,384,128]{2,1,0:T(8,128)(2,1)S(1)}, bf16[3,384,128]{2,1,0:T(8,128)(2,1)S(1)}, u32[]{:S(2)}, u32[]{:S(2)}) collective-permute-start(bf16[3,384,128]{2,1,0:T(8,128)(2,1)S(1)} %get-tuple-element.34), channel_id=1, source_target_pairs={{0,7},{1,2},{2,1},{3,4},{4,3},{5,6},{6,5},{7,0},{8,15},{9,10},{10,... | collective-permute-start | bytes 884744 | tf_op jit(solution)/shard_map/ppermute | solution.py:511
  18.5 15.0 %copy-start.5 = (bf16[128,8,300]{0,1,2:T(8,128)(2,1)S(1)}, bf16[128,8,300]{0,1,2:T(8,128)(2,1)}, u32[]{:S(2)}) copy-start(bf16[128,8,300]{0,1,2:T(8,128)(2,1)} %param.8) | copy-start | bytes 1843204
  18.5 15.0 %copy-start.7 = (f32[3,1024,128]{2,1,0:T(8,128)S(1)}, f32[3,1024,128]{2,1,0:T(8,128)}, u32[]{:S(2)}) copy-start(f32[3,1024,128]{2,1,0:T(8,128)} %copy-done.6) | copy-start | bytes 4718596
  18.6 13.5 %collective-permute-start.6 = (bf16[4,3,8,384]{3,2,1,0:T(8,128)(2,1)S(1)}, bf16[4,3,8,384]{3,2,1,0:T(8,128)(2,1)S(1)}, u32[]{:S(2)}, u32[]{:S(2)}) collective-permute-start(bf16[4,3,8,384]{3,2,1,0:T(8,128)(2,1)S(1)} %maximum_select_fusion.refs_16_), channel_id=1, source_target_pairs={{28,24},{29,25},{30,26},{31,27},{24,28},{25,29},{26,30},{27,31}} | collective-permute-start | bytes 221192 | tf_op jit(solution)/shard_map/ppermute | solution.py:409
  19.4 12.7 %collective-permute-start.4 = (bf16[3,3,8,384]{3,2,1,0:T(8,128)(2,1)S(1)}, bf16[3,3,8,384]{3,2,1,0:T(8,128)(2,1)S(1)}, u32[]{:S(2)}, u32[]{:S(2)}) collective-permute-start(bf16[3,3,8,384]{3,2,1,0:T(8,128)(2,1)S(1)} %pad_maximum_fusion.1), channel_id=1, source_target_pairs={{0,1},{1,0},{2,3},{3,2},{4,5},{5,4},{6,7},{7,6},{8,9},{9,8},{10,11... | collective-permute-start | bytes 165896 | tf_op jit(solution)/shard_map/ppermute | solution.py:515
  55.5 2.9 %collective-permute-start.7 = (bf16[3,8,384]{2,1,0:T(8,128)(2,1)S(1)}, bf16[3,8,384]{2,1,0:T(8,128)(2,1)S(1)}, u32[]{:S(2)}, u32[]{:S(2)}) collective-permute-start(bf16[3,8,384]{2,1,0:T(8,128)(2,1)S(1)} %get-tuple-element.40), channel_id=1, source_target_pairs={{0,8},{1,9},{2,10},{3,11},{4,12},{5,13},{6,14},{7,15},{8,0},{9,1},... | collective-permute-start | bytes 55304 | tf_op jit(solution)/shard_map/ppermute | solution.py:512
  57.5 0.8 collective-permute-start.8
  59.0 7.1 %collective-permute-start.12 = (bf16[3,3,8,384]{3,2,1,0:T(8,128)(2,1)}, bf16[3,3,8,384]{3,2,1,0:T(8,128)(2,1)S(1)}, u32[]{:S(2)}, u32[]{:S(2)}) collective-permute-start(bf16[3,3,8,384]{3,2,1,0:T(8,128)(2,1)} %pad_maximum_fusion.2), channel_id=1, source_target_pairs={{0,7},{1,2},{2,1},{3,4},{4,3},{5,6},{6,5},{7,0},{8,15},{9,10},{10,... | collective-permute-start | bytes 165896 | tf_op jit(solution)/shard_map/ppermute | solution.py:516
  59.7 19.4 %collective-permute-start.10 = (bf16[3,384,128]{2,1,0:T(8,128)(2,1)}, bf16[3,384,128]{2,1,0:T(8,128)(2,1)}, u32[]{:S(2)}, u32[]{:S(2)}) collective-permute-start(bf16[3,384,128]{2,1,0:T(8,128)(2,1)} %get-tuple-element.46), channel_id=1, source_target_pairs={{0,7},{1,2},{2,1},{3,4},{4,3},{5,6},{6,5},{7,0},{8,15},{9,10},{10,... | collective-permute-start | bytes 884744 | tf_op jit(solution)/shard_map/ppermute | solution.py:511
  63.7 15.4 %collective-permute-start.9 = (bf16[3,384,128]{2,1,0:T(8,128)(2,1)}, bf16[3,384,128]{2,1,0:T(8,128)(2,1)}, u32[]{:S(2)}, u32[]{:S(2)}) collective-permute-start(bf16[3,384,128]{2,1,0:T(8,128)(2,1)} %get-tuple-element.45), channel_id=1, source_target_pairs={{0,1},{1,0},{2,3},{3,2},{4,5},{5,4},{6,7},{7,6},{8,9},{9,8},{10,11... | collective-permute-start | bytes 884744 | tf_op jit(solution)/shard_map/ppermute | solution.py:510
  66.1 13.0 %collective-permute-start.13 = (bf16[4,3,8,384]{3,2,1,0:T(8,128)(2,1)S(1)}, bf16[4,3,8,384]{3,2,1,0:T(8,128)(2,1)}, u32[]{:S(2)}, u32[]{:S(2)}) collective-permute-start(bf16[4,3,8,384]{3,2,1,0:T(8,128)(2,1)S(1)} %maximum_select_fusion.1.refs_12_), channel_id=1, source_target_pairs={{28,24},{29,25},{30,26},{31,27},{24,28},{25,29},{26,30},{27,31}} | collective-permute-start | bytes 221192 | tf_op jit(solution)/shard_map/ppermute | solution.py:409
  67.4 11.7 %collective-permute-start.11 = (bf16[3,3,8,384]{3,2,1,0:T(8,128)(2,1)}, bf16[3,3,8,384]{3,2,1,0:T(8,128)(2,1)}, u32[]{:S(2)}, u32[]{:S(2)}) collective-permute-start(bf16[3,3,8,384]{3,2,1,0:T(8,128)(2,1)} %pad_maximum_fusion.2), channel_id=1, source_target_pairs={{0,1},{1,0},{2,3},{3,2},{4,5},{5,4},{6,7},{7,6},{8,9},{9,8},{10,11... | collective-permute-start | bytes 165896 | tf_op jit(solution)/shard_map/ppermute | solution.py:515
  80.2 8.1 %collective-permute-start.14 = (bf16[208,16,128]{2,1,0:T(8,128)(2,1)}, bf16[208,16,128]{2,1,0:T(8,128)(2,1)}, u32[]{:S(2)}, u32[]{:S(2)}) collective-permute-start(bf16[208,16,128]{2,1,0:T(8,128)(2,1)} %dynamic-slice_bitcast_fusion), channel_id=1, source_target_pairs={{0,8},{1,9},{2,10},{3,11},{4,12},{5,13},{6,14},{7,15},{8,0},{9,1},... | collective-permute-start | bytes 2555912 | tf_op jit(solution)/shard_map/ppermute | solution.py:452
  90.7 15.1 %collective-permute-start.15 = (bf16[52,16,128]{2,1,0:T(8,128)(2,1)S(1)}, bf16[52,16,128]{2,1,0:T(8,128)(2,1)S(1)}, u32[]{:S(2)}, u32[]{:S(2)}) collective-permute-start(bf16[52,16,128]{2,1,0:T(8,128)(2,1)S(1)} %get-tuple-element.60), channel_id=1, source_target_pairs={{0,1},{1,0},{2,3},{3,2},{4,5},{5,4},{6,7},{7,6},{8,9},{9,8},{10,11... | collective-permute-start | bytes 638984 | tf_op jit(solution)/shard_map/ppermute | solution.py:452
  92.5 13.2 %collective-permute-start.16 = (bf16[52,16,128]{2,1,0:T(8,128)(2,1)S(1)}, bf16[52,16,128]{2,1,0:T(8,128)(2,1)S(1)}, u32[]{:S(2)}, u32[]{:S(2)}) collective-permute-start(bf16[52,16,128]{2,1,0:T(8,128)(2,1)S(1)} %get-tuple-element.59), channel_id=1, source_target_pairs={{0,16},{1,17},{2,18},{3,19},{4,20},{5,21},{6,22},{7,23},{8,24},{9,... | collective-permute-start | bytes 638984 | tf_op jit(solution)/shard_map/ppermute | solution.py:452
  95.8 10.0 %collective-permute-start.17 = (bf16[52,16,128]{2,1,0:T(8,128)(2,1)S(1)}, bf16[52,16,128]{2,1,0:T(8,128)(2,1)}, u32[]{:S(2)}, u32[]{:S(2)}) collective-permute-start(bf16[52,16,128]{2,1,0:T(8,128)(2,1)S(1)} %get-tuple-element.58), channel_id=1, source_target_pairs={{0,17},{1,16},{2,19},{3,18},{4,21},{5,20},{6,23},{7,22},{8,25},{9,... | collective-permute-start | bytes 638984 | tf_op jit(solution)/shard_map/ppermute | solution.py:452
  107.0 6.5 %collective-permute-start.18 = (bf16[13,16,128]{2,1,0:T(8,128)(2,1)S(1)}, bf16[13,16,128]{2,1,0:T(8,128)(2,1)S(1)}, u32[]{:S(2)}, u32[]{:S(2)}) collective-permute-start(bf16[13,16,128]{2,1,0:T(8,128)(2,1)S(1)} %get-tuple-element.67), channel_id=1, source_target_pairs={{0,4},{1,5},{2,6},{3,7},{4,0},{5,1},{6,2},{7,3},{8,12},{9,13},{10,... | collective-permute-start | bytes 159752 | tf_op jit(solution)/shard_map/ppermute | solution.py:452
  108.7 4.9 %collective-permute-start.19 = (bf16[13,16,128]{2,1,0:T(8,128)(2,1)S(1)}, bf16[13,16,128]{2,1,0:T(8,128)(2,1)S(1)}, u32[]{:S(2)}, u32[]{:S(2)}) collective-permute-start(bf16[13,16,128]{2,1,0:T(8,128)(2,1)S(1)} %get-tuple-element.69), channel_id=1, source_target_pairs={{0,2},{1,3},{2,0},{3,1},{4,6},{5,7},{6,4},{7,5},{8,10},{9,11},{10,... | collective-permute-start | bytes 159752 | tf_op jit(solution)/shard_map/ppermute | solution.py:452
  108.8 6.0 %collective-permute-start.20 = (bf16[13,16,128]{2,1,0:T(8,128)(2,1)S(1)}, bf16[13,16,128]{2,1,0:T(8,128)(2,1)S(1)}, u32[]{:S(2)}, u32[]{:S(2)}) collective-permute-start(bf16[13,16,128]{2,1,0:T(8,128)(2,1)S(1)} %get-tuple-element.68), channel_id=1, source_target_pairs={{0,6},{1,7},{2,4},{3,5},{4,2},{5,3},{6,0},{7,1},{8,14},{9,15},{10,... | collective-permute-start | bytes 159752 | tf_op jit(solution)/shard_map/ppermute | solution.py:452
  114.9 6.2 %collective-permute-start.21 = (bf16[13,16,128]{2,1,0:T(8,128)(2,1)S(1)}, bf16[13,16,128]{2,1,0:T(8,128)(2,1)S(1)}, u32[]{:S(2)}, u32[]{:S(2)}) collective-permute-start(bf16[13,16,128]{2,1,0:T(8,128)(2,1)S(1)} %get-tuple-element.57), channel_id=1, source_target_pairs={{0,4},{1,5},{2,6},{3,7},{4,0},{5,1},{6,2},{7,3},{8,12},{9,13},{10,... | collective-permute-start | bytes 159752 | tf_op jit(solution)/shard_map/ppermute | solution.py:462
  115.4 5.7 %collective-permute-start.22 = (bf16[13,16,128]{2,1,0:T(8,128)(2,1)S(1)}, bf16[13,16,128]{2,1,0:T(8,128)(2,1)S(1)}, u32[]{:S(2)}, u32[]{:S(2)}) collective-permute-start(bf16[13,16,128]{2,1,0:T(8,128)(2,1)S(1)} %get-tuple-element.57), channel_id=1, source_target_pairs={{0,2},{1,3},{2,0},{3,1},{4,6},{5,7},{6,4},{7,5},{8,10},{9,11},{10,... | collective-permute-start | bytes 159752 | tf_op jit(solution)/shard_map/ppermute | solution.py:462
  118.0 5.9 %collective-permute-start.23 = (bf16[13,16,128]{2,1,0:T(8,128)(2,1)S(1)}, bf16[13,16,128]{2,1,0:T(8,128)(2,1)S(1)}, u32[]{:S(2)}, u32[]{:S(2)}) collective-permute-start(bf16[13,16,128]{2,1,0:T(8,128)(2,1)S(1)} %get-tuple-element.57), channel_id=1, source_target_pairs={{0,6},{1,7},{2,4},{3,5},{4,2},{5,3},{6,0},{7,1},{8,14},{9,15},{10,... | collective-permute-start | bytes 159752 | tf_op jit(solution)/shard_map/ppermute | solution.py:462
  124.0 7.1 %collective-permute-start.24 = (bf16[52,16,128]{2,1,0:T(8,128)(2,1)S(1)}, bf16[52,16,128]{2,1,0:T(8,128)(2,1)S(1)}, u32[]{:S(2)}, u32[]{:S(2)}) collective-permute-start(bf16[52,16,128]{2,1,0:T(8,128)(2,1)S(1)} %pad_maximum_fusion), channel_id=1, source_target_pairs={{0,1},{1,0},{2,3},{3,2},{4,5},{5,4},{6,7},{7,6},{8,9},{9,8},{10,11... | collective-permute-start | bytes 638984 | tf_op jit(solution)/shard_map/ppermute | solution.py:462
  125.5 8.2 %collective-permute-start.25 = (bf16[52,16,128]{2,1,0:T(8,128)(2,1)S(1)}, bf16[52,16,128]{2,1,0:T(8,128)(2,1)S(1)}, u32[]{:S(2)}, u32[]{:S(2)}) collective-permute-start(bf16[52,16,128]{2,1,0:T(8,128)(2,1)S(1)} %pad_maximum_fusion), channel_id=1, source_target_pairs={{0,16},{1,17},{2,18},{3,19},{4,20},{5,21},{6,22},{7,23},{8,24},{9,... | collective-permute-start | bytes 638984 | tf_op jit(solution)/shard_map/ppermute | solution.py:462
  127.5 7.0 %collective-permute-start.26 = (bf16[52,16,128]{2,1,0:T(8,128)(2,1)S(1)}, bf16[52,16,128]{2,1,0:T(8,128)(2,1)S(1)}, u32[]{:S(2)}, u32[]{:S(2)}) collective-permute-start(bf16[52,16,128]{2,1,0:T(8,128)(2,1)S(1)} %pad_maximum_fusion), channel_id=1, source_target_pairs={{0,17},{1,16},{2,19},{3,18},{4,21},{5,20},{6,23},{7,22},{8,25},{9,... | collective-permute-start | bytes 638984 | tf_op jit(solution)/shard_map/ppermute | solution.py:462
  134.6 2.4 %collective-permute-start.27 = (bf16[208,16,128]{2,1,0:T(8,128)(2,1)S(1)}, bf16[208,16,128]{2,1,0:T(8,128)(2,1)S(1)}, u32[]{:S(2)}, u32[]{:S(2)}) collective-permute-start(bf16[208,16,128]{2,1,0:T(8,128)(2,1)S(1)} %get-tuple-element.61), channel_id=1, source_target_pairs={{0,8},{1,9},{2,10},{3,11},{4,12},{5,13},{6,14},{7,15},{8,0},{9,1},... | collective-permute-start | bytes 2555912 | tf_op jit(solution)/shard_map/ppermute | solution.py:462
  (19 other events, 90.1 us)

commit v3 on v2

--- a/solution.py
+++ b/solution.py
@@ -17,8 +17,9 @@
 HB = 256
 VM = pl.BlockSpec(memory_space=pltpu.VMEM)
 SM = pl.BlockSpec(memory_space=pltpu.SMEM)
-
-EVEN_LON, EVEN_LAT, IS_TOP, LON, START, ME = range(6)
+ANY = pl.BlockSpec(memory_space=pl.ANY)
+
+EVEN_LON, EVEN_LAT, IS_TOP, LON, START, ME, CORE = range(7)
 
 
 def cost(us):
@@ -75,35 +76,66 @@
                     a = x_ref[l, pl.ds(pl.multiple_of(t * 64 + (first + c) * 8, 8), 8), :]
                     b = x_ref[l, pl.ds(pl.multiple_of(t * 64 + 64 + (first + c) * 8, 8), 8), :]
                     q_ref[l, (c * tt + t) * 8 : (c * tt + t) * 8 + 16, :] = jnp.concatenate([a, b], 0).astype(BF16)
-
-
-def prepare_kernel(sc, mask_ref, f_ref, c_ref, mf_ref, bk_ref, q1_ref, q2_ref, p1_ref, p2_ref, cm, rows, ct):
-    width = f_ref.shape[0]
+            q_ref[l, 3 * tt * 8 :, :] = jnp.zeros((32, 128), BF16)
+
+
+def corners_kernel(sc, p1_ref, p2_ref, _, __, q1_ref, q2_ref, lu, corner, sem):
+    even_lat, even = sc[EVEN_LAT], sc[EVEN_LON]
+    p1, p2 = p1_ref[...].astype(F32), p2_ref[...].astype(F32)
+    lower = jnp.where(even_lat == 1, p2, p1)
+    upper = jnp.where(even_lat == 1, p1, p2)
+    for l in range(LT):
+        for r in range(3):
+            lu[l, 8 * r : 8 * r + 8, :] = lower[r, :, 128 * l : 128 * (l + 1)]
+            lu[l, 24 + 8 * r : 32 + 8 * r, :] = upper[r, :, 128 * l : 128 * (l + 1)]
+        lu[l, 48:, :] = jnp.zeros((16, 128), F32)
+    copies = []
+    for n, (q_ref, first) in enumerate(((q1_ref, 5 * even), (q2_ref, 5 - 5 * even))):
+        for l in range(LT):
+            k = [lu[l, pl.ds(first + c, 8, stride=8), :] for c in range(3)]
+            k.append(jnp.zeros((8, 128), F32))
+            corner[n, l] = jnp.concatenate(k, 0).astype(BF16)
+        rows = q_ref.shape[1]
+        copies.append(pltpu.make_async_copy(corner.at[n], q_ref.at[:, pl.ds(rows - 32, 32), :], sem.at[n]))
+        copies[-1].start()
+    for copy in copies:
+        copy.wait()
+
+
+def masked_cells(mask_ref, src, cm, dst):
+    width = src.shape[0]
     m = mask_ref[...].astype(F32)[None]
     cm[width * 8 :, :] = jnp.zeros((cm.shape[0] - width * 8, 128), F32)
-    for src, dst in ((f_ref, mf_ref), (c_ref, ct)):
-        cm[: width * 8, :] = (src[...].astype(F32) * m).reshape(width * 8, 128)
-        for l in range(LT):
-            for i in range(COLS):
-
-                def put(at, v, l=l, dst=dst):
-                    dst[l, at, :] = v
-
-                to_cells(cm, l, i, put)
+    cm[: width * 8, :] = (src[...].astype(F32) * m).reshape(width * 8, 128)
+    for l in range(LT):
+        for i in range(COLS):
+
+            def put(at, v, l=l):
+                dst[l, at, :] = v
+
+            to_cells(cm, l, i, put)
+
+
+def prepare_kernel(sc, mask_ref, f_ref, mf_ref, p1_ref, p2_ref, q1_ref, q2_ref, cm, rows):
+    masked_cells(mask_ref, f_ref, cm, mf_ref)
+    row_messages(sc, mf_ref, rows, p1_ref, p2_ref)
     strip_messages(sc, mf_ref, q1_ref, q2_ref)
-    row_messages(sc, mf_ref, rows, p1_ref, p2_ref)
+
+
+def back_kernel(mask_ref, c_ref, bk_ref, cm, ct):
+    masked_cells(mask_ref, c_ref, cm, ct)
     for l in range(LT):
         bk_ref[:, 128 * l : 128 * (l + 1)] = ct[l].astype(BF16)
 
 
-def extend(sc, ext, x_ref, q1_ref, q2_ref, p1_ref, p2_ref, c1_ref, c2_ref):
+def extend(sc, ext, x_ref, q1_ref, q2_ref, p1_ref, p2_ref):
     tt = x_ref.shape[1] // 64
     even_lat, even_lon, top = sc[EVEN_LAT], sc[EVEN_LON], sc[IS_TOP]
     for l in range(LT):
         for t in range(tt):
             ext[l, ((t + 3) * QC + 3) * 8 : ((t + 3) * QC + 3) * 8 + 64, :] = x_ref[l, t * 64 : t * 64 + 64, :]
-    sides = ((q1_ref, c1_ref, even_lon), (q2_ref, c2_ref, 1 - even_lon))
-    for q_ref, _, right in sides:
+    sides = ((q1_ref, even_lon), (q2_ref, 1 - even_lon))
+    for q_ref, right in sides:
         for l in range(LT):
             for c in range(3):
                 for t in range(0, tt, 2):
@@ -127,18 +159,15 @@
         for r in range(3):
             ext[l, pl.ds((r * QC + 3) * 8, 8, stride=8), :] = lower[r, :, 128 * l : 128 * (l + 1)]
             ext[l, pl.ds(((tt + 3 + r) * QC + 3) * 8 + 7, 8, stride=8), :] = upper[r, :, 128 * l : 128 * (l + 1)]
-    for _, c_ref, right in sides:
+    for q_ref, right in sides:
         first = 11 * right
-        for r in range(3):
-            lo = c_ref[even_lat, r].astype(F32)
-            up = c_ref[1 - even_lat, r].astype(F32) * keep
+        for l in range(LT):
+            corner = q_ref[l, 3 * tt * 8 : 3 * tt * 8 + 32, :].astype(F32)
             for c in range(3):
-                lo_row = jnp.where(right == 1, lo[c : c + 1], lo[5 + c : 6 + c])
-                up_row = jnp.where(right == 1, up[c : c + 1], up[5 + c : 6 + c])
-                for l in range(LT):
-                    ext[l, pl.ds((r * QC + first + c) * 8, 1), :] = lo_row[:, 128 * l : 128 * (l + 1)]
+                for r in range(3):
+                    ext[l, pl.ds((r * QC + first + c) * 8, 1), :] = corner[8 * c + r : 8 * c + r + 1]
                     at = ((tt + 3 + r) * QC + first + c) * 8 + 7
-                    ext[l, pl.ds(at, 1), :] = up_row[:, 128 * l : 128 * (l + 1)]
+                    ext[l, pl.ds(at, 1), :] = corner[8 * c + 3 + r : 8 * c + 4 + r] * keep
 
 
 def fold_rows(sc, mir, fold_refs, buf, dst, base):
@@ -157,13 +186,19 @@
         col = jnp.where(col < 0, col + total, col)
         col = jnp.where(col >= total, col - total, col)
         m = mir[col]
-        unit = lax.shift_right_logical(m, 3) - sc[LON] + 1 + sc[EVEN_LON]
-        unit = jnp.where(unit < 0, unit + first, unit)
-        unit = jnp.where(unit >= first, unit - first, unit)
+        unit = lax.bitwise_xor(lax.shift_right_logical(m, 3), sc[LON])
         at = unit * 24 + lax.bitwise_and(m, 7)
         for k in range(3):
             for l in range(LT):
                 dst[l, pl.ds(base + (k * QC + q) * 8 + 7, 1), :] = buf[l, pl.ds(at + (2 - k) * 8, 1), :]
+
+
+def extend_all(sc, mir, ext, buf, x_ref, halos, folds):
+    extend(sc, ext, x_ref, *halos)
+
+    @pl.when(sc[IS_TOP] == 1)
+    def _():
+        fold_rows(sc, mir, folds, buf, ext, (x_ref.shape[1] // 64 + 3) * QC * 8)
 
 
 def correlate(ext, ks, tt, flip, store):
@@ -193,20 +228,23 @@
 
 DWR = 304
 DKR = 64
-
-
-def block_kernel(width, nf, sc, mir, k_ref, gain_ref, win_ref, wout_ref, mask_ref, f_ref, mf_ref, bk_ref, *refs):
-    halos, folds = refs[:6], refs[6 : 6 + nf]
-    out_ref, ext, gc_ref, q1_ref, q2_ref, g1_ref, g2_ref, dw_ref, dgain_ref = refs[6 + nf : 15 + nf]
-    ks, buf, conv, normed, act, gp, res, rows, cm = refs[15 + nf :]
+DKT = LT * DKR // 16
+
+
+def block_kernel(width, nf, sc, mir, k_ref, gain_ref, mask_ref, mf_ref, win_any, wout_any, f_any, bk_any, *refs):
+    halos, folds = refs[:4], refs[4 : 4 + nf]
+    out_ref, gc_ref, g1_ref, g2_ref, q1_ref, q2_ref, dw_ref, dgain_ref = refs[4 + nf : 12 + nf]
+    ks, buf, ext, conv, normed, act, gp, res, rows, cm, win_ref, wout_ref, f_ref, bk_ref, sem = refs[12 + nf :]
+    late = [
+        pltpu.make_async_copy(src, dst, sem.at[n])
+        for n, (src, dst) in enumerate(((win_any, win_ref), (wout_any, wout_ref), (bk_any, bk_ref), (f_any, f_ref)))
+    ]
+    for copy in late:
+        copy.start()
     cells = mf_ref.shape[1]
     tt = cells // 64
     hidden = win_ref.shape[1]
-    extend(sc, ext, mf_ref, *halos)
-
-    @pl.when(sc[IS_TOP] == 1)
-    def _():
-        fold_rows(sc, mir, folds, buf, ext, (tt + 3) * QC * 8)
+    extend_all(sc, mir, ext, buf, mf_ref, halos, folds)
 
     tap_rows(k_ref, ks, width)
 
@@ -214,6 +252,8 @@
         conv[pl.ds(pl.multiple_of(t * 64 + i * 8, 8), 8), 128 * l : 128 * (l + 1)] = v
 
     correlate(ext, ks, tt, False, put)
+    for copy in late:
+        copy.wait()
     size = 256
     gain = gain_ref[...]
     valid = (lax.broadcasted_iota(jnp.int32, (1, CP), 1) < width).astype(F32)
@@ -256,8 +296,8 @@
         return carry
 
     lax.fori_loop(0, cells // size, chunk, 0)
+    row_messages(sc, gc_ref, rows, g1_ref, g2_ref)
     strip_messages(sc, gc_ref, q1_ref, q2_ref)
-    row_messages(sc, gc_ref, rows, g1_ref, g2_ref)
     tiles = (hidden // 128) * (DWR // 16)
     for m, (left, right) in enumerate(((normed, gp), (bk_ref, act))):
         for h in range(0, hidden, HB):
@@ -274,8 +314,11 @@
     out_ref[...] = (mask_ref[...].astype(F32)[None] * (f_ref[...].astype(F32) + mixed)).astype(BF16)
 
 
-def taps_kernel(count, ext, gc_ref, dgain_ref, dw_ref, dk_ref, part, rows, tiles, sem):
+def taps_kernel(nf, sc, mir, x_ref, gc_ref, dgain_ref, *refs):
+    halos, folds = refs[:4], refs[4 : 4 + nf]
+    tiles, buf, ext, part, rows = refs[4 + nf :]
     tt = gc_ref.shape[1] // 64
+    extend_all(sc, mir, ext, buf, x_ref, halos, folds)
     for l in range(LT):
 
         def tap_column(b, carry, l=l):
@@ -301,14 +344,11 @@
         rows[l, 49:50, :] = dgain_ref[0:1, 128 * l : 128 * (l + 1)]
         for r in range(DKR // 16):
             tiles[l * (DKR // 16) + r] = rows[l, 16 * r : 16 * r + 16, :].astype(BF16)
-    copy = pltpu.make_async_copy(tiles, dk_ref.at[pl.ds(count, LT * (DKR // 16))], sem)
-    copy.start()
-    copy.wait()
 
 
 def field_kernel(width, nf, sc, mir, k_ref, mask_ref, c_ref, gc_ref, *refs):
-    halos, folds = refs[:6], refs[6 : 6 + nf]
-    out_ref, ks, buf, ext, ghost, dm, cm = refs[6 + nf :]
+    halos, folds = refs[:4], refs[4 : 4 + nf]
+    out_ref, ks, buf, ext, ghost, dm, cm = refs[4 + nf :]
     cells = gc_ref.shape[1]
     tt = cells // 64
     extend(sc, ext, gc_ref, *halos)
@@ -344,29 +384,38 @@
     out_ref[...] = (mask_ref[...].astype(F32)[None] * (c_ref[...].astype(F32) + total)).astype(BF16)
 
 
-def unpack_kernel(width, hidden, factor, per, sc, x_ref, gin_ref, gout_ref, gk_ref, gg_ref):
+def unpack_kernel(width, hidden, factor, per, half, sc, own_ref, got_ref, gin_ref, gout_ref, gk_ref, gg_ref):
     blocks = (hidden + 127) // 128
     blocks += blocks % 2
     tr = DWR // 16
 
-    def tile(n):
-        chunk = lax.bitwise_xor(jnp.int32(n // per), sc[ME])
-        return x_ref[chunk * per + n % per].astype(F32) * factor
-
-    for cb in range(blocks):
-        w = min(128, hidden - 128 * cb)
-        if w <= 0:
-            continue
-        for r in range(tr):
-            rows = min(16, width - 16 * r)
-            gin_ref[16 * r : 16 * r + rows, 128 * cb : 128 * cb + w] = tile(cb * tr + r)[:rows, :w]
-            gout_ref[16 * r : 16 * r + rows, 128 * cb : 128 * cb + w] = tile((blocks + cb) * tr + r)[:rows, :w]
+    for core in range(2):
+
+        @pl.when(sc[CORE] == core)
+        def _(core=core):
+            def tile(n):
+                ref = own_ref if n // half == core else got_ref
+                chunk = lax.bitwise_xor(jnp.int32((n % half) // per), sc[ME])
+                return ref[chunk * per + n % per].astype(F32) * factor
+
+            for m, out in enumerate((gin_ref, gout_ref)):
+                for cb in range(blocks):
+                    w = min(128, hidden - 128 * cb)
+                    if w <= 0:
+                        continue
+                    for r in range(tr):
+                        rows = min(16, width - 16 * r)
+                        out[16 * r : 16 * r + rows, 128 * cb : 128 * cb + w] = tile((m * blocks + cb) * tr + r)[:rows, :w]
+
     for l in range(LT):
         w = lanes(l, width)
-        base = 2 * blocks * tr + l * (DKR // 16)
-        taps = jnp.concatenate([tile(base + r) for r in range(DKR // 16)], axis=0)
-        gk_ref[:, 128 * l : 128 * l + w] = taps[:49, :w]
-        gg_ref[:, 128 * l : 128 * l + w] = taps[49:50, :w]
+        for r in range(DKR // 16):
+            n = half + l * (DKR // 16) + r
+            v = (own_ref[n].astype(F32) + got_ref[n].astype(F32)) * factor
+            rows = min(16, 49 - 16 * r)
+            gk_ref[16 * r : 16 * r + rows, 128 * l : 128 * l + w] = v[:rows, :w]
+            if rows < 16:
+                gg_ref[:, 128 * l : 128 * l + w] = v[rows : rows + 1, :w]
 
 
 def swaps(n_lat, n_lon, bits):
@@ -397,17 +446,17 @@
     return first, second
 
 
-def fold_gather(own, pair, c2, even_lon, n_lat, n_lon):
-    up = jnp.stack([c2[1], c2[2], own, pair])
-    down = jnp.stack([pair, own, c2[2], c2[1]])
-    units = [jnp.where(even_lon, up, down)]
+def fold_gather(own, pair, n_lat, n_lon):
+    units = [jnp.stack([own, pair])]
     top = n_lat - 1
-    step = 4
-    while step < n_lon:
+    bit = 2
+    while bit < n_lon:
         have = jnp.concatenate(units) if len(units) > 1 else units[0]
-        pairs = [(top * n_lon + (o + step) % n_lon, top * n_lon + o) for o in range(n_lon)]
-        units.append(lax.ppermute(have, AXES, pairs))
-        step *= 2
+        end = min(4 * bit, n_lon)
+        for d in range(bit, end, bit):
+            pairs = [(top * n_lon + o, top * n_lon + (o ^ d)) for o in range(n_lon)]
+            units.append(lax.ppermute(have, AXES, pairs))
+        bit = end
     return units
 
 
@@ -439,29 +488,53 @@
     return masks
 
 
-def all_sum(x, beside, lat, lon, n_lat, n_lon):
-    groups = stages(n_lat, n_lon)
-    for k, group in enumerate(groups):
-        n = 1 << len(group)
-        x = x.reshape((n, x.shape[0] // n) + x.shape[1:])
-        idx = group_index(group, lat, lon)
-        masks = group_masks(group)
-        got = []
-        for d in range(1, n):
-            piece = lax.dynamic_index_in_dim(x, idx ^ d, 0, False)
-            got.append(lax.ppermute(piece, AXES, swaps(n_lat, n_lon, masks[d])))
-        if k == 1:
-            got, beside = lax.optimization_barrier((got, beside))
-        total = lax.dynamic_index_in_dim(x, idx, 0, False).astype(F32)
-        for g in got:
-            total = total + g.astype(F32)
-        x = total.astype(BF16)
-    for group in reversed(groups):
-        masks = group_masks(group)
-        x = jnp.concatenate(
-            [x] + [lax.ppermute(x, AXES, swaps(n_lat, n_lon, masks[d])) for d in range(1, len(masks))], axis=0
-        )
-    return x, beside
+def scatter_stage(x, group, lat, lon, n_lat, n_lon, beside=None):
+    n = 1 << len(group)
+    x = x.reshape((n, x.shape[0] // n) + x.shape[1:])
+    idx = group_index(group, lat, lon)
+    masks = group_masks(group)
+    got = []
+    for d in range(1, n):
+        piece = lax.dynamic_index_in_dim(x, idx ^ d, 0, False)
+        got.append(lax.ppermute(piece, AXES, swaps(n_lat, n_lon, masks[d])))
+    if beside is not None:
+        got, beside = lax.optimization_barrier((got, beside))
+    total = lax.dynamic_index_in_dim(x, idx, 0, False).astype(F32)
+    for g in got:
+        total = total + g.astype(F32)
+    return total.astype(BF16), beside
+
+
+def packet_kernel(*refs):
+    ins, out_ref = refs[:-1], refs[-1]
+    size = ins[0].shape[0] - DKT
+    total = ins[0][size:].astype(F32)
+    for k, ref in enumerate(ins):
+        out_ref[k * size : (k + 1) * size] = ref[:size]
+        if k:
+            total = total + ref[size:].astype(F32)
+    out_ref[len(ins) * size :] = total.astype(BF16)
+
+
+def gather_stage(packet, group, n_lat, n_lon, beside=None):
+    masks = group_masks(group)
+    got = [lax.ppermute(packet, AXES, swaps(n_lat, n_lon, masks[d])) for d in range(1, len(masks))]
+    if beside is not None:
+        got, beside = lax.optimization_barrier((got, beside))
+    return [packet] + got, beside
+
+
+def join(pieces):
+    n, size = len(pieces), pieces[0].shape[0] - DKT
+    return pl.pallas_call(
+        packet_kernel,
+        out_shape=jax.ShapeDtypeStruct((n * size + DKT, 16, 128), BF16),
+        in_specs=[VM] * n,
+        out_specs=VM,
+        compiler_params=params(),
+        name="join",
+        cost_estimate=cost(1),
+    )(*pieces)
 
 
 def body(field_in, sea_mask, mirror, kernel, norm_gain, proj_in, proj_out, cotangent):
@@ -474,10 +547,10 @@
     tt = nrows // SUB
     groups = stages(n_lat, n_lon)
     me = jnp.int32(0)
-    for group in groups:
+    for group in groups[1:]:
         me = (me << len(group)) + group_index(group, lat, lon)
     sc = jnp.stack(
-        [1 - lon % 2, 1 - lat % 2, (lat == n_lat - 1).astype(jnp.int32), lon, lon * ncols, me, jnp.int32(0), jnp.int32(0)]
+        [1 - lon % 2, 1 - lat % 2, (lat == n_lat - 1).astype(jnp.int32), lon, lon * ncols, me, lat % 2, jnp.int32(0)]
     ).astype(jnp.int32)
     assert nrows == 128 and n_lon % 4 == 0
     hp = -(-hidden // HB) * HB
@@ -490,117 +563,148 @@
 
     s = jax.ShapeDtypeStruct
     row_msg = s((3, COLS, CP), BF16)
-    strip_msg = s((LT, 3 * tt * 8, 128), BF16)
+    strip_msg = s((LT, 3 * tt * 8 + 32, 128), BF16)
     channels = pltpu.VMEM((CP * 8, 128), F32)
-    mf, bk, q1, q2, p1, p2 = pl.pallas_call(
+    cells_f32 = pltpu.VMEM((LT, cells, 128), F32)
+    ext_f32 = pltpu.VMEM((LT, (tt + 6) * QC * 8, 128), F32)
+    fold_f32 = pltpu.VMEM((LT, n_lon * 24, 128), F32)
+    rows_f32 = pltpu.VMEM((6, COLS, CP), F32)
+    taps_f32 = pltpu.VMEM((LT, 56, 128), F32)
+    mf, p1, p2, q1, q2 = pl.pallas_call(
         prepare_kernel,
-        out_shape=(s((LT, cells, 128), F32), s((cells, CP), BF16), strip_msg, strip_msg, row_msg, row_msg),
-        in_specs=[SM, VM, VM, VM],
-        out_specs=(VM,) * 6,
-        scratch_shapes=[channels, pltpu.VMEM((6, COLS, CP), F32), pltpu.VMEM((LT, cells, 128), F32)],
-        compiler_params=params(9),
+        out_shape=(s((LT, cells, 128), F32), row_msg, row_msg, strip_msg, strip_msg),
+        in_specs=[SM, VM, VM],
+        out_specs=(VM,) * 5,
+        scratch_shapes=[channels, rows_f32],
+        compiler_params=params(),
         name="prepare",
-        cost_estimate=cost(5),
-    )(sc, mask_c, field_c, cot_c)
+        cost_estimate=cost(3),
+    )(sc, mask_c, field_c)
+    bk = pl.pallas_call(
+        back_kernel,
+        out_shape=s((cells, CP), BF16),
+        in_specs=[VM, VM],
+        out_specs=VM,
+        scratch_shapes=[channels, cells_f32],
+        compiler_params=params(),
+        name="back",
+        cost_estimate=cost(3),
+    )(mask_c, cot_c)
 
     lat1, lat2 = lat_swaps(n_lat, n_lon)
     lon1, lon2 = lon_swaps(n_lat, n_lon)
 
-    def halo(q1, q2, p1, p2):
+    def halo(q1, q2, p1, p2, beside):
+        r1 = lax.ppermute(p1, AXES, lat1)
+        r2 = lax.ppermute(p2, AXES, lat2)
+        r1, r2, beside = lax.optimization_barrier((r1, r2, beside))
+        q1, q2 = pl.pallas_call(
+            corners_kernel,
+            out_shape=(strip_msg, strip_msg),
+            in_specs=[SM, VM, VM, ANY, ANY],
+            out_specs=(ANY, ANY),
+            scratch_shapes=[
+                pltpu.VMEM((LT, 64, 128), F32),
+                pltpu.VMEM((2, LT, 32, 128), BF16),
+                pltpu.SemaphoreType.DMA((2,)),
+            ],
+            input_output_aliases={3: 0, 4: 1},
+            compiler_params=params(),
+            name="corners",
+            cost_estimate=cost(1),
+        )(sc, r1, r2, q1, q2)
         s1 = lax.ppermute(q1, AXES, lon1)
         s2 = lax.ppermute(q2, AXES, lon2)
-        r1 = lax.ppermute(p1, AXES, lat1)
-        r2 = lax.ppermute(p2, AXES, lat2)
-        rows = jnp.stack([r1, r2, p2])
-        c1 = lax.ppermute(rows, AXES, lon1)
-        c2 = lax.ppermute(rows, AXES, lon2)
-        folds = fold_gather(p2, r2, c2, lon % 2 == 0, n_lat, n_lon)
-        return [s1, s2, r1, r2, c1, c2] + folds, rows
-
-    halos, _ = halo(q1, q2, p1, p2)
-    nf = len(halos) - 6
+        return [s1, s2, r1, r2] + fold_gather(p2, r2, n_lat, n_lon), beside
+
+    halos, bk = halo(q1, q2, p1, p2, bk)
+    nf = len(halos) - 4
     count = 2 * (hp // 128) * (DWR // 16)
     devices = n_lat * n_lon
-    per = -(-(count + LT * DKR // 16) // devices)
-    out, ext, gc, q1, q2, g1, g2, dw, dgain = pl.pallas_call(
+    per = -(-count // devices)
+    half = per * devices // 2
+    out, gc, g1, g2, q1, q2, dw, dgain = pl.pallas_call(
         lambda *refs: block_kernel(width, nf, *refs),
         out_shape=(
             s((width, COLS, nrows), BF16),
-            s((LT, (tt + 6) * QC * 8, 128), F32),
             s((LT, cells, 128), F32),
+            row_msg,
+            row_msg,
             strip_msg,
             strip_msg,
-            row_msg,
-            row_msg,
             s((per * devices, 16, 128), BF16),
             s((8, CP), F32),
         ),
-        in_specs=[SM, SM] + [VM] * (len(halos) + 8),
-        out_specs=(VM,) * 9,
+        in_specs=[SM, SM] + [VM] * 4 + [ANY] * 4 + [VM] * len(halos),
+        out_specs=(VM,) * 8,
         scratch_shapes=[
-            pltpu.VMEM((LT, 56, 128), F32),
-            pltpu.VMEM((LT, n_lon * 24, 128), F32),
+            taps_f32,
+            fold_f32,
+            ext_f32,
             pltpu.VMEM((cells, CP), F32),
             pltpu.VMEM((cells, CP), BF16),
             pltpu.VMEM((cells, hp), BF16),
             pltpu.VMEM((cells, hp), BF16),
-            pltpu.VMEM((LT, cells, 128), F32),
-            pltpu.VMEM((6, COLS, CP), F32),
+            cells_f32,
+            rows_f32,
             channels,
+            pltpu.VMEM((CP, hp), BF16),
+            pltpu.VMEM((CP, hp), BF16),
+            pltpu.VMEM((width, COLS, nrows), BF16),
+            pltpu.VMEM((cells, CP), BF16),
+            pltpu.SemaphoreType.DMA((4,)),
         ],
-        compiler_params=params(20),
+        compiler_params=params(),
         name="block",
-        cost_estimate=cost(20),
-    )(sc, mirror, kernel, gain, win, wout, mask_c, field_c, mf, bk, *halos)
-
-    ghalos, rows = halo(q1, q2, g1, g2)
-    gc_late, _ = lax.optimization_barrier((gc, rows))
-    packed = pl.pallas_call(
-        lambda *refs: taps_kernel(count, *refs),
-        out_shape=s((per * devices, 16, 128), BF16),
-        in_specs=[VM] * 3 + [pl.BlockSpec(memory_space=pl.ANY)],
-        out_specs=pl.BlockSpec(memory_space=pl.ANY),
-        scratch_shapes=[
-            pltpu.VMEM((LT, 49 * 8, 128), F32),
-            pltpu.VMEM((LT, DKR, 128), F32),
-            pltpu.VMEM((LT * DKR // 16, 16, 128), BF16),
-            pltpu.SemaphoreType.DMA,
-        ],
-        input_output_aliases={3: 0},
-        compiler_params=params(6),
+        cost_estimate=cost(18),
+    )(sc, mirror, kernel, gain, mask_c, mf, win, wout, field_c, bk, *halos)
+
+    first, _ = scatter_stage(dw, groups[0], lat, lon, n_lat, n_lon)
+    ghalos, first = halo(q1, q2, g1, g2, first)
+    gc_taps, dgain, _ = lax.optimization_barrier((gc, dgain, first))
+    dk = pl.pallas_call(
+        lambda *refs: taps_kernel(nf, *refs),
+        out_shape=s((LT * DKR // 16, 16, 128), BF16),
+        in_specs=[SM, SM] + [VM] * (len(halos) + 3),
+        out_specs=VM,
+        scratch_shapes=[fold_f32, ext_f32, pltpu.VMEM((LT, 49 * 8, 128), F32), pltpu.VMEM((LT, DKR, 128), F32)],
+        compiler_params=params(),
         name="taps",
-        cost_estimate=cost(9),
-    )(ext, gc_late, dgain, dw)
+        cost_estimate=cost(1),
+    )(sc, mirror, mf, gc_taps, dgain, *halos)
+    x = first
+    for k, group in enumerate(groups[1:]):
+        beside = (dk, ghalos) if k == 0 else None
+        x, beside = scatter_stage(x, group, lat, lon, n_lat, n_lon, beside)
+        if beside is not None:
+            dk, ghalos = beside
     grad_field = pl.pallas_call(
         lambda *refs: field_kernel(width, nf, *refs),
         out_shape=s((width, COLS, nrows), BF16),
         in_specs=[SM, SM] + [VM] * (len(ghalos) + 4),
         out_specs=VM,
-        scratch_shapes=[
-            pltpu.VMEM((LT, 56, 128), F32),
-            pltpu.VMEM((LT, n_lon * 24, 128), F32),
-            pltpu.VMEM((LT, (tt + 6) * QC * 8, 128), F32),
-            pltpu.VMEM((LT, 3 * QC * 8, 128), F32),
-            pltpu.VMEM((LT, cells, 128), F32),
-            channels,
-        ],
-        compiler_params=params(12),
+        scratch_shapes=[taps_f32, fold_f32, ext_f32, pltpu.VMEM((LT, 3 * QC * 8, 128), F32), cells_f32, channels],
+        compiler_params=params(),
         name="field",
-        cost_estimate=cost(11),
+        cost_estimate=cost(10),
     )(sc, mirror, kernel, mask_c, cot_c, gc, *ghalos)
-
-    packed, _ = lax.optimization_barrier((packed, ghalos))
-    summed, grad_field = all_sum(packed, grad_field, lat, lon, n_lat, n_lon)
+    packet = jnp.concatenate([x, dk], axis=0)
+    for group in reversed(groups[1:]):
+        beside = grad_field if group is groups[1] else None
+        pieces, beside = gather_stage(packet, group, n_lat, n_lon, beside)
+        grad_field = grad_field if beside is None else beside
+        packet = join(pieces)
+    pieces, _ = gather_stage(packet, groups[0], n_lat, n_lon)
     factor = float(1.0 / np.sqrt(np.float32(nrows * n_lat * ncols * n_lon)))
     gin, gout, gk, gg = pl.pallas_call(
-        lambda *refs: unpack_kernel(width, hidden, factor, per, *refs),
+        lambda *refs: unpack_kernel(width, hidden, factor, per, half, *refs),
         out_shape=(s((width, hidden), F32), s((width, hidden), F32), s((49, width), F32), s((1, width), F32)),
-        in_specs=[SM, VM],
+        in_specs=[SM, VM, VM],
         out_specs=(VM,) * 4,
-        compiler_params=params(8),
+        compiler_params=params(),
         name="unpack",
-        cost_estimate=cost(4),
-    )(sc, summed)
+        cost_estimate=cost(3),
+    )(sc, pieces[0], pieces[1])
     return out.transpose(2, 1, 0), grad_field.transpose(2, 1, 0), gin, gout.T, gk, gg.reshape(width)
 
 

time: 141 us -> 137 us (0.972)
  Pallas kernels: 43.5 us -> 60 us
  waiting for transfers between devices: 34.8 us -> 23.5 us
  local copies, waits for them, and re-layouts: 15.1 us -> 9.84 us
  starting transfers between devices: 41.9 us -> 39.9 us
  other arithmetic: 3.91 us -> 2.39 us
    ppermute x18 -> x14, waiting for transfers between devices: 34.4 us -> 18.6 us  [the longest x7 10.2 us: scatter_stage(): got.append(lax.ppermute(piece, AXES, swaps(n_lat, n_lon, masks[d])))]
    pallas_call x3 -> x8, Pallas kernels: 15.3 us -> 29.6 us  [the longest x1 12.2 us: body(): pl.pallas_call(lambda *refs: taps_kernel(nf, *refs), out_shape=s((LT * DK...]
    unnamed x52 -> x62, local copies, waits for them, and re-layouts: 13.3 us -> 5.09 us
    ppermute x18 -> x14, starting transfers between devices: 30.1 us -> 22.1 us  [the longest x7 14.2 us: scatter_stage(): got.append(lax.ppermute(piece, AXES, swaps(n_lat, n_lon, masks[d])))]
    ppermute x2, waiting for transfers between devices: 0.01 us -> 4.9 us  [halo(): s1 = lax.ppermute(q1, AXES, lon1)]
    ppermute x2, starting transfers between devices: 0.01 us -> 4.78 us  [halo(): s1 = lax.ppermute(q1, AXES, lon1)]
    convert_element_type x2 -> x3, other arithmetic: 2.55 us -> 0.35 us  [scatter_stage(): return (total.astype(BF16), beside)]
    ppermute x2, starting transfers between devices: 2.5 us -> 0.55 us  [halo(): r1 = lax.ppermute(p1, AXES, lat1)]
  transfers between devices with their start and end apart: 28 -> 28, of which waited for: 15 -> 9; matrix products, arithmetic and copies ran while one was open for 0% -> 3% of each run, Pallas kernels for 14% -> 20%
where the time goes in v3:
time: 137 us
  Pallas kernels  60 us (44%)
  starting transfers between devices  39.9 us (29%)
  waiting for transfers between devices  23.5 us (17%)
  local copies, waits for them, and re-layouts  9.84 us (7%)
  other arithmetic  2.39 us (2%)
    pallas_call x1, Pallas kernels, body(): pl.pallas_call(lambda *refs: block_kernel(width, nf, *refs), out_shape=(s...  19.8 us
    ppermute x7, starting transfers between devices, scatter_stage(): got.append(lax.ppermute(piece, AXES, swaps(n_lat, n_lon, masks[d])))  14.2 us
    pallas_call x1, Pallas kernels, body(): pl.pallas_call(lambda *refs: taps_kernel(nf, *refs), out_shape=s((LT * DK...  12.2 us
    pallas_call x1, Pallas kernels, body(): pl.pallas_call(lambda *refs: field_kernel(width, nf, *refs), out_shape=s(...  10.7 us
    ppermute x7, waiting for transfers between devices, scatter_stage(): got.append(lax.ppermute(piece, AXES, swaps(n_lat, n_lon, masks[d])))  10.2 us
    ppermute x7, waiting for transfers between devices, gather_stage(): lax.ppermute(packet, AXES, swaps(n_lat, n_lon, masks[d]))  8.45 us
    ppermute x7, starting transfers between devices, gather_stage(): lax.ppermute(packet, AXES, swaps(n_lat, n_lon, masks[d]))  7.94 us
    ppermute x2, starting transfers between devices, halo(): s2 = lax.ppermute(q2, AXES, lon2)  7.15 us
  transfers between devices with their start and end apart: 28, of which 9 were waited for; matrix products, arithmetic and copies ran while one was open for 3% of the time, Pallas kernels for 20%

profile of v3, /device:TPU:0, one launch (start us, length us, event | category | flops | bytes accessed | tf_op | source)
XLA Modules:
  0.0 136.8 jit_solution(10651503775760264415)
XLA Ops:
  1.3 3.7 %prepare.1 = (f32[3,1024,128]{2,1,0:T(8,128)}, bf16[3,8,384]{2,1,0:T(8,128)(2,1)}, bf16[3,8,384]{2,1,0:T(8,128)(2,1)}, bf16[3,416,128]{2,1,0:T(8,128)(2,1)}, bf16[3,416,128]{2,1,0:T(8,128)(2,1)}) custom-call(s32[8]{0:T(128)} %stack.53.sc.refs_0_, s32[8,128]{1,0:T(8,128)} %bitcast.58, bf16[300,8,128]{2,1,0:T(8,128)(2,1)} %bitcast.48), custom_call_target="tpu_custom_call" | custom-call | flops 3000000 | bytes 6000000 | tf_op jit(solution)/shard_map/prepare/pallas_call | solution.py:573
  6.2 3.4 %back.1.refs_9_ = bf16[1024,384]{1,0:T(8,128)(2,1)} custom-call(s32[8,128]{1,0:T(8,128)} %bitcast.59, bf16[300,8,128]{2,1,0:T(8,128)(2,1)} %bitcast.46), custom_call_target="tpu_custom_call" | custom-call | flops 3000000 | bytes 6000000 | tf_op jit(solution)/shard_map/back/pallas_call | solution.py:583
  10.1 1.4 %corners.2 = (bf16[3,416,128]{2,1,0:T(8,128)(2,1)}, bf16[3,416,128]{2,1,0:T(8,128)(2,1)}) custom-call(s32[8]{0:T(128)} %stack.53.sc.refs_0_, bf16[3,8,384]{2,1,0:T(8,128)(2,1)} %copy-done.15, bf16[3,8,384]{2,1,0:T(8,128)(2,1)} %copy-done.10, bf16[3,416,128]{2,1,0:T(8,128)(2,1)} %get-tuple-element.57._, ...), custom_call_target="tpu_custom_call", output_to_operand_aliasing={{0}: (3, {}), {1}: (4, {})} | custom-call | flops 1000000 | bytes 2000000 | tf_op jit(solution)/shard_map/corners/pallas_call | solution.py:601
  11.5 2.7 %collective-permute-start.2 = (bf16[3,416,128]{2,1,0:T(8,128)(2,1)}, bf16[3,416,128]{2,1,0:T(8,128)(2,1)S(1)}, u32[]{:S(2)}, u32[]{:S(2)}) collective-permute-start(bf16[3,416,128]{2,1,0:T(8,128)(2,1)} %get-tuple-element.59), channel_id=1, source_target_pairs={{0,1},{1,0},{2,3},{3,2},{4,5},{5,4},{6,7},{7,6},{8,9},{9,8},{10,11... | collective-permute-start | bytes 958472 | tf_op jit(solution)/shard_map/ppermute | solution.py:616
  14.2 3.6 %collective-permute-start.3 = (bf16[3,416,128]{2,1,0:T(8,128)(2,1)}, bf16[3,416,128]{2,1,0:T(8,128)(2,1)S(1)}, u32[]{:S(2)}, u32[]{:S(2)}) collective-permute-start(bf16[3,416,128]{2,1,0:T(8,128)(2,1)} %get-tuple-element.60), channel_id=1, source_target_pairs={{0,7},{1,2},{2,1},{3,4},{4,3},{5,6},{6,5},{7,0},{8,15},{9,10},{10,... | collective-permute-start | bytes 958472 | tf_op jit(solution)/shard_map/ppermute | solution.py:617
  23.3 4.9 %collective-permute-done.2.refs_10_.refs_5_ = bf16[3,416,128]{2,1,0:T(8,128)(2,1)S(1)} collective-permute-done((bf16[3,416,128]{2,1,0:T(8,128)(2,1)}, bf16[3,416,128]{2,1,0:T(8,128)(2,1)S(1)}, u32[]{:S(2)}, u32[]{:S(2)}) %collective-permute-start.2) | collective-permute-done | bytes 319520 | tf_op jit(solution)/shard_map/ppermute | solution.py:616
  29.0 19.8 %block.1 = (bf16[300,8,128]{2,1,0:T(8,128)(2,1)}, f32[3,1024,128]{2,1,0:T(8,128)}, bf16[3,8,384]{2,1,0:T(8,128)(2,1)}, bf16[3,8,384]{2,1,0:T(8,128)(2,1)}, bf16[...) custom-call(s32[8]{0:T(128)} %stack.53.sc.refs_0_, ...), custom_call_target="tpu_custom_call" | custom-call | flops 18000000 | bytes 36000000 | tf_op jit(solution)/shard_map/block/pallas_call | solution.py:626
  48.8 1.4 %dynamic-slice_bitcast_fusion = bf16[192,16,128]{2,1,0:T(8,128)(2,1)S(1)} fusion(bf16[2,192,16,128]{3,2,1,0:T(8,128)(2,1)} %bitcast.50, s32[]{:T(128)S(6)} %select_n.49), kind=kLoop, calls=%fused_computation.2 | loop fusion | bytes 1572868 | tf_op jit(solution)/shard_map/jit(dynamic_index_in_dim)/squeeze | solution.py:498
  50.2 1.4 %collective-permute-start.9 = (bf16[192,16,128]{2,1,0:T(8,128)(2,1)S(1)}, bf16[192,16,128]{2,1,0:T(8,128)(2,1)S(1)}, u32[]{:S(2)}, u32[]{:S(2)}) collective-permute-start(bf16[192,16,128]{2,1,0:T(8,128)(2,1)S(1)} %dynamic-slice_bitcast_fusion), channel_id=1, source_target_pairs={{0,8},{1,9},{2,10},{3,11},{4,12},{5,13},{6,14},{7,15},{8,0},{9,1},... | collective-permute-start | bytes 2359304 | tf_op jit(solution)/shard_map/ppermute | solution.py:499
  52.4 1.2 collective-permute-done.9
  55.9 1.4 %corners.3 = (bf16[3,416,128]{2,1,0:T(8,128)(2,1)}, bf16[3,416,128]{2,1,0:T(8,128)(2,1)}) custom-call(s32[8]{0:T(128)} %stack.53.sc.refs_0_, bf16[3,8,384]{2,1,0:T(8,128)(2,1)} %copy-done.24, bf16[3,8,384]{2,1,0:T(8,128)(2,1)} %copy-done.16, bf16[3,416,128]{2,1,0:T(8,128)(2,1)} %get-tuple-element.72._, ...), custom_call_target="tpu_custom_call", output_to_operand_aliasing={{0}: (3, {}), {1}: (4, {})} | custom-call | flops 1000000 | bytes 2000000 | tf_op jit(solution)/shard_map/corners/pallas_call | solution.py:601
  57.3 2.1 %collective-permute-start.13 = (bf16[3,416,128]{2,1,0:T(8,128)(2,1)}, bf16[3,416,128]{2,1,0:T(8,128)(2,1)S(1)}, u32[]{:S(2)}, u32[]{:S(2)}) collective-permute-start(bf16[3,416,128]{2,1,0:T(8,128)(2,1)} %get-tuple-element.74), channel_id=1, source_target_pairs={{0,1},{1,0},{2,3},{3,2},{4,5},{5,4},{6,7},{7,6},{8,9},{9,8},{10,11... | collective-permute-start | bytes 958472 | tf_op jit(solution)/shard_map/ppermute | solution.py:616
  59.4 3.6 %collective-permute-start.14 = (bf16[3,416,128]{2,1,0:T(8,128)(2,1)}, bf16[3,416,128]{2,1,0:T(8,128)(2,1)S(1)}, u32[]{:S(2)}, u32[]{:S(2)}) collective-permute-start(bf16[3,416,128]{2,1,0:T(8,128)(2,1)} %get-tuple-element.75), channel_id=1, source_target_pairs={{0,7},{1,2},{2,1},{3,4},{4,3},{5,6},{6,5},{7,0},{8,15},{9,10},{10,... | collective-permute-start | bytes 958472 | tf_op jit(solution)/shard_map/ppermute | solution.py:617
  63.1 6.7 %collective-permute-start.11 = (bf16[48,16,128]{2,1,0:T(8,128)(2,1)S(1)}, bf16[48,16,128]{2,1,0:T(8,128)(2,1)S(1)}, u32[]{:S(2)}, u32[]{:S(2)}) collective-permute-start(bf16[48,16,128]{2,1,0:T(8,128)(2,1)S(1)} %get-tuple-element.97), channel_id=1, source_target_pairs={{0,16},{1,17},{2,18},{3,19},{4,20},{5,21},{6,22},{7,23},{8,24},{9,... | collective-permute-start | bytes 589832 | tf_op jit(solution)/shard_map/ppermute | solution.py:499
  69.9 1.5 %collective-permute-start.12 = (bf16[48,16,128]{2,1,0:T(8,128)(2,1)S(1)}, bf16[48,16,128]{2,1,0:T(8,128)(2,1)S(1)}, u32[]{:S(2)}, u32[]{:S(2)}) collective-permute-start(bf16[48,16,128]{2,1,0:T(8,128)(2,1)S(1)} %get-tuple-element.96), channel_id=1, source_target_pairs={{0,17},{1,16},{2,19},{3,18},{4,21},{5,20},{6,23},{7,22},{8,25},{9,... | collective-permute-start | bytes 589832 | tf_op jit(solution)/shard_map/ppermute | solution.py:499
  71.3 12.2 %taps.1 = bf16[12,16,128]{2,1,0:T(8,128)(2,1)} custom-call(s32[8]{0:T(128)} %stack.53.sc.refs_0_, s32[64]{0:T(128)} %refs_1_.5, f32[3,1024,128]{2,1,0:T(8,128)} %get-tuple-element.51.refs_5_.refs_2_, f32[3,1024,128]{2,1,0:T(8,128)} %get-tuple-element.68.refs_3_.refs_5_, f32[8,384]{1,0:T(8,128)} %get-tuple-element.69.refs_4_, bf16[3,416,128]{2,1,0:T(8,128)(2,1)} %copy-done.1, ...), custom_call_target="tpu_custom_call" | custom-call | flops 1000000 | bytes 2000000 | tf_op jit(solution)/shard_map/taps/pallas_call | solution.py:665
  83.7 3.5 %collective-permute-done.12 = bf16[48,16,128]{2,1,0:T(8,128)(2,1)S(1)} collective-permute-done((bf16[48,16,128]{2,1,0:T(8,128)(2,1)S(1)}, bf16[48,16,128]{2,1,0:T(8,128)(2,1)S(1)}, u32[]{:S(2)}, u32[]{:S(2)}) %collective-permute-start.12) | collective-permute-done | bytes 196640 | tf_op jit(solution)/shard_map/ppermute | solution.py:499
  87.3 2.8 %collective-permute-start.18 = (bf16[12,16,128]{2,1,0:T(8,128)(2,1)S(1)}, bf16[12,16,128]{2,1,0:T(8,128)(2,1)S(1)}, u32[]{:S(2)}, u32[]{:S(2)}) collective-permute-start(bf16[12,16,128]{2,1,0:T(8,128)(2,1)S(1)} %get-tuple-element.99), channel_id=1, source_target_pairs={{0,4},{1,5},{2,6},{3,7},{4,0},{5,1},{6,2},{7,3},{8,12},{9,13},{10,... | collective-permute-start | bytes 147464 | tf_op jit(solution)/shard_map/ppermute | solution.py:499
  90.1 1.3 collective-permute-start.19
  92.4 1.8 %collective-permute-done.19 = bf16[12,16,128]{2,1,0:T(8,128)(2,1)S(1)} collective-permute-done((bf16[12,16,128]{2,1,0:T(8,128)(2,1)S(1)}, bf16[12,16,128]{2,1,0:T(8,128)(2,1)S(1)}, u32[]{:S(2)}, u32[]{:S(2)}) %collective-permute-start.19) | collective-permute-done | bytes 49184 | tf_op jit(solution)/shard_map/ppermute | solution.py:499
  94.2 3.1 %collective-permute-done.20 = bf16[12,16,128]{2,1,0:T(8,128)(2,1)S(1)} collective-permute-done((bf16[12,16,128]{2,1,0:T(8,128)(2,1)S(1)}, bf16[12,16,128]{2,1,0:T(8,128)(2,1)S(1)}, u32[]{:S(2)}, u32[]{:S(2)}) %collective-permute-start.20) | collective-permute-done | bytes 49184 | tf_op jit(solution)/shard_map/ppermute | solution.py:499
  98.0 1.1 collective-permute-start.22
  99.1 2.7 %collective-permute-start.23 = (bf16[24,16,128]{2,1,0:T(8,128)(2,1)S(1)}, bf16[24,16,128]{2,1,0:T(8,128)(2,1)S(1)}, u32[]{:S(2)}, u32[]{:S(2)}) collective-permute-start(bf16[24,16,128]{2,1,0:T(8,128)(2,1)S(1)} %pad_maximum_fusion.refs_0_), channel_id=1, source_target_pairs={{0,6},{1,7},{2,4},{3,5},{4,2},{5,3},{6,0},{7,1},{8,14},{9,15},{10,... | collective-permute-start | bytes 294920 | tf_op jit(solution)/shard_map/ppermute | solution.py:521
  101.8 2.8 %collective-permute-done.21.refs_1_ = bf16[24,16,128]{2,1,0:T(8,128)(2,1)S(1)} collective-permute-done((bf16[24,16,128]{2,1,0:T(8,128)(2,1)S(1)}, bf16[24,16,128]{2,1,0:T(8,128)(2,1)S(1)}, u32[]{:S(2)}, u32[]{:S(2)}) %collective-permute-start.21) | collective-permute-done | bytes 98336 | tf_op jit(solution)/shard_map/ppermute | solution.py:521
  104.6 3.1 %collective-permute-done.22.refs_2_ = bf16[24,16,128]{2,1,0:T(8,128)(2,1)S(1)} collective-permute-done((bf16[24,16,128]{2,1,0:T(8,128)(2,1)S(1)}, bf16[24,16,128]{2,1,0:T(8,128)(2,1)S(1)}, u32[]{:S(2)}, u32[]{:S(2)}) %collective-permute-start.22) | collective-permute-done | bytes 98336 | tf_op jit(solution)/shard_map/ppermute | solution.py:521
  109.0 1.8 %join.2.refs_0_ = bf16[60,16,128]{2,1,0:T(8,128)(2,1)} custom-call(bf16[24,16,128]{2,1,0:T(8,128)(2,1)} %copy-done.6, bf16[24,16,128]{2,1,0:T(8,128)(2,1)} %copy-done.21, bf16[24,16,128]{2,1,0:T(8,128)(2,1)} %copy-done.22, bf16[24,16,128]{2,1,0:T(8,128)(2,1)} %copy-done.23), custom_call_target="tpu_custom_call" | custom-call | flops 1000000 | bytes 2000000 | tf_op jit(solution)/shard_map/join/pallas_call | solution.py:529
  110.8 3.5 %collective-permute-start.26 = (bf16[60,16,128]{2,1,0:T(8,128)(2,1)}, bf16[60,16,128]{2,1,0:T(8,128)(2,1)S(1)}, u32[]{:S(2)}, u32[]{:S(2)}) collective-permute-start(bf16[60,16,128]{2,1,0:T(8,128)(2,1)} %join.2.refs_0_), channel_id=1, source_target_pairs={{0,17},{1,16},{2,19},{3,18},{4,21},{5,20},{6,23},{7,22},{8,25},{9,... | collective-permute-start | bytes 737288 | tf_op jit(solution)/shard_map/ppermute | solution.py:521
  114.2 10.7 %field.1 = bf16[300,8,128]{2,1,0:T(8,128)(2,1)} custom-call(s32[8]{0:T(128)} %stack.53.sc.refs_0_, s32[64]{0:T(128)} %refs_1_.5, f32[49,300]{1,0:T(8,128)} %refs_2_.3, s32[8,128]{1,0:T(8,128)} %bitcast.61, bf16[300,8,128]{2,1,0:T(8,128)(2,1)} %bitcast.47, f32[3,1024,128]{2,1,0:T(8,128)} %get-tuple-element.68.refs_3_.refs_5_, bf16[3,416,128]{2,1,0:T(8,128)(2,1)} %copy-done.8, ...), custom_call_target="tpu_custom_call" | custom-call | flops 10000000 | bytes 20000000 | tf_op jit(solution)/shard_map/field/pallas_call | solution.py:681
  126.4 2.3 %join.3.refs_1_ = bf16[204,16,128]{2,1,0:T(8,128)(2,1)} custom-call(bf16[60,16,128]{2,1,0:T(8,128)(2,1)} %join.2.refs_0_, bf16[60,16,128]{2,1,0:T(8,128)(2,1)} %copy-done.11, bf16[60,16,128]{2,1,0:T(8,128)(2,1)} %copy-done.12, bf16[60,16,128]{2,1,0:T(8,128)(2,1)} %copy-done.13), custom_call_target="tpu_custom_call" | custom-call | flops 1000000 | bytes 2000000 | tf_op jit(solution)/shard_map/join/pallas_call | solution.py:529
  128.7 2.6 %collective-permute-done.27.refs_2_ = bf16[204,16,128]{2,1,0:T(8,128)(2,1)S(1)} collective-permute-done((bf16[204,16,128]{2,1,0:T(8,128)(2,1)}, bf16[204,16,128]{2,1,0:T(8,128)(2,1)S(1)}, u32[]{:S(2)}, u32[]{:S(2)}) %collective-permute-start.27) | collective-permute-done | bytes 835616 | tf_op jit(solution)/shard_map/ppermute | solution.py:521
  132.1 3.3 %unpack.1 = (f32[300,1200]{1,0:T(8,128)}, f32[300,1200]{1,0:T(8,128)}, f32[49,300]{1,0:T(8,128)}, f32[1,300]{1,0:T(1,128)}) custom-call(s32[8]{0:T(128)} %stack.53.sc.refs_0_, bf16[204,16,128]{2,1,0:T(8,128)(2,1)} %join.3.refs_1_, bf16[204,16,128]{2,1,0:T(8,128)(2,1)} %copy-done.3), custom_call_target="tpu_custom_call" | custom-call | flops 3000000 | bytes 6000000 | tf_op jit(solution)/shard_map/unpack/pallas_call | solution.py:699
  135.5 1.3 reduce
  (111 shorter events, 17.2 us)
Async XLA Ops:
  5.1 4.5 %collective-permute-start = (bf16[3,8,384]{2,1,0:T(8,128)(2,1)}, bf16[3,8,384]{2,1,0:T(8,128)(2,1)S(1)}, u32[]{:S(2)}, u32[]{:S(2)}) collective-permute-start(bf16[3,8,384]{2,1,0:T(8,128)(2,1)} %get-tuple-element.52), channel_id=1, source_target_pairs={{0,8},{1,9},{2,10},{3,11},{4,12},{5,13},{6,14},{7,15},{8,0},{9,1},... | collective-permute-start | bytes 55304 | tf_op jit(solution)/shard_map/ppermute | solution.py:598
  5.5 4.0 %collective-permute-start.1 = (bf16[3,8,384]{2,1,0:T(8,128)(2,1)}, bf16[3,8,384]{2,1,0:T(8,128)(2,1)S(1)}, u32[]{:S(2)}, u32[]{:S(2)}) collective-permute-start(bf16[3,8,384]{2,1,0:T(8,128)(2,1)} %get-tuple-element.53), channel_id=1, source_target_pairs={{8,16},{9,17},{10,18},{11,19},{12,20},{13,21},{14,22},{15,23},{16,... | collective-permute-start | bytes 55304 | tf_op jit(solution)/shard_map/ppermute | solution.py:599
  11.5 16.6 %collective-permute-start.2 = (bf16[3,416,128]{2,1,0:T(8,128)(2,1)}, bf16[3,416,128]{2,1,0:T(8,128)(2,1)S(1)}, u32[]{:S(2)}, u32[]{:S(2)}) collective-permute-start(bf16[3,416,128]{2,1,0:T(8,128)(2,1)} %get-tuple-element.59), channel_id=1, source_target_pairs={{0,1},{1,0},{2,3},{3,2},{4,5},{5,4},{6,7},{7,6},{8,9},{9,8},{10,11... | collective-permute-start | bytes 958472 | tf_op jit(solution)/shard_map/ppermute | solution.py:616
  14.2 13.9 %collective-permute-start.3 = (bf16[3,416,128]{2,1,0:T(8,128)(2,1)}, bf16[3,416,128]{2,1,0:T(8,128)(2,1)S(1)}, u32[]{:S(2)}, u32[]{:S(2)}) collective-permute-start(bf16[3,416,128]{2,1,0:T(8,128)(2,1)} %get-tuple-element.60), channel_id=1, source_target_pairs={{0,7},{1,2},{2,1},{3,4},{4,3},{5,6},{6,5},{7,0},{8,15},{9,10},{10,... | collective-permute-start | bytes 958472 | tf_op jit(solution)/shard_map/ppermute | solution.py:617
  18.6 4.7 %collective-permute-start.4 = (bf16[2,3,8,384]{3,2,1,0:T(8,128)(2,1)S(1)}, bf16[2,3,8,384]{3,2,1,0:T(8,128)(2,1)S(1)}, u32[]{:S(2)}, u32[]{:S(2)}) collective-permute-start(bf16[2,3,8,384]{3,2,1,0:T(8,128)(2,1)S(1)} %pad_maximum_fusion.1.refs_14_.refs_9_), channel_id=1, source_target_pairs={{24,26},{25,27},{26,24},{27,25},{28,30},{29,31},{30,28},{31,29}} | collective-permute-start | bytes 110600 | tf_op jit(solution)/shard_map/ppermute | solution.py:458
  19.2 4.0 %collective-permute-start.5 = (bf16[2,3,8,384]{3,2,1,0:T(8,128)(2,1)S(1)}, bf16[2,3,8,384]{3,2,1,0:T(8,128)(2,1)S(1)}, u32[]{:S(2)}, u32[]{:S(2)}) collective-permute-start(bf16[2,3,8,384]{3,2,1,0:T(8,128)(2,1)S(1)} %pad_maximum_fusion.1.refs_14_.refs_9_), channel_id=1, source_target_pairs={{24,28},{25,29},{26,30},{27,31},{28,24},{29,25},{30,26},{31,27}} | collective-permute-start | bytes 110600 | tf_op jit(solution)/shard_map/ppermute | solution.py:458
  19.9 3.3 %collective-permute-start.6 = (bf16[2,3,8,384]{3,2,1,0:T(8,128)(2,1)S(1)}, bf16[2,3,8,384]{3,2,1,0:T(8,128)(2,1)S(1)}, u32[]{:S(2)}, u32[]{:S(2)}) collective-permute-start(bf16[2,3,8,384]{3,2,1,0:T(8,128)(2,1)S(1)} %pad_maximum_fusion.1.refs_14_.refs_9_), channel_id=1, source_target_pairs={{24,30},{25,31},{26,28},{27,29},{28,26},{29,27},{30,24},{31,25}} | collective-permute-start | bytes 110600 | tf_op jit(solution)/shard_map/ppermute | solution.py:458
  50.2 3.4 %collective-permute-start.9 = (bf16[192,16,128]{2,1,0:T(8,128)(2,1)S(1)}, bf16[192,16,128]{2,1,0:T(8,128)(2,1)S(1)}, u32[]{:S(2)}, u32[]{:S(2)}) collective-permute-start(bf16[192,16,128]{2,1,0:T(8,128)(2,1)S(1)} %dynamic-slice_bitcast_fusion), channel_id=1, source_target_pairs={{0,8},{1,9},{2,10},{3,11},{4,12},{5,13},{6,14},{7,15},{8,0},{9,1},... | collective-permute-start | bytes 2359304 | tf_op jit(solution)/shard_map/ppermute | solution.py:499
  51.6 2.2 %collective-permute-start.7 = (bf16[3,8,384]{2,1,0:T(8,128)(2,1)}, bf16[3,8,384]{2,1,0:T(8,128)(2,1)S(1)}, u32[]{:S(2)}, u32[]{:S(2)}) collective-permute-start(bf16[3,8,384]{2,1,0:T(8,128)(2,1)} %get-tuple-element.62), channel_id=1, source_target_pairs={{0,8},{1,9},{2,10},{3,11},{4,12},{5,13},{6,14},{7,15},{8,0},{9,1},... | collective-permute-start | bytes 55304 | tf_op jit(solution)/shard_map/ppermute | solution.py:598
  51.7 2.1 %collective-permute-start.8 = (bf16[3,8,384]{2,1,0:T(8,128)(2,1)S(1)}, bf16[3,8,384]{2,1,0:T(8,128)(2,1)S(1)}, u32[]{:S(2)}, u32[]{:S(2)}) collective-permute-start(bf16[3,8,384]{2,1,0:T(8,128)(2,1)S(1)} %copy-done.28), channel_id=1, source_target_pairs={{8,16},{9,17},{10,18},{11,19},{12,20},{13,21},{14,22},{15,23},{16,... | collective-permute-start | bytes 55304 | tf_op jit(solution)/shard_map/ppermute | solution.py:599
  53.8 29.8 %copy-start.20 = (bf16[2,3,8,384]{3,2,1,0:T(8,128)(2,1)}, bf16[2,3,8,384]{3,2,1,0:T(8,128)(2,1)S(1)}, u32[]{:S(2)}) copy-start(bf16[2,3,8,384]{3,2,1,0:T(8,128)(2,1)S(1)} %pad_maximum_fusion.2.refs_10_) | copy-start | bytes 110596
  53.8 9.2 %collective-permute-start.15 = (bf16[2,3,8,384]{3,2,1,0:T(8,128)(2,1)S(1)}, bf16[2,3,8,384]{3,2,1,0:T(8,128)(2,1)S(1)}, u32[]{:S(2)}, u32[]{:S(2)}) collective-permute-start(bf16[2,3,8,384]{3,2,1,0:T(8,128)(2,1)S(1)} %pad_maximum_fusion.2.refs_10_), channel_id=1, source_target_pairs={{24,26},{25,27},{26,24},{27,25},{28,30},{29,31},{30,28},{31,29}} | collective-permute-start | bytes 110600 | tf_op jit(solution)/shard_map/ppermute | solution.py:458
  54.5 8.6 %collective-permute-start.16 = (bf16[2,3,8,384]{3,2,1,0:T(8,128)(2,1)S(1)}, bf16[2,3,8,384]{3,2,1,0:T(8,128)(2,1)S(1)}, u32[]{:S(2)}, u32[]{:S(2)}) collective-permute-start(bf16[2,3,8,384]{3,2,1,0:T(8,128)(2,1)S(1)} %pad_maximum_fusion.2.refs_10_), channel_id=1, source_target_pairs={{24,28},{25,29},{26,30},{27,31},{28,24},{29,25},{30,26},{31,27}} | collective-permute-start | bytes 110600 | tf_op jit(solution)/shard_map/ppermute | solution.py:458
  55.2 14.7 %collective-permute-start.17 = (bf16[2,3,8,384]{3,2,1,0:T(8,128)(2,1)S(1)}, bf16[2,3,8,384]{3,2,1,0:T(8,128)(2,1)S(1)}, u32[]{:S(2)}, u32[]{:S(2)}) collective-permute-start(bf16[2,3,8,384]{3,2,1,0:T(8,128)(2,1)S(1)} %pad_maximum_fusion.2.refs_10_), channel_id=1, source_target_pairs={{24,30},{25,31},{26,28},{27,29},{28,26},{29,27},{30,24},{31,25}} | collective-permute-start | bytes 110600 | tf_op jit(solution)/shard_map/ppermute | solution.py:458
  57.3 29.9 %collective-permute-start.13 = (bf16[3,416,128]{2,1,0:T(8,128)(2,1)}, bf16[3,416,128]{2,1,0:T(8,128)(2,1)S(1)}, u32[]{:S(2)}, u32[]{:S(2)}) collective-permute-start(bf16[3,416,128]{2,1,0:T(8,128)(2,1)} %get-tuple-element.74), channel_id=1, source_target_pairs={{0,1},{1,0},{2,3},{3,2},{4,5},{5,4},{6,7},{7,6},{8,9},{9,8},{10,11... | collective-permute-start | bytes 958472 | tf_op jit(solution)/shard_map/ppermute | solution.py:616
  59.4 27.8 %collective-permute-start.14 = (bf16[3,416,128]{2,1,0:T(8,128)(2,1)}, bf16[3,416,128]{2,1,0:T(8,128)(2,1)S(1)}, u32[]{:S(2)}, u32[]{:S(2)}) collective-permute-start(bf16[3,416,128]{2,1,0:T(8,128)(2,1)} %get-tuple-element.75), channel_id=1, source_target_pairs={{0,7},{1,2},{2,1},{3,4},{4,3},{5,6},{6,5},{7,0},{8,15},{9,10},{10,... | collective-permute-start | bytes 958472 | tf_op jit(solution)/shard_map/ppermute | solution.py:617
  63.0 20.6 %copy-start.25 = (bf16[2,3,8,384]{3,2,1,0:T(8,128)(2,1)}, bf16[2,3,8,384]{3,2,1,0:T(8,128)(2,1)S(1)}, u32[]{:S(2)}) copy-start(bf16[2,3,8,384]{3,2,1,0:T(8,128)(2,1)S(1)} %collective-permute-done.15.refs_11_) | copy-start | bytes 110596
  63.1 20.6 %collective-permute-start.10 = (bf16[48,16,128]{2,1,0:T(8,128)(2,1)S(1)}, bf16[48,16,128]{2,1,0:T(8,128)(2,1)S(1)}, u32[]{:S(2)}, u32[]{:S(2)}) collective-permute-start(bf16[48,16,128]{2,1,0:T(8,128)(2,1)S(1)} %get-tuple-element.98), channel_id=1, source_target_pairs={{0,1},{1,0},{2,3},{3,2},{4,5},{5,4},{6,7},{7,6},{8,9},{9,8},{10,11... | collective-permute-start | bytes 589832 | tf_op jit(solution)/shard_map/ppermute | solution.py:499
  63.1 20.5 %collective-permute-start.11 = (bf16[48,16,128]{2,1,0:T(8,128)(2,1)S(1)}, bf16[48,16,128]{2,1,0:T(8,128)(2,1)S(1)}, u32[]{:S(2)}, u32[]{:S(2)}) collective-permute-start(bf16[48,16,128]{2,1,0:T(8,128)(2,1)S(1)} %get-tuple-element.97), channel_id=1, source_target_pairs={{0,16},{1,17},{2,18},{3,19},{4,20},{5,21},{6,22},{7,23},{8,24},{9,... | collective-permute-start | bytes 589832 | tf_op jit(solution)/shard_map/ppermute | solution.py:499
  69.9 17.3 %collective-permute-start.12 = (bf16[48,16,128]{2,1,0:T(8,128)(2,1)S(1)}, bf16[48,16,128]{2,1,0:T(8,128)(2,1)S(1)}, u32[]{:S(2)}, u32[]{:S(2)}) collective-permute-start(bf16[48,16,128]{2,1,0:T(8,128)(2,1)S(1)} %get-tuple-element.96), channel_id=1, source_target_pairs={{0,17},{1,16},{2,19},{3,18},{4,21},{5,20},{6,23},{7,22},{8,25},{9,... | collective-permute-start | bytes 589832 | tf_op jit(solution)/shard_map/ppermute | solution.py:499
  87.2 27.1 %copy-start.8 = (bf16[3,416,128]{2,1,0:T(8,128)(2,1)}, bf16[3,416,128]{2,1,0:T(8,128)(2,1)S(1)}, u32[]{:S(2)}) copy-start(bf16[3,416,128]{2,1,0:T(8,128)(2,1)S(1)} %collective-permute-done.13.refs_6_) | copy-start | bytes 958468
  87.2 27.1 %copy-start.9 = (bf16[3,416,128]{2,1,0:T(8,128)(2,1)}, bf16[3,416,128]{2,1,0:T(8,128)(2,1)S(1)}, u32[]{:S(2)}) copy-start(bf16[3,416,128]{2,1,0:T(8,128)(2,1)S(1)} %collective-permute-done.14.refs_7_) | copy-start | bytes 958468
  87.3 5.1 %collective-permute-start.18 = (bf16[12,16,128]{2,1,0:T(8,128)(2,1)S(1)}, bf16[12,16,128]{2,1,0:T(8,128)(2,1)S(1)}, u32[]{:S(2)}, u32[]{:S(2)}) collective-permute-start(bf16[12,16,128]{2,1,0:T(8,128)(2,1)S(1)} %get-tuple-element.99), channel_id=1, source_target_pairs={{0,4},{1,5},{2,6},{3,7},{4,0},{5,1},{6,2},{7,3},{8,12},{9,13},{10,... | collective-permute-start | bytes 147464 | tf_op jit(solution)/shard_map/ppermute | solution.py:499
  90.1 4.1 %collective-permute-start.19 = (bf16[12,16,128]{2,1,0:T(8,128)(2,1)S(1)}, bf16[12,16,128]{2,1,0:T(8,128)(2,1)S(1)}, u32[]{:S(2)}, u32[]{:S(2)}) collective-permute-start(bf16[12,16,128]{2,1,0:T(8,128)(2,1)S(1)} %get-tuple-element.101), channel_id=1, source_target_pairs={{0,2},{1,3},{2,0},{3,1},{4,6},{5,7},{6,4},{7,5},{8,10},{9,11},{10,... | collective-permute-start | bytes 147464 | tf_op jit(solution)/shard_map/ppermute | solution.py:499
  91.4 5.9 %collective-permute-start.20 = (bf16[12,16,128]{2,1,0:T(8,128)(2,1)S(1)}, bf16[12,16,128]{2,1,0:T(8,128)(2,1)S(1)}, u32[]{:S(2)}, u32[]{:S(2)}) collective-permute-start(bf16[12,16,128]{2,1,0:T(8,128)(2,1)S(1)} %get-tuple-element.100), channel_id=1, source_target_pairs={{0,6},{1,7},{2,4},{3,5},{4,2},{5,3},{6,0},{7,1},{8,14},{9,15},{10,... | collective-permute-start | bytes 147464 | tf_op jit(solution)/shard_map/ppermute | solution.py:499
  97.4 7.2 %collective-permute-start.21 = (bf16[24,16,128]{2,1,0:T(8,128)(2,1)S(1)}, bf16[24,16,128]{2,1,0:T(8,128)(2,1)S(1)}, u32[]{:S(2)}, u32[]{:S(2)}) collective-permute-start(bf16[24,16,128]{2,1,0:T(8,128)(2,1)S(1)} %pad_maximum_fusion.refs_0_), channel_id=1, source_target_pairs={{0,4},{1,5},{2,6},{3,7},{4,0},{5,1},{6,2},{7,3},{8,12},{9,13},{10,... | collective-permute-start | bytes 294920 | tf_op jit(solution)/shard_map/ppermute | solution.py:521
  98.0 9.6 %collective-permute-start.22 = (bf16[24,16,128]{2,1,0:T(8,128)(2,1)S(1)}, bf16[24,16,128]{2,1,0:T(8,128)(2,1)S(1)}, u32[]{:S(2)}, u32[]{:S(2)}) collective-permute-start(bf16[24,16,128]{2,1,0:T(8,128)(2,1)S(1)} %pad_maximum_fusion.refs_0_), channel_id=1, source_target_pairs={{0,2},{1,3},{2,0},{3,1},{4,6},{5,7},{6,4},{7,5},{8,10},{9,11},{10,... | collective-permute-start | bytes 294920 | tf_op jit(solution)/shard_map/ppermute | solution.py:521
  99.1 8.6 %collective-permute-start.23 = (bf16[24,16,128]{2,1,0:T(8,128)(2,1)S(1)}, bf16[24,16,128]{2,1,0:T(8,128)(2,1)S(1)}, u32[]{:S(2)}, u32[]{:S(2)}) collective-permute-start(bf16[24,16,128]{2,1,0:T(8,128)(2,1)S(1)} %pad_maximum_fusion.refs_0_), channel_id=1, source_target_pairs={{0,6},{1,7},{2,4},{3,5},{4,2},{5,3},{6,0},{7,1},{8,14},{9,15},{10,... | collective-permute-start | bytes 294920 | tf_op jit(solution)/shard_map/ppermute | solution.py:521
  110.7 14.1 %collective-permute-start.24 = (bf16[60,16,128]{2,1,0:T(8,128)(2,1)}, bf16[60,16,128]{2,1,0:T(8,128)(2,1)S(1)}, u32[]{:S(2)}, u32[]{:S(2)}) collective-permute-start(bf16[60,16,128]{2,1,0:T(8,128)(2,1)} %join.2.refs_0_), channel_id=1, source_target_pairs={{0,1},{1,0},{2,3},{3,2},{4,5},{5,4},{6,7},{7,6},{8,9},{9,8},{10,11... | collective-permute-start | bytes 737288 | tf_op jit(solution)/shard_map/ppermute | solution.py:521
  110.7 14.2 %collective-permute-start.25 = (bf16[60,16,128]{2,1,0:T(8,128)(2,1)}, bf16[60,16,128]{2,1,0:T(8,128)(2,1)S(1)}, u32[]{:S(2)}, u32[]{:S(2)}) collective-permute-start(bf16[60,16,128]{2,1,0:T(8,128)(2,1)} %join.2.refs_0_), channel_id=1, source_target_pairs={{0,16},{1,17},{2,18},{3,19},{4,20},{5,21},{6,22},{7,23},{8,24},{9,... | collective-permute-start | bytes 737288 | tf_op jit(solution)/shard_map/ppermute | solution.py:521
  110.8 14.2 %collective-permute-start.26 = (bf16[60,16,128]{2,1,0:T(8,128)(2,1)}, bf16[60,16,128]{2,1,0:T(8,128)(2,1)S(1)}, u32[]{:S(2)}, u32[]{:S(2)}) collective-permute-start(bf16[60,16,128]{2,1,0:T(8,128)(2,1)} %join.2.refs_0_), channel_id=1, source_target_pairs={{0,17},{1,16},{2,19},{3,18},{4,21},{5,20},{6,23},{7,22},{8,25},{9,... | collective-permute-start | bytes 737288 | tf_op jit(solution)/shard_map/ppermute | solution.py:521
  128.7 2.6 %collective-permute-start.27 = (bf16[204,16,128]{2,1,0:T(8,128)(2,1)}, bf16[204,16,128]{2,1,0:T(8,128)(2,1)S(1)}, u32[]{:S(2)}, u32[]{:S(2)}) collective-permute-start(bf16[204,16,128]{2,1,0:T(8,128)(2,1)} %join.3.refs_1_), channel_id=1, source_target_pairs={{0,8},{1,9},{2,10},{3,11},{4,12},{5,13},{6,14},{7,15},{8,0},{9,1},... | collective-permute-start | bytes 2506760 | tf_op jit(solution)/shard_map/ppermute | solution.py:521
  (27 other events, 146.0 us)

commit v4 on v3

--- a/solution.py
+++ b/solution.py
@@ -415,7 +415,7 @@
             rows = min(16, 49 - 16 * r)
             gk_ref[16 * r : 16 * r + rows, 128 * l : 128 * l + w] = v[:rows, :w]
             if rows < 16:
-                gg_ref[:, 128 * l : 128 * l + w] = v[rows : rows + 1, :w]
+                gg_ref[128 * l : 128 * l + w] = v[rows, :w]
 
 
 def swaps(n_lat, n_lon, bits):
@@ -531,7 +531,7 @@
         out_shape=jax.ShapeDtypeStruct((n * size + DKT, 16, 128), BF16),
         in_specs=[VM] * n,
         out_specs=VM,
-        compiler_params=params(),
+        compiler_params=params(8),
         name="join",
         cost_estimate=cost(1),
     )(*pieces)
@@ -609,7 +609,7 @@
                 pltpu.SemaphoreType.DMA((2,)),
             ],
             input_output_aliases={3: 0, 4: 1},
-            compiler_params=params(),
+            compiler_params=params(4),
             name="corners",
             cost_estimate=cost(1),
         )(sc, r1, r2, q1, q2)
@@ -660,7 +660,7 @@
     )(sc, mirror, kernel, gain, mask_c, mf, win, wout, field_c, bk, *halos)
 
     first, _ = scatter_stage(dw, groups[0], lat, lon, n_lat, n_lon)
-    ghalos, first = halo(q1, q2, g1, g2, first)
+    ghalos, dgain = halo(q1, q2, g1, g2, dgain)
     gc_taps, dgain, _ = lax.optimization_barrier((gc, dgain, first))
     dk = pl.pallas_call(
         lambda *refs: taps_kernel(nf, *refs),
@@ -698,14 +698,14 @@
     factor = float(1.0 / np.sqrt(np.float32(nrows * n_lat * ncols * n_lon)))
     gin, gout, gk, gg = pl.pallas_call(
         lambda *refs: unpack_kernel(width, hidden, factor, per, half, *refs),
-        out_shape=(s((width, hidden), F32), s((width, hidden), F32), s((49, width), F32), s((1, width), F32)),
+        out_shape=(s((width, hidden), F32), s((width, hidden), F32), s((49, width), F32), s((width,), F32)),
         in_specs=[SM, VM, VM],
         out_specs=(VM,) * 4,
-        compiler_params=params(),
+        compiler_params=params(12),
         name="unpack",
         cost_estimate=cost(3),
     )(sc, pieces[0], pieces[1])
-    return out.transpose(2, 1, 0), grad_field.transpose(2, 1, 0), gin, gout.T, gk, gg.reshape(width)
+    return out.transpose(2, 1, 0), grad_field.transpose(2, 1, 0), gin, gout.T, gk, gg
 
 
 def solution(mesh):

time: 137 us -> 126 us (0.920)
  Pallas kernels: 60 us -> 53.6 us
  waiting for transfers between devices: 23.5 us -> 19.3 us
  local copies, waits for them, and re-layouts: 9.84 us -> 6.51 us
  starting transfers between devices: 39.9 us -> 42.2 us
    ppermute x7, waiting for transfers between devices: 10.2 us -> 3.21 us  [scatter_stage(): got.append(lax.ppermute(piece, AXES, swaps(n_lat, n_lon, masks[d])))]
    unnamed x62 -> x56, local copies, waits for them, and re-layouts: 5.09 us -> 0.9 us
    pallas_call x2, Pallas kernels: 4.09 us -> 0.12 us  [join(): pl.pallas_call(packet_kernel, out_shape=jax.ShapeDtypeStruct((n * size +...]
    ppermute x7, starting transfers between devices: 7.94 us -> 9.95 us  [gather_stage(): lax.ppermute(packet, AXES, swaps(n_lat, n_lon, masks[d]))]
    pallas_call x2, Pallas kernels: 2.81 us -> 1.23 us  [halo(): pl.pallas_call(corners_kernel, out_shape=(strip_msg, strip_msg), in_specs...]
  transfers between devices with their start and end apart: 28 -> 28, of which waited for: 9 -> 9; matrix products, arithmetic and copies ran while one was open for 3% -> 4% of each run, Pallas kernels for 20% -> 22%
where the time goes in v4:
time: 126 us; the launch traced here: 125 us
  Pallas kernels  53.6 us (43%)
  starting transfers between devices  42.2 us (33%)
  waiting for transfers between devices  19.3 us (15%)
  local copies, waits for them, and re-layouts  6.51 us (5%)
  other arithmetic  2.25 us (2%)
    pallas_call x1, Pallas kernels, body(): pl.pallas_call(lambda *refs: block_kernel(width, nf, *refs), out_shape=(s...  19.8 us
    ppermute x7, starting transfers between devices, scatter_stage(): got.append(lax.ppermute(piece, AXES, swaps(n_lat, n_lon, masks[d])))  14.5 us
    pallas_call x1, Pallas kernels, body(): pl.pallas_call(lambda *refs: taps_kernel(nf, *refs), out_shape=s((LT * DK...  12.3 us
    pallas_call x1, Pallas kernels, body(): pl.pallas_call(lambda *refs: field_kernel(width, nf, *refs), out_shape=s(...  10.7 us
    ppermute x7, starting transfers between devices, gather_stage(): lax.ppermute(packet, AXES, swaps(n_lat, n_lon, masks[d]))  9.95 us
    ppermute x7, waiting for transfers between devices, gather_stage(): lax.ppermute(packet, AXES, swaps(n_lat, n_lon, masks[d]))  9.43 us
    ppermute x2, starting transfers between devices, halo(): s2 = lax.ppermute(q2, AXES, lon2)  7.15 us
    ppermute x2, waiting for transfers between devices, halo(): s1 = lax.ppermute(q1, AXES, lon1)  5.28 us
  transfers between devices with their start and end apart: 28, of which 9 were waited for; matrix products, arithmetic and copies ran while one was open for 4% of the time, Pallas kernels for 22%

profile of v4, /device:TPU:0, one launch (start us, length us, event | category | flops | bytes accessed | tf_op | source)
XLA Modules:
  0.0 125.0 jit_solution(16757890392035956581)
XLA Ops:
  1.3 3.7 %prepare.1 = (f32[3,1024,128]{2,1,0:T(8,128)}, bf16[3,8,384]{2,1,0:T(8,128)(2,1)}, bf16[3,8,384]{2,1,0:T(8,128)(2,1)}, bf16[3,416,128]{2,1,0:T(8,128)(2,1)}, bf16[3,416,128]{2,1,0:T(8,128)(2,1)}) custom-call(s32[8]{0:T(128)} %stack.53.sc.refs_0_, s32[8,128]{1,0:T(8,128)} %bitcast.58, bf16[300,8,128]{2,1,0:T(8,128)(2,1)} %bitcast.50), custom_call_target="tpu_custom_call" | custom-call | flops 3000000 | bytes 6000000 | tf_op jit(solution)/shard_map/prepare/pallas_call | solution.py:573
  6.2 3.4 %back.1.refs_9_ = bf16[1024,384]{1,0:T(8,128)(2,1)} custom-call(s32[8,128]{1,0:T(8,128)} %bitcast.59, bf16[300,8,128]{2,1,0:T(8,128)(2,1)} %bitcast.48), custom_call_target="tpu_custom_call" | custom-call | flops 3000000 | bytes 6000000 | tf_op jit(solution)/shard_map/back/pallas_call | solution.py:583
  10.2 2.7 %collective-permute-start.2 = (bf16[3,416,128]{2,1,0:T(8,128)(2,1)S(1)}, bf16[3,416,128]{2,1,0:T(8,128)(2,1)S(1)}, u32[]{:S(2)}, u32[]{:S(2)}) collective-permute-start(bf16[3,416,128]{2,1,0:T(8,128)(2,1)S(1)} %get-tuple-element.59), channel_id=1, source_target_pairs={{0,1},{1,0},{2,3},{3,2},{4,5},{5,4},{6,7},{7,6},{8,9},{9,8},{10,11... | collective-permute-start | bytes 958472 | tf_op jit(solution)/shard_map/ppermute | solution.py:616
  12.9 3.6 %collective-permute-start.3 = (bf16[3,416,128]{2,1,0:T(8,128)(2,1)S(1)}, bf16[3,416,128]{2,1,0:T(8,128)(2,1)S(1)}, u32[]{:S(2)}, u32[]{:S(2)}) collective-permute-start(bf16[3,416,128]{2,1,0:T(8,128)(2,1)S(1)} %get-tuple-element.60), channel_id=1, source_target_pairs={{0,7},{1,2},{2,1},{3,4},{4,3},{5,6},{6,5},{7,0},{8,15},{9,10},{10,... | collective-permute-start | bytes 958472 | tf_op jit(solution)/shard_map/ppermute | solution.py:617
  16.5 0.7 collective-permute-start.4
  18.6 1.0 pad.12.refs_6_
  19.6 1.0 pad.13.refs_7_
  21.3 5.3 %collective-permute-done.2.refs_10_.refs_5_ = bf16[3,416,128]{2,1,0:T(8,128)(2,1)S(1)} collective-permute-done((bf16[3,416,128]{2,1,0:T(8,128)(2,1)S(1)}, bf16[3,416,128]{2,1,0:T(8,128)(2,1)S(1)}, u32[]{:S(2)}, u32[]{:S(2)}) %collective-permute-start.2) | collective-permute-done | bytes 319520 | tf_op jit(solution)/shard_map/ppermute | solution.py:616
  26.6 0.7 copy-done.12
  27.3 19.8 %block.1 = (bf16[300,8,128]{2,1,0:T(8,128)(2,1)}, f32[3,1024,128]{2,1,0:T(8,128)}, bf16[3,8,384]{2,1,0:T(8,128)(2,1)}, bf16[3,8,384]{2,1,0:T(8,128)(2,1)}, bf16[...) custom-call(s32[8]{0:T(128)} %stack.53.sc.refs_0_, ...), custom_call_target="tpu_custom_call" | custom-call | flops 18000000 | bytes 36000000 | tf_op jit(solution)/shard_map/block/pallas_call | solution.py:626
  47.2 2.3 %dynamic-slice_bitcast_fusion = bf16[192,16,128]{2,1,0:T(8,128)(2,1)} fusion(bf16[2,192,16,128]{3,2,1,0:T(8,128)(2,1)} %bitcast.52, s32[]{:T(128)S(6)} %select_n.49), kind=kLoop, calls=%fused_computation.2 | loop fusion | bytes 1572868 | tf_op jit(solution)/shard_map/jit(dynamic_index_in_dim)/squeeze | solution.py:498
  49.5 1.5 %collective-permute-start.7 = (bf16[192,16,128]{2,1,0:T(8,128)(2,1)}, bf16[192,16,128]{2,1,0:T(8,128)(2,1)}, u32[]{:S(2)}, u32[]{:S(2)}) collective-permute-start(bf16[192,16,128]{2,1,0:T(8,128)(2,1)} %dynamic-slice_bitcast_fusion), channel_id=1, source_target_pairs={{0,8},{1,9},{2,10},{3,11},{4,12},{5,13},{6,14},{7,15},{8,0},{9,1},... | collective-permute-start | bytes 2359304 | tf_op jit(solution)/shard_map/ppermute | solution.py:499
  51.6 1.3 %collective-permute-done.11.p1_ref.refs_8_ = bf16[3,8,384]{2,1,0:T(8,128)(2,1)S(1)} collective-permute-done((bf16[3,8,384]{2,1,0:T(8,128)(2,1)}, bf16[3,8,384]{2,1,0:T(8,128)(2,1)S(1)}, u32[]{:S(2)}, u32[]{:S(2)}) %collective-permute-start.11) | collective-permute-done | bytes 18464 | tf_op jit(solution)/shard_map/ppermute | solution.py:598
  53.0 0.7 pad_maximum_fusion.2.refs_10_
  56.4 2.1 %collective-permute-start.13 = (bf16[3,416,128]{2,1,0:T(8,128)(2,1)S(1)}, bf16[3,416,128]{2,1,0:T(8,128)(2,1)S(1)}, u32[]{:S(2)}, u32[]{:S(2)}) collective-permute-start(bf16[3,416,128]{2,1,0:T(8,128)(2,1)S(1)} %get-tuple-element.74), channel_id=1, source_target_pairs={{0,1},{1,0},{2,3},{3,2},{4,5},{5,4},{6,7},{7,6},{8,9},{9,8},{10,11... | collective-permute-start | bytes 958472 | tf_op jit(solution)/shard_map/ppermute | solution.py:616
  58.5 3.6 %collective-permute-start.14 = (bf16[3,416,128]{2,1,0:T(8,128)(2,1)S(1)}, bf16[3,416,128]{2,1,0:T(8,128)(2,1)}, u32[]{:S(2)}, u32[]{:S(2)}) collective-permute-start(bf16[3,416,128]{2,1,0:T(8,128)(2,1)S(1)} %get-tuple-element.75), channel_id=1, source_target_pairs={{0,7},{1,2},{2,1},{3,4},{4,3},{5,6},{6,5},{7,0},{8,15},{9,10},{10,... | collective-permute-start | bytes 958472 | tf_op jit(solution)/shard_map/ppermute | solution.py:617
  62.0 1.3 %fusion = bf16[192,16,128]{2,1,0:T(8,128)(2,1)S(1)} fusion(bf16[192,16,128]{2,1,0:T(8,128)(2,1)} %collective-permute-done.7, bf16[2,192,16,128]{3,2,1,0:T(8,128)(2,1)S(1)} %bitcast.53, s32[]{:T(128)S(6)} %select_n.48), kind=kLoop, calls=%fused_computation.1 | loop fusion | flops 1572864 | bytes 2359300 | tf_op jit(solution)/shard_map/convert_element_type | solution.py:505
  63.5 5.3 %collective-permute-start.10 = (bf16[48,16,128]{2,1,0:T(8,128)(2,1)S(1)}, bf16[48,16,128]{2,1,0:T(8,128)(2,1)S(1)}, u32[]{:S(2)}, u32[]{:S(2)}) collective-permute-start(bf16[48,16,128]{2,1,0:T(8,128)(2,1)S(1)} %get-tuple-element.96), channel_id=1, source_target_pairs={{0,17},{1,16},{2,19},{3,18},{4,21},{5,20},{6,23},{7,22},{8,25},{9,... | collective-permute-start | bytes 589832 | tf_op jit(solution)/shard_map/ppermute | solution.py:499
  68.9 3.3 %collective-permute-start.8 = (bf16[48,16,128]{2,1,0:T(8,128)(2,1)S(1)}, bf16[48,16,128]{2,1,0:T(8,128)(2,1)S(1)}, u32[]{:S(2)}, u32[]{:S(2)}) collective-permute-start(bf16[48,16,128]{2,1,0:T(8,128)(2,1)S(1)} %get-tuple-element.98), channel_id=1, source_target_pairs={{0,1},{1,0},{2,3},{3,2},{4,5},{5,4},{6,7},{7,6},{8,9},{9,8},{10,11... | collective-permute-start | bytes 589832 | tf_op jit(solution)/shard_map/ppermute | solution.py:499
  72.2 12.3 %taps.1 = bf16[12,16,128]{2,1,0:T(8,128)(2,1)} custom-call(s32[8]{0:T(128)} %stack.53.sc.refs_0_, s32[64]{0:T(128)} %refs_1_.5, f32[3,1024,128]{2,1,0:T(8,128)} %get-tuple-element.51.refs_5_.refs_2_, f32[3,1024,128]{2,1,0:T(8,128)} %get-tuple-element.68.refs_3_.refs_5_, f32[8,384]{1,0:T(8,128)} %get-tuple-element.69.refs_4_, ...), custom_call_target="tpu_custom_call" | custom-call | flops 1000000 | bytes 2000000 | tf_op jit(solution)/shard_map/taps/pallas_call | solution.py:665
  84.7 1.7 %collective-permute-start.19 = (bf16[12,16,128]{2,1,0:T(8,128)(2,1)S(1)}, bf16[12,16,128]{2,1,0:T(8,128)(2,1)S(1)}, u32[]{:S(2)}, u32[]{:S(2)}) collective-permute-start(bf16[12,16,128]{2,1,0:T(8,128)(2,1)S(1)} %get-tuple-element.101), channel_id=1, source_target_pairs={{0,2},{1,3},{2,0},{3,1},{4,6},{5,7},{6,4},{7,5},{8,10},{9,11},{10,... | collective-permute-start | bytes 147464 | tf_op jit(solution)/shard_map/ppermute | solution.py:499
  86.4 2.7 %collective-permute-start.20 = (bf16[12,16,128]{2,1,0:T(8,128)(2,1)S(1)}, bf16[12,16,128]{2,1,0:T(8,128)(2,1)S(1)}, u32[]{:S(2)}, u32[]{:S(2)}) collective-permute-start(bf16[12,16,128]{2,1,0:T(8,128)(2,1)S(1)} %get-tuple-element.100), channel_id=1, source_target_pairs={{0,6},{1,7},{2,4},{3,5},{4,2},{5,3},{6,0},{7,1},{8,14},{9,15},{10,... | collective-permute-start | bytes 147464 | tf_op jit(solution)/shard_map/ppermute | solution.py:499
  89.7 2.6 %collective-permute-done.20 = bf16[12,16,128]{2,1,0:T(8,128)(2,1)S(1)} collective-permute-done((bf16[12,16,128]{2,1,0:T(8,128)(2,1)S(1)}, bf16[12,16,128]{2,1,0:T(8,128)(2,1)S(1)}, u32[]{:S(2)}, u32[]{:S(2)}) %collective-permute-start.20) | collective-permute-done | bytes 49184 | tf_op jit(solution)/shard_map/ppermute | solution.py:499
  92.5 3.3 %collective-permute-start.22 = (bf16[24,16,128]{2,1,0:T(8,128)(2,1)S(1)}, bf16[24,16,128]{2,1,0:T(8,128)(2,1)S(1)}, u32[]{:S(2)}, u32[]{:S(2)}) collective-permute-start(bf16[24,16,128]{2,1,0:T(8,128)(2,1)S(1)} %pad_maximum_fusion.refs_0_), channel_id=1, source_target_pairs={{0,2},{1,3},{2,0},{3,1},{4,6},{5,7},{6,4},{7,5},{8,10},{9,11},{10,... | collective-permute-start | bytes 294920 | tf_op jit(solution)/shard_map/ppermute | solution.py:521
  95.8 1.0 collective-permute-start.23
  96.8 2.2 %collective-permute-done.21.refs_1_ = bf16[24,16,128]{2,1,0:T(8,128)(2,1)S(1)} collective-permute-done((bf16[24,16,128]{2,1,0:T(8,128)(2,1)S(1)}, bf16[24,16,128]{2,1,0:T(8,128)(2,1)S(1)}, u32[]{:S(2)}, u32[]{:S(2)}) %collective-permute-start.21) | collective-permute-done | bytes 98336 | tf_op jit(solution)/shard_map/ppermute | solution.py:521
  99.4 3.9 %collective-permute-done.23.refs_3_ = bf16[24,16,128]{2,1,0:T(8,128)(2,1)S(1)} collective-permute-done((bf16[24,16,128]{2,1,0:T(8,128)(2,1)S(1)}, bf16[24,16,128]{2,1,0:T(8,128)(2,1)S(1)}, u32[]{:S(2)}, u32[]{:S(2)}) %collective-permute-start.23) | collective-permute-done | bytes 98336 | tf_op jit(solution)/shard_map/ppermute | solution.py:521
  104.0 3.8 %collective-permute-start.25 = (bf16[60,16,128]{2,1,0:T(8,128)(2,1)S(1)}, bf16[60,16,128]{2,1,0:T(8,128)(2,1)S(1)}, u32[]{:S(2)}, u32[]{:S(2)}) collective-permute-start(bf16[60,16,128]{2,1,0:T(8,128)(2,1)S(1)} %join.2.refs_0_), channel_id=1, source_target_pairs={{0,16},{1,17},{2,18},{3,19},{4,20},{5,21},{6,22},{7,23},{8,24},{9,... | collective-permute-start | bytes 737288 | tf_op jit(solution)/shard_map/ppermute | solution.py:521
  107.7 1.0 collective-permute-start.26
  108.7 10.7 %field.1 = bf16[300,8,128]{2,1,0:T(8,128)(2,1)} custom-call(s32[8]{0:T(128)} %stack.53.sc.refs_0_, s32[64]{0:T(128)} %refs_1_.5, f32[49,300]{1,0:T(8,128)} %refs_2_.3, s32[8,128]{1,0:T(8,128)} %bitcast.61, bf16[300,8,128]{2,1,0:T(8,128)(2,1)} %bitcast.49, f32[3,1024,128]{2,1,0:T(8,128)} %get-tuple-element.68.refs_3_.refs_5_, ...), custom_call_target="tpu_custom_call" | custom-call | flops 10000000 | bytes 20000000 | tf_op jit(solution)/shard_map/field/pallas_call | solution.py:681
  120.2 2.3 %collective-permute-done.27.refs_2_ = bf16[204,16,128]{2,1,0:T(8,128)(2,1)S(1)} collective-permute-done((bf16[204,16,128]{2,1,0:T(8,128)(2,1)S(1)}, bf16[204,16,128]{2,1,0:T(8,128)(2,1)S(1)}, u32[]{:S(2)}, u32[]{:S(2)}) %collective-permute-start.27) | collective-permute-done | bytes 835616 | tf_op jit(solution)/shard_map/ppermute | solution.py:521
  122.6 2.5 %unpack.1 = (f32[300,1200]{1,0:T(8,128)}, f32[300,1200]{1,0:T(8,128)}, f32[49,300]{1,0:T(8,128)}, f32[300]{0:T(512)}) custom-call(s32[8]{0:T(128)S(1)} %copy-done.10, bf16[204,16,128]{2,1,0:T(8,128)(2,1)S(1)} %join.3.refs_1_, bf16[204,16,128]{2,1,0:T(8,128)(2,1)S(1)} %collective-permute-done.27.refs_2_), custom_call_target="tpu_custom_call" | custom-call | flops 3000000 | bytes 6000000 | tf_op jit(solution)/shard_map/unpack/pallas_call | solution.py:699
  (104 shorter events, 10.7 us)
Async XLA Ops:
  0.6 17.9 %copy-start.14 = (bf16[300,1200]{1,0:T(8,128)(2,1)S(1)}, bf16[300,1200]{1,0:T(8,128)(2,1)}, u32[]{:S(2)}) copy-start(bf16[300,1200]{1,0:T(8,128)(2,1)} %param.13) | copy-start | bytes 2160004
  5.0 4.5 %collective-permute-start = (bf16[3,8,384]{2,1,0:T(8,128)(2,1)}, bf16[3,8,384]{2,1,0:T(8,128)(2,1)S(1)}, u32[]{:S(2)}, u32[]{:S(2)}) collective-permute-start(bf16[3,8,384]{2,1,0:T(8,128)(2,1)} %get-tuple-element.52), channel_id=1, source_target_pairs={{0,8},{1,9},{2,10},{3,11},{4,12},{5,13},{6,14},{7,15},{8,0},{9,1},... | collective-permute-start | bytes 55304 | tf_op jit(solution)/shard_map/ppermute | solution.py:598
  5.5 4.0 %collective-permute-start.1 = (bf16[3,8,384]{2,1,0:T(8,128)(2,1)}, bf16[3,8,384]{2,1,0:T(8,128)(2,1)S(1)}, u32[]{:S(2)}, u32[]{:S(2)}) collective-permute-start(bf16[3,8,384]{2,1,0:T(8,128)(2,1)} %get-tuple-element.53), channel_id=1, source_target_pairs={{8,16},{9,17},{10,18},{11,19},{12,20},{13,21},{14,22},{15,23},{16,... | collective-permute-start | bytes 55304 | tf_op jit(solution)/shard_map/ppermute | solution.py:599
  10.2 16.3 %collective-permute-start.2 = (bf16[3,416,128]{2,1,0:T(8,128)(2,1)S(1)}, bf16[3,416,128]{2,1,0:T(8,128)(2,1)S(1)}, u32[]{:S(2)}, u32[]{:S(2)}) collective-permute-start(bf16[3,416,128]{2,1,0:T(8,128)(2,1)S(1)} %get-tuple-element.59), channel_id=1, source_target_pairs={{0,1},{1,0},{2,3},{3,2},{4,5},{5,4},{6,7},{7,6},{8,9},{9,8},{10,11... | collective-permute-start | bytes 958472 | tf_op jit(solution)/shard_map/ppermute | solution.py:616
  12.9 13.6 %collective-permute-start.3 = (bf16[3,416,128]{2,1,0:T(8,128)(2,1)S(1)}, bf16[3,416,128]{2,1,0:T(8,128)(2,1)S(1)}, u32[]{:S(2)}, u32[]{:S(2)}) collective-permute-start(bf16[3,416,128]{2,1,0:T(8,128)(2,1)S(1)} %get-tuple-element.60), channel_id=1, source_target_pairs={{0,7},{1,2},{2,1},{3,4},{4,3},{5,6},{6,5},{7,0},{8,15},{9,10},{10,... | collective-permute-start | bytes 958472 | tf_op jit(solution)/shard_map/ppermute | solution.py:617
  16.5 4.7 %collective-permute-start.4 = (bf16[2,3,8,384]{3,2,1,0:T(8,128)(2,1)S(1)}, bf16[2,3,8,384]{3,2,1,0:T(8,128)(2,1)S(1)}, u32[]{:S(2)}, u32[]{:S(2)}) collective-permute-start(bf16[2,3,8,384]{3,2,1,0:T(8,128)(2,1)S(1)} %pad_maximum_fusion.1.refs_14_.refs_9_), channel_id=1, source_target_pairs={{24,26},{25,27},{26,24},{27,25},{28,30},{29,31},{30,28},{31,29}} | collective-permute-start | bytes 110600 | tf_op jit(solution)/shard_map/ppermute | solution.py:458
  17.2 4.0 %collective-permute-start.5 = (bf16[2,3,8,384]{3,2,1,0:T(8,128)(2,1)S(1)}, bf16[2,3,8,384]{3,2,1,0:T(8,128)(2,1)S(1)}, u32[]{:S(2)}, u32[]{:S(2)}) collective-permute-start(bf16[2,3,8,384]{3,2,1,0:T(8,128)(2,1)S(1)} %pad_maximum_fusion.1.refs_14_.refs_9_), channel_id=1, source_target_pairs={{24,28},{25,29},{26,30},{27,31},{28,24},{29,25},{30,26},{31,27}} | collective-permute-start | bytes 110600 | tf_op jit(solution)/shard_map/ppermute | solution.py:458
  17.9 3.4 %collective-permute-start.6 = (bf16[2,3,8,384]{3,2,1,0:T(8,128)(2,1)S(1)}, bf16[2,3,8,384]{3,2,1,0:T(8,128)(2,1)S(1)}, u32[]{:S(2)}, u32[]{:S(2)}) collective-permute-start(bf16[2,3,8,384]{3,2,1,0:T(8,128)(2,1)S(1)} %pad_maximum_fusion.1.refs_14_.refs_9_), channel_id=1, source_target_pairs={{24,30},{25,31},{26,28},{27,29},{28,26},{29,27},{30,24},{31,25}} | collective-permute-start | bytes 110600 | tf_op jit(solution)/shard_map/ppermute | solution.py:458
  49.5 9.0 %collective-permute-start.7 = (bf16[192,16,128]{2,1,0:T(8,128)(2,1)}, bf16[192,16,128]{2,1,0:T(8,128)(2,1)}, u32[]{:S(2)}, u32[]{:S(2)}) collective-permute-start(bf16[192,16,128]{2,1,0:T(8,128)(2,1)} %dynamic-slice_bitcast_fusion), channel_id=1, source_target_pairs={{0,8},{1,9},{2,10},{3,11},{4,12},{5,13},{6,14},{7,15},{8,0},{9,1},... | collective-permute-start | bytes 2359304 | tf_op jit(solution)/shard_map/ppermute | solution.py:499
  50.9 2.0 %collective-permute-start.11 = (bf16[3,8,384]{2,1,0:T(8,128)(2,1)}, bf16[3,8,384]{2,1,0:T(8,128)(2,1)S(1)}, u32[]{:S(2)}, u32[]{:S(2)}) collective-permute-start(bf16[3,8,384]{2,1,0:T(8,128)(2,1)} %get-tuple-element.64), channel_id=1, source_target_pairs={{0,8},{1,9},{2,10},{3,11},{4,12},{5,13},{6,14},{7,15},{8,0},{9,1},... | collective-permute-start | bytes 55304 | tf_op jit(solution)/shard_map/ppermute | solution.py:598
  50.9 2.0 %collective-permute-start.12 = (bf16[3,8,384]{2,1,0:T(8,128)(2,1)}, bf16[3,8,384]{2,1,0:T(8,128)(2,1)S(1)}, u32[]{:S(2)}, u32[]{:S(2)}) collective-permute-start(bf16[3,8,384]{2,1,0:T(8,128)(2,1)} %get-tuple-element.65), channel_id=1, source_target_pairs={{8,16},{9,17},{10,18},{11,19},{12,20},{13,21},{14,22},{15,23},{16,... | collective-permute-start | bytes 55304 | tf_op jit(solution)/shard_map/ppermute | solution.py:599
  53.7 9.8 %collective-permute-start.15 = (bf16[2,3,8,384]{3,2,1,0:T(8,128)(2,1)S(1)}, bf16[2,3,8,384]{3,2,1,0:T(8,128)(2,1)S(1)}, u32[]{:S(2)}, u32[]{:S(2)}) collective-permute-start(bf16[2,3,8,384]{3,2,1,0:T(8,128)(2,1)S(1)} %pad_maximum_fusion.2.refs_10_), channel_id=1, source_target_pairs={{24,26},{25,27},{26,24},{27,25},{28,30},{29,31},{30,28},{31,29}} | collective-permute-start | bytes 110600 | tf_op jit(solution)/shard_map/ppermute | solution.py:458
  54.4 14.5 %collective-permute-start.16 = (bf16[2,3,8,384]{3,2,1,0:T(8,128)(2,1)S(1)}, bf16[2,3,8,384]{3,2,1,0:T(8,128)(2,1)S(1)}, u32[]{:S(2)}, u32[]{:S(2)}) collective-permute-start(bf16[2,3,8,384]{3,2,1,0:T(8,128)(2,1)S(1)} %pad_maximum_fusion.2.refs_10_), channel_id=1, source_target_pairs={{24,28},{25,29},{26,30},{27,31},{28,24},{29,25},{30,26},{31,27}} | collective-permute-start | bytes 110600 | tf_op jit(solution)/shard_map/ppermute | solution.py:458
  55.0 17.1 %collective-permute-start.17 = (bf16[2,3,8,384]{3,2,1,0:T(8,128)(2,1)S(1)}, bf16[2,3,8,384]{3,2,1,0:T(8,128)(2,1)S(1)}, u32[]{:S(2)}, u32[]{:S(2)}) collective-permute-start(bf16[2,3,8,384]{3,2,1,0:T(8,128)(2,1)S(1)} %pad_maximum_fusion.2.refs_10_), channel_id=1, source_target_pairs={{24,30},{25,31},{26,28},{27,29},{28,26},{29,27},{30,24},{31,25}} | collective-permute-start | bytes 110600 | tf_op jit(solution)/shard_map/ppermute | solution.py:458
  56.4 28.1 %collective-permute-start.13 = (bf16[3,416,128]{2,1,0:T(8,128)(2,1)S(1)}, bf16[3,416,128]{2,1,0:T(8,128)(2,1)S(1)}, u32[]{:S(2)}, u32[]{:S(2)}) collective-permute-start(bf16[3,416,128]{2,1,0:T(8,128)(2,1)S(1)} %get-tuple-element.74), channel_id=1, source_target_pairs={{0,1},{1,0},{2,3},{3,2},{4,5},{5,4},{6,7},{7,6},{8,9},{9,8},{10,11... | collective-permute-start | bytes 958472 | tf_op jit(solution)/shard_map/ppermute | solution.py:616
  58.5 26.0 %collective-permute-start.14 = (bf16[3,416,128]{2,1,0:T(8,128)(2,1)S(1)}, bf16[3,416,128]{2,1,0:T(8,128)(2,1)}, u32[]{:S(2)}, u32[]{:S(2)}) collective-permute-start(bf16[3,416,128]{2,1,0:T(8,128)(2,1)S(1)} %get-tuple-element.75), channel_id=1, source_target_pairs={{0,7},{1,2},{2,1},{3,4},{4,3},{5,6},{6,5},{7,0},{8,15},{9,10},{10,... | collective-permute-start | bytes 958472 | tf_op jit(solution)/shard_map/ppermute | solution.py:617
  63.5 20.9 %copy-start.23 = (bf16[2,3,8,384]{3,2,1,0:T(8,128)(2,1)}, bf16[2,3,8,384]{3,2,1,0:T(8,128)(2,1)S(1)}, u32[]{:S(2)}) copy-start(bf16[2,3,8,384]{3,2,1,0:T(8,128)(2,1)S(1)} %collective-permute-done.15.refs_11_) | copy-start | bytes 110596
  63.5 20.9 %collective-permute-start.10 = (bf16[48,16,128]{2,1,0:T(8,128)(2,1)S(1)}, bf16[48,16,128]{2,1,0:T(8,128)(2,1)S(1)}, u32[]{:S(2)}, u32[]{:S(2)}) collective-permute-start(bf16[48,16,128]{2,1,0:T(8,128)(2,1)S(1)} %get-tuple-element.96), channel_id=1, source_target_pairs={{0,17},{1,16},{2,19},{3,18},{4,21},{5,20},{6,23},{7,22},{8,25},{9,... | collective-permute-start | bytes 589832 | tf_op jit(solution)/shard_map/ppermute | solution.py:499
  68.9 15.5 %copy-start.24 = (bf16[2,3,8,384]{3,2,1,0:T(8,128)(2,1)}, bf16[2,3,8,384]{3,2,1,0:T(8,128)(2,1)S(1)}, u32[]{:S(2)}) copy-start(bf16[2,3,8,384]{3,2,1,0:T(8,128)(2,1)S(1)} %collective-permute-done.16.refs_12_) | copy-start | bytes 110596
  68.9 15.6 %collective-permute-start.8 = (bf16[48,16,128]{2,1,0:T(8,128)(2,1)S(1)}, bf16[48,16,128]{2,1,0:T(8,128)(2,1)S(1)}, u32[]{:S(2)}, u32[]{:S(2)}) collective-permute-start(bf16[48,16,128]{2,1,0:T(8,128)(2,1)S(1)} %get-tuple-element.98), channel_id=1, source_target_pairs={{0,1},{1,0},{2,3},{3,2},{4,5},{5,4},{6,7},{7,6},{8,9},{9,8},{10,11... | collective-permute-start | bytes 589832 | tf_op jit(solution)/shard_map/ppermute | solution.py:499
  72.1 12.4 %collective-permute-start.9 = (bf16[48,16,128]{2,1,0:T(8,128)(2,1)S(1)}, bf16[48,16,128]{2,1,0:T(8,128)(2,1)S(1)}, u32[]{:S(2)}, u32[]{:S(2)}) collective-permute-start(bf16[48,16,128]{2,1,0:T(8,128)(2,1)S(1)} %get-tuple-element.97), channel_id=1, source_target_pairs={{0,16},{1,17},{2,18},{3,19},{4,20},{5,21},{6,22},{7,23},{8,24},{9,... | collective-permute-start | bytes 589832 | tf_op jit(solution)/shard_map/ppermute | solution.py:499
  84.4 24.3 %copy-start.17 = (bf16[3,416,128]{2,1,0:T(8,128)(2,1)}, bf16[3,416,128]{2,1,0:T(8,128)(2,1)S(1)}, u32[]{:S(2)}) copy-start(bf16[3,416,128]{2,1,0:T(8,128)(2,1)S(1)} %collective-permute-done.13.refs_6_) | copy-start | bytes 958468
  84.7 5.1 %collective-permute-start.18 = (bf16[12,16,128]{2,1,0:T(8,128)(2,1)S(1)}, bf16[12,16,128]{2,1,0:T(8,128)(2,1)S(1)}, u32[]{:S(2)}, u32[]{:S(2)}) collective-permute-start(bf16[12,16,128]{2,1,0:T(8,128)(2,1)S(1)} %get-tuple-element.99), channel_id=1, source_target_pairs={{0,4},{1,5},{2,6},{3,7},{4,0},{5,1},{6,2},{7,3},{8,12},{9,13},{10,... | collective-permute-start | bytes 147464 | tf_op jit(solution)/shard_map/ppermute | solution.py:499
  84.7 5.0 %collective-permute-start.19 = (bf16[12,16,128]{2,1,0:T(8,128)(2,1)S(1)}, bf16[12,16,128]{2,1,0:T(8,128)(2,1)S(1)}, u32[]{:S(2)}, u32[]{:S(2)}) collective-permute-start(bf16[12,16,128]{2,1,0:T(8,128)(2,1)S(1)} %get-tuple-element.101), channel_id=1, source_target_pairs={{0,2},{1,3},{2,0},{3,1},{4,6},{5,7},{6,4},{7,5},{8,10},{9,11},{10,... | collective-permute-start | bytes 147464 | tf_op jit(solution)/shard_map/ppermute | solution.py:499
  86.4 5.9 %collective-permute-start.20 = (bf16[12,16,128]{2,1,0:T(8,128)(2,1)S(1)}, bf16[12,16,128]{2,1,0:T(8,128)(2,1)S(1)}, u32[]{:S(2)}, u32[]{:S(2)}) collective-permute-start(bf16[12,16,128]{2,1,0:T(8,128)(2,1)S(1)} %get-tuple-element.100), channel_id=1, source_target_pairs={{0,6},{1,7},{2,4},{3,5},{4,2},{5,3},{6,0},{7,1},{8,14},{9,15},{10,... | collective-permute-start | bytes 147464 | tf_op jit(solution)/shard_map/ppermute | solution.py:499
  92.4 6.6 %collective-permute-start.21 = (bf16[24,16,128]{2,1,0:T(8,128)(2,1)S(1)}, bf16[24,16,128]{2,1,0:T(8,128)(2,1)S(1)}, u32[]{:S(2)}, u32[]{:S(2)}) collective-permute-start(bf16[24,16,128]{2,1,0:T(8,128)(2,1)S(1)} %pad_maximum_fusion.refs_0_), channel_id=1, source_target_pairs={{0,4},{1,5},{2,6},{3,7},{4,0},{5,1},{6,2},{7,3},{8,12},{9,13},{10,... | collective-permute-start | bytes 294920 | tf_op jit(solution)/shard_map/ppermute | solution.py:521
  92.5 6.9 %collective-permute-start.22 = (bf16[24,16,128]{2,1,0:T(8,128)(2,1)S(1)}, bf16[24,16,128]{2,1,0:T(8,128)(2,1)S(1)}, u32[]{:S(2)}, u32[]{:S(2)}) collective-permute-start(bf16[24,16,128]{2,1,0:T(8,128)(2,1)S(1)} %pad_maximum_fusion.refs_0_), channel_id=1, source_target_pairs={{0,2},{1,3},{2,0},{3,1},{4,6},{5,7},{6,4},{7,5},{8,10},{9,11},{10,... | collective-permute-start | bytes 294920 | tf_op jit(solution)/shard_map/ppermute | solution.py:521
  95.8 7.5 %collective-permute-start.23 = (bf16[24,16,128]{2,1,0:T(8,128)(2,1)S(1)}, bf16[24,16,128]{2,1,0:T(8,128)(2,1)S(1)}, u32[]{:S(2)}, u32[]{:S(2)}) collective-permute-start(bf16[24,16,128]{2,1,0:T(8,128)(2,1)S(1)} %pad_maximum_fusion.refs_0_), channel_id=1, source_target_pairs={{0,6},{1,7},{2,4},{3,5},{4,2},{5,3},{6,0},{7,1},{8,14},{9,15},{10,... | collective-permute-start | bytes 294920 | tf_op jit(solution)/shard_map/ppermute | solution.py:521
  103.3 16.1 %collective-permute-start.24 = (bf16[60,16,128]{2,1,0:T(8,128)(2,1)S(1)}, bf16[60,16,128]{2,1,0:T(8,128)(2,1)S(1)}, u32[]{:S(2)}, u32[]{:S(2)}) collective-permute-start(bf16[60,16,128]{2,1,0:T(8,128)(2,1)S(1)} %join.2.refs_0_), channel_id=1, source_target_pairs={{0,1},{1,0},{2,3},{3,2},{4,5},{5,4},{6,7},{7,6},{8,9},{9,8},{10,11... | collective-permute-start | bytes 737288 | tf_op jit(solution)/shard_map/ppermute | solution.py:521
  104.0 15.4 %collective-permute-start.25 = (bf16[60,16,128]{2,1,0:T(8,128)(2,1)S(1)}, bf16[60,16,128]{2,1,0:T(8,128)(2,1)S(1)}, u32[]{:S(2)}, u32[]{:S(2)}) collective-permute-start(bf16[60,16,128]{2,1,0:T(8,128)(2,1)S(1)} %join.2.refs_0_), channel_id=1, source_target_pairs={{0,16},{1,17},{2,18},{3,19},{4,20},{5,21},{6,22},{7,23},{8,24},{9,... | collective-permute-start | bytes 737288 | tf_op jit(solution)/shard_map/ppermute | solution.py:521
  107.7 12.3 %collective-permute-start.26 = (bf16[60,16,128]{2,1,0:T(8,128)(2,1)S(1)}, bf16[60,16,128]{2,1,0:T(8,128)(2,1)S(1)}, u32[]{:S(2)}, u32[]{:S(2)}) collective-permute-start(bf16[60,16,128]{2,1,0:T(8,128)(2,1)S(1)} %join.2.refs_0_), channel_id=1, source_target_pairs={{0,17},{1,16},{2,19},{3,18},{4,21},{5,20},{6,23},{7,22},{8,25},{9,... | collective-permute-start | bytes 737288 | tf_op jit(solution)/shard_map/ppermute | solution.py:521
  120.1 2.4 %collective-permute-start.27 = (bf16[204,16,128]{2,1,0:T(8,128)(2,1)S(1)}, bf16[204,16,128]{2,1,0:T(8,128)(2,1)S(1)}, u32[]{:S(2)}, u32[]{:S(2)}) collective-permute-start(bf16[204,16,128]{2,1,0:T(8,128)(2,1)S(1)} %join.3.refs_1_), channel_id=1, source_target_pairs={{0,8},{1,9},{2,10},{3,11},{4,12},{5,13},{6,14},{7,15},{8,0},{9,1},... | collective-permute-start | bytes 2506760 | tf_op jit(solution)/shard_map/ppermute | solution.py:521
  (24 other events, 179.9 us)
